TPU v7x, 32 devices: a whole 2x2x4 slice. The times are simulated.
32 devices in a mesh: wide: 8 (over z, x), narrow: 4 (over y, core).
Axes of the slice: x: 2, y: 2, z: 4, core: 2. Of those that a mesh axis runs over, the one named last changes fastest.
Arguments:
- block_input: bfloat16 [4096, 2048], P('wide'), may hold values from -6 to 6
- attn_gain: bfloat16 [2048], replicated, may hold values from 0.5 to 1.5
- query_weight: bfloat16 [2048, 2048], P(None, 'narrow'), may hold values from -0.125 to 0.125
- key_weight: bfloat16 [2048, 2048], P(None, 'narrow'), may hold values from -0.125 to 0.125
- value_weight: bfloat16 [2048, 2048], P(None, 'narrow'), may hold values from -0.125 to 0.125
- query_gain: bfloat16 [2048], P('narrow'), may hold values from 0.5 to 1.5
- key_gain: bfloat16 [2048], P('narrow'), may hold values from 0.5 to 1.5
- out_weight: bfloat16 [2048, 2048], P('narrow'), may hold values from -1.5 to 1.5
- moe_gain: bfloat16 [2048], replicated, may hold values from 0.5 to 1.5
- router_weight: bfloat16 [2048, 32], replicated, may hold values from -0.0625 to 0.0625
- gate_weight: bfloat16 [32, 2048, 1024], P('wide', None, 'narrow'), may hold values from -0.125 to 0.125
- up_weight: bfloat16 [32, 2048, 1024], P('wide', None, 'narrow'), may hold values from -0.125 to 0.125
- down_weight: bfloat16 [32, 1024, 2048], P('wide', 'narrow'), may hold values from -6 to 6
- segment_ids: int32 [4096], P('wide'), may hold values from 0 to 3, as said below
- expert_ids: int32 [4096, 8], P(('wide', 'narrow')), may hold values from 0 to 31, all different within a row; in each aligned block of 128 rows (0 to 127, 128 to 255, ...) at most 48 rows name the same one
- out_cotangent: bfloat16 [4096, 2048], P(('wide', 'narrow')), may hold values from -6 to 6
Outputs:
- block_output: bfloat16 [4096, 2048], P(('wide', 'narrow'))
- input_grad: bfloat16 [4096, 2048], P(('wide', 'narrow'))
- attn_gain_grad: float32 [2048], replicated
- query_weight_grad: float32 [2048, 2048], P(None, 'narrow')
- key_weight_grad: float32 [2048, 2048], P(None, 'narrow')
- value_weight_grad: float32 [2048, 2048], P(None, 'narrow')
- query_gain_grad: float32 [2048], P('narrow')
- key_gain_grad: float32 [2048], P('narrow')
- out_weight_grad: float32 [2048, 2048], P('narrow')
- moe_gain_grad: float32 [2048], replicated
- router_weight_grad: float32 [2048, 32], replicated
- gate_weight_grad: float32 [32, 2048, 1024], P('wide', None, 'narrow')
- up_weight_grad: float32 [32, 2048, 1024], P('wide', None, 'narrow')
- down_weight_grad: float32 [32, 1024, 2048], P('wide', 'narrow')
Inputs may be any that keep to these rules, and one draw needn't show every extreme that they name: `segment_ids`: within each group of 512 consecutive tokens the ids start at 0 and never fall; a sequence is a run of equal ids inside one group. One group holds a single sequence of 512 tokens, each other group up to four sequences. `expert_ids`: each row names 8 different experts. Among the rows of one device no expert is named more than 48 times, a bound that some block reaches.
All inputs are finite; a program needn't handle non-finite values.
Results may differ from a plain program's by a relative error of at most 0.025.
Values may be sent and summed in bfloat16 or wider, within the bound.
A program may use at most 448 MiB of HBM per device.

v0:
```python
import jax
import jax.numpy as jnp
from jax import lax
from jax.sharding import PartitionSpec as P

HEAD_DIM = 128
QBLK = 512


norm_epsilon = 1e-05
rope_base = 10000.0
masked_score = -1e30


def rms_scale(values, gain):
    inverse = lax.rsqrt(jnp.mean(values * values, axis=-1, keepdims=True) + norm_epsilon)
    return values * inverse * gain


def rope_tables(length, head_size):
    half_size = head_size // 2
    exponent = jnp.arange(half_size, dtype=jnp.float32) * (2.0 / head_size)
    angle = jnp.arange(length, dtype=jnp.float32)[:, None] * (rope_base ** (-exponent))[None, :]
    return (jnp.cos(angle), jnp.sin(angle))


def rotate(normed, rope_cos, rope_sin, head_size):
    tokens_here = normed.shape[0]
    by_head = normed.reshape(tokens_here, -1, head_size)
    half_size = head_size // 2
    first_half = by_head[..., :half_size]
    second_half = by_head[..., half_size:]
    cos_rows = rope_cos[:, None, :]
    sin_rows = rope_sin[:, None, :]
    turned = jnp.concatenate(
        [
            first_half * cos_rows - second_half * sin_rows,
            second_half * cos_rows + first_half * sin_rows,
        ],
        axis=-1,
    )
    return turned.reshape(tokens_here, -1)


def gated_unit(gate_pre, up_pre):
    return jax.nn.silu(gate_pre) * up_pre


def contract_rows(left, right):
    return lax.dot_general(
        left, right, (((0,), (0,)), ((), ())), preferred_element_type=jnp.float32
    )


def contract_last(left, right):
    return lax.dot_general(
        left, right, (((1,), (1,)), ((), ())), preferred_element_type=jnp.float32
    )


def local(
    block_input,
    attn_gain,
    query_weight,
    key_weight,
    value_weight,
    query_gain,
    key_gain,
    out_weight,
    moe_gain,
    router_weight,
    gate_weight,
    up_weight,
    down_weight,
    segment_ids,
    expert_ids,
    out_cotangent,
):
    group_rows, model_width = block_input.shape
    own_rows = out_cotangent.shape[0]
    local_width = query_weight.shape[1]
    head_size = HEAD_DIM
    local_heads = local_width // head_size
    wide_size = lax.axis_size("wide")
    experts_all = router_weight.shape[1]
    experts_here = gate_weight.shape[0]
    choose_count = expert_ids.shape[1]
    capacity = 3 * own_rows * choose_count // (2 * experts_all)
    row_begin = lax.axis_index("narrow") * own_rows
    blocks = group_rows // QBLK
    highest_precision = lax.Precision.HIGHEST
    inputs_all = block_input.astype(jnp.float32)
    normed_one = rms_scale(inputs_all, attn_gain.astype(jnp.float32)).astype(jnp.bfloat16)
    joined_weight = jnp.concatenate([query_weight, key_weight, value_weight], axis=1)
    projected = jnp.dot(normed_one, joined_weight, preferred_element_type=jnp.float32)
    query_proj = projected[:, :local_width]
    key_proj = projected[:, local_width : 2 * local_width]
    value_proj = projected[:, 2 * local_width :]
    rope_cos, rope_sin = rope_tables(group_rows, head_size)
    query_total, key_total = lax.psum(
        (jnp.sum(query_proj * query_proj, axis=1), jnp.sum(key_proj * key_proj, axis=1)), "narrow"
    )
    query_inverse = lax.rsqrt(query_total / model_width + norm_epsilon)[:, None]
    key_inverse = lax.rsqrt(key_total / model_width + norm_epsilon)[:, None]
    query_scale = query_gain.astype(jnp.float32)
    key_scale = key_gain.astype(jnp.float32)
    query_normed = query_proj * query_inverse * query_scale
    key_normed = key_proj * key_inverse * key_scale

    def turn_both(query_in, key_in):
        return (
            rotate(query_in, rope_cos, rope_sin, head_size) * head_size ** (-0.5),
            rotate(key_in, rope_cos, rope_sin, head_size),
        )

    (turned_query, turned_key), turn_back = jax.vjp(turn_both, query_normed, key_normed)
    query_heads = turned_query.astype(jnp.bfloat16).reshape(group_rows, local_heads, head_size)
    key_heads = turned_key.astype(jnp.bfloat16).reshape(group_rows, local_heads, head_size)
    value_heads = value_proj.astype(jnp.bfloat16).reshape(group_rows, local_heads, head_size)
    positions = jnp.arange(group_rows)

    def block_scores(block_index):
        block_begin = block_index * QBLK
        query_block = lax.dynamic_slice_in_dim(query_heads, block_begin, QBLK, 0)
        query_segments = lax.dynamic_slice_in_dim(segment_ids, block_begin, QBLK, 0)
        query_places = block_begin + jnp.arange(QBLK)
        allowed = (query_segments[:, None] == segment_ids[None, :]) & (
            query_places[:, None] >= positions[None, :]
        )
        scores = jnp.einsum(
            "qhd,khd->hqk", query_block, key_heads, preferred_element_type=jnp.float32
        )
        return (query_block, jnp.where(allowed[None], scores, masked_score))

    def attend(block_index):
        query_block, scores = block_scores(block_index)
        highest = jnp.max(scores, axis=-1, keepdims=True)
        weights = jnp.exp(scores - highest)
        totals = jnp.sum(weights, axis=-1, keepdims=True)
        probs_low = (weights / totals).astype(jnp.bfloat16)
        mixed_rows = jnp.einsum(
            "hqk,khd->qhd", probs_low, value_heads, preferred_element_type=jnp.float32
        )
        return (mixed_rows, highest + jnp.log(totals))

    mixed_blocks, log_totals = lax.map(attend, jnp.arange(blocks))
    heads_out = mixed_blocks.reshape(group_rows, local_width).astype(jnp.bfloat16)
    attn_own = lax.psum_scatter(
        jnp.dot(heads_out, out_weight, preferred_element_type=jnp.float32).astype(jnp.bfloat16),
        "narrow",
        scatter_dimension=0,
        tiled=True,
    ).astype(jnp.float32)
    input_own = lax.dynamic_slice_in_dim(inputs_all, row_begin, own_rows, 0)
    hidden = input_own + attn_own
    normed_two_full, norm_two_back = jax.vjp(rms_scale, hidden, moe_gain.astype(jnp.float32))
    normed_two = normed_two_full.astype(jnp.bfloat16)
    logits = jnp.dot(normed_two, router_weight, preferred_element_type=jnp.float32)
    route_probs = jax.nn.softmax(logits, axis=-1)
    gates = jnp.take_along_axis(route_probs, expert_ids, axis=1)
    flat_ids = expert_ids.reshape(-1)
    expert_match = (flat_ids[:, None] == jnp.arange(experts_all)[None, :]).astype(jnp.int32)
    earlier = jnp.cumsum(expert_match, axis=0) - expert_match
    slot_of = jnp.sum(earlier * expert_match, axis=1)
    token_of = jnp.arange(own_rows * choose_count) // choose_count
    slot_token = (
        jnp.full((experts_all, capacity), own_rows, jnp.int32).at[flat_ids, slot_of].set(token_of)
    )
    slot_gate = (
        jnp.zeros((experts_all, capacity), jnp.float32).at[flat_ids, slot_of].set(gates.reshape(-1))
    )
    padded_rows = jnp.concatenate([normed_two, jnp.zeros((1, model_width), jnp.bfloat16)], axis=0)
    cotangent_full = out_cotangent.astype(jnp.float32)
    padded_grads = jnp.concatenate(
        [cotangent_full, jnp.zeros((1, model_width), jnp.float32)], axis=0
    )
    send_rows = padded_rows[slot_token].reshape(wide_size, experts_here, capacity, model_width)
    send_grads = (
        (padded_grads[slot_token] * slot_gate[:, :, None])
        .astype(jnp.bfloat16)
        .reshape(wide_size, experts_here, capacity, model_width)
    )
    recv_rows, recv_grads = (
        lax.all_to_all(send_rows, "wide", split_axis=0, concat_axis=0, tiled=True),
        lax.all_to_all(send_grads, "wide", split_axis=0, concat_axis=0, tiled=True),
    )
    all_rows, all_grads = (
        lax.all_gather(recv_rows, "narrow", axis=0, tiled=True),
        lax.all_gather(recv_grads, "narrow", axis=0, tiled=True),
    )
    gate_pre = jnp.einsum(
        "secd,edf->secf", all_rows, gate_weight, preferred_element_type=jnp.float32
    )
    up_pre = jnp.einsum("secd,edf->secf", all_rows, up_weight, preferred_element_type=jnp.float32)
    activated, unit_back = jax.vjp(gated_unit, gate_pre, up_pre)
    act_low = activated.astype(jnp.bfloat16)
    expert_mine = lax.psum_scatter(
        jnp.einsum(
            "secf,efd->secd", act_low, down_weight, preferred_element_type=jnp.float32
        ).astype(jnp.bfloat16),
        "narrow",
        scatter_dimension=0,
        tiled=True,
    )
    act_grad = jnp.einsum(
        "secd,efd->secf", all_grads, down_weight, preferred_element_type=jnp.float32
    )
    gate_grad_full, up_grad_full = unit_back(act_grad)
    gate_grad_low = gate_grad_full.astype(jnp.bfloat16)
    up_grad_low = up_grad_full.astype(jnp.bfloat16)
    down_weight_grad = jnp.einsum(
        "secf,secd->efd", act_low, all_grads, preferred_element_type=jnp.float32
    )
    gate_weight_grad = jnp.einsum(
        "secd,secf->edf", all_rows, gate_grad_low, preferred_element_type=jnp.float32
    )
    up_weight_grad = jnp.einsum(
        "secd,secf->edf", all_rows, up_grad_low, preferred_element_type=jnp.float32
    )
    gate_term = jnp.einsum(
        "secf,edf->secd", gate_grad_low, gate_weight, preferred_element_type=jnp.float32
    )
    back_mine = lax.psum_scatter(
        (
            gate_term
            + jnp.einsum(
                "secf,edf->secd", up_grad_low, up_weight, preferred_element_type=jnp.float32
            )
        ).astype(jnp.bfloat16),
        "narrow",
        scatter_dimension=0,
        tiled=True,
    )
    expert_back = lax.all_to_all(expert_mine, "wide", split_axis=0, concat_axis=0, tiled=True)
    input_back = lax.all_to_all(back_mine, "wide", split_axis=0, concat_axis=0, tiled=True)
    gather_index = flat_ids * capacity + slot_of
    returned = (
        expert_back.reshape(-1, model_width)[gather_index]
        .reshape(own_rows, choose_count, model_width)
        .astype(jnp.float32)
    )
    moe_out = jnp.einsum("tk,tkd->td", gates, returned, precision=highest_precision)
    block_output = (hidden + moe_out).astype(jnp.bfloat16)
    gate_grads = jnp.einsum("td,tkd->tk", cotangent_full, returned, precision=highest_precision)
    picked = (expert_ids[:, :, None] == jnp.arange(experts_all)[None, None, :]).astype(jnp.float32)
    prob_grads = jnp.einsum("tk,tke->te", gate_grads, picked, precision=highest_precision)
    logit_grads = route_probs * (
        prob_grads - jnp.sum(route_probs * prob_grads, axis=-1, keepdims=True)
    )
    router_part = lax.dot_general(
        normed_two.astype(jnp.float32),
        logit_grads,
        (((0,), (0,)), ((), ())),
        precision=highest_precision,
    )
    rows_back = (
        input_back.reshape(-1, model_width)[gather_index]
        .reshape(own_rows, choose_count, model_width)
        .astype(jnp.float32)
    )
    router_back = lax.dot_general(
        logit_grads,
        router_weight.astype(jnp.float32),
        (((1,), (1,)), ((), ())),
        precision=highest_precision,
    )
    normed_two_grad = jnp.sum(rows_back, axis=1) + router_back
    hidden_path, moe_gain_part = norm_two_back(normed_two_grad)
    hidden_grad = cotangent_full + hidden_path
    hidden_grad_low = hidden_grad.astype(jnp.bfloat16)
    gathered_piece = lax.all_gather(hidden_grad_low, "narrow", axis=0, tiled=True)
    heads_grad_acc = contract_last(gathered_piece, out_weight)
    out_weight_acc = contract_rows(heads_out, gathered_piece)
    heads_grad_low = heads_grad_acc.astype(jnp.bfloat16).reshape(group_rows, local_heads, head_size)

    def back_block(running, items):
        key_acc, value_acc = running
        block_index, log_total = items
        query_block, scores = block_scores(block_index)
        probs = jnp.exp(scores - log_total)
        probs_low = probs.astype(jnp.bfloat16)
        grad_block = lax.dynamic_slice_in_dim(heads_grad_low, block_index * QBLK, QBLK, 0)
        weight_grads = jnp.einsum(
            "qhd,khd->hqk", grad_block, value_heads, preferred_element_type=jnp.float32
        )
        row_dots = jnp.sum(probs * weight_grads, axis=-1, keepdims=True)
        score_grads = (probs * (weight_grads - row_dots)).astype(jnp.bfloat16)
        query_grad_block = jnp.einsum(
            "hqk,khd->qhd", score_grads, key_heads, preferred_element_type=jnp.float32
        )
        key_acc = key_acc + jnp.einsum(
            "hqk,qhd->khd", score_grads, query_block, preferred_element_type=jnp.float32
        )
        value_acc = value_acc + jnp.einsum(
            "hqk,qhd->khd", probs_low, grad_block, preferred_element_type=jnp.float32
        )
        return ((key_acc, value_acc), query_grad_block)

    zero_heads = jnp.zeros((group_rows, local_heads, head_size), jnp.float32)
    (key_grad, value_grad), query_grads = lax.scan(
        back_block, (zero_heads, zero_heads), (jnp.arange(blocks), log_totals)
    )
    query_normed_grad, key_normed_grad = turn_back(
        (query_grads.reshape(group_rows, local_width), key_grad.reshape(group_rows, local_width))
    )
    query_gain_part = jnp.sum(query_normed_grad * query_proj * query_inverse, axis=0)
    key_gain_part = jnp.sum(key_normed_grad * key_proj * key_inverse, axis=0)
    query_gained = query_normed_grad * query_scale
    key_gained = key_normed_grad * key_scale
    query_dot, key_dot = lax.psum(
        (jnp.sum(query_proj * query_gained, axis=1), jnp.sum(key_proj * key_gained, axis=1)),
        "narrow",
    )
    query_proj_grad = (
        query_inverse * query_gained
        - query_proj * query_inverse**3 * (query_dot / model_width)[:, None]
    )
    key_proj_grad = (
        key_inverse * key_gained - key_proj * key_inverse**3 * (key_dot / model_width)[:, None]
    )
    proj_grad_low = jnp.concatenate(
        [query_proj_grad, key_proj_grad, value_grad.reshape(group_rows, local_width)], axis=1
    ).astype(jnp.bfloat16)
    joined_grad = contract_rows(normed_one, proj_grad_low)
    normed_one_grad = lax.psum_scatter(
        contract_last(proj_grad_low, joined_weight).astype(jnp.bfloat16),
        "narrow",
        scatter_dimension=0,
        tiled=True,
    ).astype(jnp.float32)
    normed_again, norm_one_back = jax.vjp(rms_scale, input_own, attn_gain.astype(jnp.float32))
    input_path, attn_gain_part = norm_one_back(normed_one_grad)
    input_grad = (hidden_grad + input_path).astype(jnp.bfloat16)
    summed = (
        lax.psum(joined_grad[:, :local_width].astype(jnp.bfloat16), "wide").astype(jnp.float32),
        lax.psum(joined_grad[:, local_width : 2 * local_width].astype(jnp.bfloat16), "wide").astype(
            jnp.float32
        ),
        lax.psum(joined_grad[:, 2 * local_width :].astype(jnp.bfloat16), "wide").astype(
            jnp.float32
        ),
        lax.psum(out_weight_acc.astype(jnp.bfloat16), "wide").astype(jnp.float32),
        lax.psum(query_gain_part.astype(jnp.bfloat16), "wide").astype(jnp.float32),
        lax.psum(key_gain_part.astype(jnp.bfloat16), "wide").astype(jnp.float32),
    )
    (
        query_weight_grad,
        key_weight_grad,
        value_weight_grad,
        out_weight_grad,
        query_gain_grad,
        key_gain_grad,
    ) = summed
    router_weight_grad, attn_gain_grad, moe_gain_grad = lax.psum(
        (router_part, attn_gain_part, moe_gain_part), ("wide", "narrow")
    )
    return (
        block_output,
        input_grad,
        attn_gain_grad,
        query_weight_grad,
        key_weight_grad,
        value_weight_grad,
        query_gain_grad,
        key_gain_grad,
        out_weight_grad,
        moe_gain_grad,
        router_weight_grad,
        gate_weight_grad,
        up_weight_grad,
        down_weight_grad,
    )


def solution(mesh):
    in_specs = (
        P("wide", None),
        P(),
        P(None, "narrow"),
        P(None, "narrow"),
        P(None, "narrow"),
        P("narrow"),
        P("narrow"),
        P("narrow", None),
        P(),
        P(),
        P("wide", None, "narrow"),
        P("wide", None, "narrow"),
        P("wide", "narrow", None),
        P("wide"),
        P(("wide", "narrow"), None),
        P(("wide", "narrow"), None),
    )
    out_specs = (
        P(("wide", "narrow"), None),
        P(("wide", "narrow"), None),
        P(),
        P(None, "narrow"),
        P(None, "narrow"),
        P(None, "narrow"),
        P("narrow"),
        P("narrow"),
        P("narrow", None),
        P(),
        P(),
        P("wide", None, "narrow"),
        P("wide", None, "narrow"),
        P("wide", "narrow", None),
    )
    return jax.shard_map(local, mesh=mesh, in_specs=in_specs, out_specs=out_specs, check_vma=False)
```

profile of v0, /device:TPU:0, one launch (start us, length us, event | category | flops | bytes accessed | tf_op | source)
XLA Modules:
  0.0 2144.4 jit_solution(17642516615929906324)
XLA Ops:
  22.5 8.4 all-reduce.8
  56.7 9.0 reduce-window.6
  70.9 12.6 reduce-scatter.11.cloned.1.call-done
  94.8 143.5 %all_to_all.20 = bf16[8,4,48,2048]{3,2,1,0:T(8,128)(2,1)S(1)} all-to-all(bf16[8,4,48,2048]{3,2,1,0:T(8,128)(2,1)} %bitcast.247), channel_id=1, replica_groups=mesh['wide'=8,'narrow'=4] {'wide'}, dimensions={0} | all-to-all | bytes 12582912 | tf_op jit(solution)/shard_map/all_to_all | solution.py:184
  241.6 152.0 %all-gather.4.cloned.1.call-done = bf16[32,4,48,2048]{3,2,0,1:T(8,128)(2,1)} async-done(((bf16[8,4,48,2048]{3,2,0,1:T(8,128)(2,1)}), bf16[32,4,48,2048]{3,2,0,1:T(8,128)(2,1)}) %all-gather.4.cloned.1.call-update) | async-done | bytes 25165840 | tf_op jit(solution)/shard_map/all_gather | solution.py:188
  393.6 14.6 fusion.14
  408.1 16.0 fusion.5
  424.2 14.4 convert_bitcast_fusion
  438.6 11.9 copy.169
  450.5 41.1 %copy.181 = bf16[4,8,192,2048]{3,1,2,0:T(8,128)(2,1)} copy(bf16[4,8,192,2048]{3,2,1,0:T(8,128)(2,1)S(1)} %bitcast.242) | data formatting | bytes 50331648
  491.6 182.1 %reduce-scatter.15.cloned.1.call-done = bf16[8,393216]{1,0:T(8,128)(2,1)} async-done(((bf16[32,393216]{1,0:T(8,128)(2,1)}), bf16[8,393216]{1,0:T(8,128)(2,1)}) %reduce-scatter.15.cloned.1.call-update) | async-done | bytes 6291472
  673.7 8.8 copy.182
  699.1 127.0 %all-to-all-done.1 = bf16[8,4,48,2048]{3,2,1,0:T(8,128)(2,1)} async-done(((bf16[8,4,48,2048]{3,2,1,0:T(8,128)(2,1)}), bf16[8,4,48,2048]{3,2,1,0:T(8,128)(2,1)}, u32[]{:S(2)}, u32[]{:S(2)}) %all-to-all-start.1) | async-done | bytes 6291488 | tf_op jit(solution)/shard_map/all_to_all | solution.py:234
  826.1 12.5 gather_fusion.1
  864.1 141.9 %all_to_all.21 = bf16[8,4,48,2048]{3,2,1,0:T(8,128)(2,1)S(1)} all-to-all(bf16[8,4,48,2048]{3,2,1,0:T(8,128)(2,1)} %multiply_convert_fusion), channel_id=1, replica_groups=mesh['wide'=8,'narrow'=4] {'wide'}, dimensions={0} | all-to-all | bytes 12582912 | tf_op jit(solution)/shard_map/all_to_all | solution.py:185
  1009.3 152.0 %all-gather.6.cloned.1.call-done = bf16[32,4,48,2048]{3,2,0,1:T(8,128)(2,1)} async-done(((bf16[8,4,48,2048]{3,2,0,1:T(8,128)(2,1)}), bf16[32,4,48,2048]{3,2,0,1:T(8,128)(2,1)}) %all-gather.6.cloned.1.call-update) | async-done | bytes 25165840 | tf_op jit(solution)/shard_map/all_gather | solution.py:189
  1161.3 19.3 fusion.4
  1180.6 21.4 fusion.12
  1202.0 28.9 %fusion = bf16[32,4,48,2048]{3,2,0,1:T(8,128)(2,1)} fusion(f32[4,32,48,2048]{3,2,1,0:T(8,128)} %fusion.12, bf16[32,4,48,256]{3,2,0,1:T(8,128)(2,1)} %get-tuple-element.99, bf16[4,2048,256]{2,1,0:T(8,128)(2,1)} %param.27), kind=kOutput, calls=%fused_computation.8 | convolution fusion | flops 6467616768 | bytes 82837504 | tf_op jit(solution)/shard_map/secf,edf->secd/dot_general | solution.py:226
  1230.9 11.9 copy.171
  1242.9 41.1 %copy.183 = bf16[4,8,192,2048]{3,1,2,0:T(8,128)(2,1)} copy(bf16[4,8,192,2048]{3,2,1,0:T(8,128)(2,1)S(1)} %bitcast.243) | data formatting | bytes 50331648
  1284.1 182.0 %reduce-scatter.17.cloned.1.call-done = bf16[8,393216]{1,0:T(8,128)(2,1)} async-done(((bf16[32,393216]{1,0:T(8,128)(2,1)}), bf16[8,393216]{1,0:T(8,128)(2,1)}) %reduce-scatter.17.cloned.1.call-update) | async-done | bytes 6291472
  1472.3 143.4 %all_to_all.22 = bf16[8,4,48,2048]{3,2,1,0:T(8,128)(2,1)} all-to-all(bf16[8,4,48,2048]{3,2,1,0:T(8,128)(2,1)S(1)} %bitcast.246), channel_id=1, replica_groups=mesh['wide'=8,'narrow'=4] {'wide'}, dimensions={0} | all-to-all | bytes 12582912 | tf_op jit(solution)/shard_map/all_to_all | solution.py:235
  1615.7 12.4 gather_fusion.3
  1636.8 20.5 all-gather.8.cloned.1.call-done
  1716.0 17.9 convolution_bitcast_fusion
  1733.9 17.1 convolution_bitcast_fusion.1
  1751.0 16.4 convolution_bitcast_fusion.2
  1767.4 22.7 %all-reduce.9 = (bf16[512]{0:T(512)(128)(2,1)S(1)}, bf16[512]{0:T(512)(128)(2,1)S(1)}) all-reduce(bf16[512]{0:T(512)(128)(2,1)S(1)} %get-tuple-element.78, bf16[512]{0:T(512)(128)(2,1)S(1)} %get-tuple-element.62), channel_id=1, replica_groups=mesh['wide'=8,'narrow'=4] {'wide'}, use_global_device_ids=true, to_apply=%region_35.36 | all-reduce | flops 1024 | bytes 4096 | tf_op jit(solution)/shard_map/psum | solution.py:343
  1796.7 40.5 %all-reduce.6 = (f32[2048]{0:T(1024)}, f32[2048]{0:T(1024)}) all-reduce(f32[2048]{0:T(1024)S(1)} %get-tuple-element.60, f32[2048]{0:T(1024)S(1)} %get-tuple-element.81), channel_id=1, replica_groups=mesh['wide'=8,'narrow'=4] {'wide','narrow'}, use_global_device_ids=true, to_apply=%region_30.31 | all-reduce | flops 4096 | bytes 32768 | tf_op jit(solution)/shard_map/psum | solution.py:354
  1837.2 166.7 %all-reduce.16.cloned.1.call-done = (bf16[2048,512]{1,0:T(8,128)(2,1)}, bf16[2048,512]{1,0:T(8,128)(2,1)}, bf16[2048,512]{1,0:T(8,128)(2,1)}, bf16[512,2048]{1,0:T(8,128)(2,1)}) async-done(((bf16[2048,512]{1,0:T(8,128)(2,1)}, bf16[2048,512]{1,0:T(8,128)(2,1)}, bf16[2048,512]{1,0:T(8,128)(2,1)}, bf16[512,2048]{1,0:T(8,128)(2,1)}), (bf16[2048,512]{1,0:T(8,128)(2,1)}, bf16[2048,512]{1,0:T(8,128)(2,1)}, ...) | async-done | bytes 8388624 | tf_op jit(solution)/shard_map/psum | solution.py:335
  2016.1 119.7 %all-reduce.14.cloned.1.call-done = f32[2048,32]{0,1:T(8,128)} async-done(((f32[2048,32]{0,1:T(8,128)}), f32[2048,32]{0,1:T(8,128)}) %all-reduce.14.cloned.1.call-update) | async-done | bytes 262160 | tf_op jit(solution)/shard_map/psum | solution.py:354
  (291 shorter events, 199.3 us)
Async XLA Ops:
  7.2 42.0 %copy-start = (bf16[512,2048]{1,0:T(8,128)(2,1)S(1)}, bf16[512,2048]{1,0:T(8,128)(2,1)}, u32[]{:S(2)}) copy-start(bf16[512,2048]{1,0:T(8,128)(2,1)} %param.23) | copy-start | bytes 6291460
  7.2 76.4 %reduce-scatter.11.cloned.1.call-start = ((), (), s32[]{:S(2)}) async-start(), calls=%async_computation.8 | async-start | bytes 2621440 | tf_op jit(solution)/shard_map/reduce_scatter | solution.py:148
  7.2 7.6 copy-start.32
  7.3 7.7 copy-start.33
  8.1 23.4 %copy-start.55 = (f32[512]{0:T(512)}, f32[512]{0:T(512)S(1)}, u32[]{:S(2)}) copy-start(f32[512]{0:T(512)S(1)} %convert_element_type.153) | copy-start | bytes 6148
  9.3 22.2 %copy-start.57 = (f32[512]{0:T(512)}, f32[512]{0:T(512)S(1)}, u32[]{:S(2)}) copy-start(f32[512]{0:T(512)S(1)} %convert_element_type.155) | copy-start | bytes 6148
  13.1 32.1 %copy-start.15 = (pred[512,512]{0,1:T(8,128)(4,1)}, pred[512,512]{0,1:T(8,128)(4,1)S(1)}, u32[]{:S(2)}) copy-start(pred[512,512]{0,1:T(8,128)(4,1)S(1)} %fusion.53) | copy-start | bytes 786436
  51.8 14.4 copy-start.74
  51.8 14.5 copy-start.73
  51.8 341.7 %all-gather.4.cloned.1.call-start = ((), (), s32[]{:S(2)}) async-start(), calls=%async_computation.9 | async-start | bytes 31457280 | tf_op jit(solution)/shard_map/all_gather | solution.py:188
  56.6 29.2 %copy-start.46 = (f32[2048]{0:T(1024)}, f32[2048]{0:T(1024)S(1)}, u32[]{:S(2)}) copy-start(f32[2048]{0:T(1024)S(1)} %convert_element_type.162) | copy-start | bytes 24580
  66.4 19.4 copy-start.70
  85.8 9.0 copy-start.76
  85.8 9.0 copy-start.67
  241.5 432.2 %reduce-scatter.15.cloned.1.call-start = ((), (), s32[]{:S(2)}) async-start(), calls=%async_computation.14 | async-start | bytes 31457280
  393.6 14.6 copy-start.25
  682.5 143.6 %all-to-all-start.1 = ((bf16[8,4,48,2048]{3,2,1,0:T(8,128)(2,1)}), bf16[8,4,48,2048]{3,2,1,0:T(8,128)(2,1)}, u32[]{:S(2)}, u32[]{:S(2)}) async-start(bf16[8,4,48,2048]{3,2,1,0:T(8,128)(2,1)} %bitcast.245), calls=%async_computation.2 | async-start | bytes 12582912 | tf_op jit(solution)/shard_map/all_to_all | solution.py:234
  688.0 473.2 %all-gather.6.cloned.1.call-start = ((), (), s32[]{:S(2)}) async-start(), calls=%async_computation.10 | async-start | bytes 31457280 | tf_op jit(solution)/shard_map/all_gather | solution.py:189
  689.4 8.3 copy-start.44
  826.1 12.5 copy-start.19
  851.4 12.7 copy-start.52
  1009.2 456.9 %reduce-scatter.17.cloned.1.call-start = ((), (), s32[]{:S(2)}) async-start(), calls=%async_computation.15 | async-start | bytes 31457280
  1284.0 373.3 %all-gather.8.cloned.1.call-start = ((), (), s32[]{:S(2)}) async-start(), calls=%async_computation.11 | async-start | bytes 2621440 | tf_op jit(solution)/shard_map/all_gather | solution.py:271
  1628.1 6.2 copy-start.77
  1628.1 7.2 copy-start.20
  1636.5 23.9 %copy-start.16 = (pred[512,512]{0,1:T(8,128)(4,1)S(1)}, pred[512,512]{0,1:T(8,128)(4,1)}, u32[]{:S(2)}) copy-start(pred[512,512]{0,1:T(8,128)(4,1)} %copy-done.15) | copy-start | bytes 786436
  1636.5 154.7 %reduce-scatter.13.cloned.1.call-start = ((), (), s32[]{:S(2)}) async-start(), calls=%async_computation.12 | async-start | bytes 2621440 | tf_op jit(solution)/shard_map/reduce_scatter | solution.py:325
  1666.3 5.8 copy-start.27
  1675.3 7.8 copy-start.65
  1675.3 7.8 copy-start.66
  1695.0 308.9 %all-reduce.16.cloned.1.call-start = ((), (), s32[]{:S(2)}) async-start(), calls=%async_computation.16 | async-start | bytes 16777216 | tf_op jit(solution)/shard_map/psum | solution.py:335
  1706.5 429.3 %all-reduce.14.cloned.1.call-start = ((), (), s32[]{:S(2)}) async-start(), calls=%async_computation.13 | async-start | bytes 524288 | tf_op jit(solution)/shard_map/psum | solution.py:354
  (57 other events, 170.7 us)
Sparse Core Ops, SparseCore 0:
  51.9 31.5 reduce-scatter.10
  241.7 151.8 all-gather.3
  491.8 181.8 reduce-scatter.14
  1009.3 151.8 all-gather.5
  1284.1 181.8 reduce-scatter.16
  1636.7 20.6 all-gather.7
  1695.1 32.2 reduce-scatter.12
  1732.5 271.3 all-reduce.15
  2010.1 125.6 all-reduce.13
where the time goes:
time: 2150 us; the launch traced here: 2140 us
  waiting for transfers between devices  1110 us (52%)
  blocking collectives  506 us (24%)
  matrix products  220 us (10%)
  local copies, waits for them, and re-layouts  210 us (10%)
  other arithmetic  71.1 us (3%)
    unnamed x11, waiting for transfers between devices  364 us
    psum x1, waiting for transfers between devices, local(): lax.psum(joined_grad[:, :local_width].astype(jnp.bfloat16), 'wide')  167 us
    all_gather x1, waiting for transfers between devices, local(): lax.all_gather(recv_grads, 'narrow', axis=0, tiled=True)  152 us
    all_gather x1, waiting for transfers between devices, local(): lax.all_gather(recv_rows, 'narrow', axis=0, tiled=True)  152 us
    all_to_all x1, blocking collectives, local(): lax.all_to_all(send_rows, 'wide', split_axis=0, concat_axis=0, tiled=True)  143 us
    all_to_all x1, blocking collectives, local(): lax.all_to_all(back_mine, 'wide', split_axis=0, concat_axis=0, tiled=True)  143 us
    unnamed x170, local copies, waits for them, and re-layouts  142 us
    all_to_all x1, blocking collectives, local(): lax.all_to_all(send_grads, 'wide', split_axis=0, concat_axis=0, tiled=True)  142 us
  transfers between devices with their start and end apart: 10, of which 9 were waited for; matrix products, arithmetic and copies ran while one was open for 6% of the time, Pallas kernels for 0%

commit v1 on v0

--- a/solution.py
+++ b/solution.py
@@ -56,6 +56,17 @@
     return lax.dot_general(
         left, right, (((1,), (1,)), ((), ())), preferred_element_type=jnp.float32
     )
+
+
+BOTH = ("wide", "narrow")
+
+
+def gather_all(block):
+    return lax.all_gather(block, BOTH, axis=0, tiled=True)
+
+
+def scatter_all(parts):
+    return lax.psum_scatter(parts, BOTH, scatter_dimension=0, tiled=True)
 
 
 def local(
@@ -89,6 +100,16 @@
     row_begin = lax.axis_index("narrow") * own_rows
     blocks = group_rows // QBLK
     highest_precision = lax.Precision.HIGHEST
+    block_count = wide_size * lax.axis_size("narrow")
+    chosen = (expert_ids[:, :, None] == jnp.arange(experts_all)[None, None, :]).any(axis=1)
+    token_order = jnp.arange(own_rows)
+    earlier = jnp.dot(
+        (token_order[:, None] > token_order[None, :]).astype(jnp.bfloat16),
+        chosen.astype(jnp.bfloat16),
+        preferred_element_type=jnp.float32,
+    )
+    places_all = gather_all(jnp.where(chosen, earlier, -1.0).T)
+    grads_all = gather_all(out_cotangent)
     inputs_all = block_input.astype(jnp.float32)
     normed_one = rms_scale(inputs_all, attn_gain.astype(jnp.float32)).astype(jnp.bfloat16)
     joined_weight = jnp.concatenate([query_weight, key_weight, value_weight], axis=1)
@@ -157,93 +178,79 @@
     normed_two = normed_two_full.astype(jnp.bfloat16)
     logits = jnp.dot(normed_two, router_weight, preferred_element_type=jnp.float32)
     route_probs = jax.nn.softmax(logits, axis=-1)
-    gates = jnp.take_along_axis(route_probs, expert_ids, axis=1)
-    flat_ids = expert_ids.reshape(-1)
-    expert_match = (flat_ids[:, None] == jnp.arange(experts_all)[None, :]).astype(jnp.int32)
-    earlier = jnp.cumsum(expert_match, axis=0) - expert_match
-    slot_of = jnp.sum(earlier * expert_match, axis=1)
-    token_of = jnp.arange(own_rows * choose_count) // choose_count
-    slot_token = (
-        jnp.full((experts_all, capacity), own_rows, jnp.int32).at[flat_ids, slot_of].set(token_of)
-    )
-    slot_gate = (
-        jnp.zeros((experts_all, capacity), jnp.float32).at[flat_ids, slot_of].set(gates.reshape(-1))
-    )
-    padded_rows = jnp.concatenate([normed_two, jnp.zeros((1, model_width), jnp.bfloat16)], axis=0)
-    cotangent_full = out_cotangent.astype(jnp.float32)
-    padded_grads = jnp.concatenate(
-        [cotangent_full, jnp.zeros((1, model_width), jnp.float32)], axis=0
-    )
-    send_rows = padded_rows[slot_token].reshape(wide_size, experts_here, capacity, model_width)
-    send_grads = (
-        (padded_grads[slot_token] * slot_gate[:, :, None])
-        .astype(jnp.bfloat16)
-        .reshape(wide_size, experts_here, capacity, model_width)
-    )
-    recv_rows, recv_grads = (
-        lax.all_to_all(send_rows, "wide", split_axis=0, concat_axis=0, tiled=True),
-        lax.all_to_all(send_grads, "wide", split_axis=0, concat_axis=0, tiled=True),
-    )
-    all_rows, all_grads = (
-        lax.all_gather(recv_rows, "narrow", axis=0, tiled=True),
-        lax.all_gather(recv_grads, "narrow", axis=0, tiled=True),
-    )
-    gate_pre = jnp.einsum(
-        "secd,edf->secf", all_rows, gate_weight, preferred_element_type=jnp.float32
-    )
-    up_pre = jnp.einsum("secd,edf->secf", all_rows, up_weight, preferred_element_type=jnp.float32)
+    rows_all = gather_all(normed_two)
+    probs_all = gather_all(route_probs.T)
+    expert_begin = lax.axis_index("wide") * experts_here
+    places_here = lax.dynamic_slice_in_dim(
+        places_all.reshape(block_count, experts_all, own_rows), expert_begin, experts_here, 1
+    )
+    probs_here = lax.dynamic_slice_in_dim(
+        probs_all.reshape(block_count, experts_all, own_rows), expert_begin, experts_here, 1
+    )
+    pick = places_here[:, :, None, :] == jnp.arange(capacity, dtype=jnp.float32)[None, None, :, None]
+    pick_low = pick.astype(jnp.bfloat16)
+    slot_gate = jnp.sum(jnp.where(pick, probs_here[:, :, None, :], 0.0), axis=-1)
+    slot_gate = slot_gate.transpose(1, 0, 2).reshape(experts_here, block_count * capacity, 1)
+
+    def spread(rows):
+        out = jnp.einsum(
+            "best,btd->ebsd",
+            pick_low,
+            rows.reshape(block_count, own_rows, model_width),
+            preferred_element_type=jnp.float32,
+        )
+        return out.astype(jnp.bfloat16).reshape(experts_here, block_count * capacity, model_width)
+
+    def collect(slots):
+        out = jnp.einsum(
+            "best,ebsd->btd",
+            pick_low,
+            slots.reshape(experts_here, block_count, capacity, model_width),
+            preferred_element_type=jnp.float32,
+        )
+        return out.astype(jnp.bfloat16).reshape(block_count * own_rows, model_width)
+
+    slot_rows = spread(rows_all)
+    slot_grads = spread(grads_all)
+    gate_pre = jnp.einsum("erd,edf->erf", slot_rows, gate_weight, preferred_element_type=jnp.float32)
+    up_pre = jnp.einsum("erd,edf->erf", slot_rows, up_weight, preferred_element_type=jnp.float32)
     activated, unit_back = jax.vjp(gated_unit, gate_pre, up_pre)
-    act_low = activated.astype(jnp.bfloat16)
-    expert_mine = lax.psum_scatter(
-        jnp.einsum(
-            "secf,efd->secd", act_low, down_weight, preferred_element_type=jnp.float32
-        ).astype(jnp.bfloat16),
-        "narrow",
-        scatter_dimension=0,
-        tiled=True,
-    )
-    act_grad = jnp.einsum(
-        "secd,efd->secf", all_grads, down_weight, preferred_element_type=jnp.float32
-    )
-    gate_grad_full, up_grad_full = unit_back(act_grad)
+    gated_act = (activated * slot_gate).astype(jnp.bfloat16)
+    raw_act_grad = jnp.einsum(
+        "erd,efd->erf", slot_grads, down_weight, preferred_element_type=jnp.float32
+    )
+    slot_gate_grads = jnp.sum(activated * raw_act_grad, axis=-1)
+    gate_grad_full, up_grad_full = unit_back(raw_act_grad * slot_gate)
     gate_grad_low = gate_grad_full.astype(jnp.bfloat16)
     up_grad_low = up_grad_full.astype(jnp.bfloat16)
+    gate_grad_parts = jnp.einsum(
+        "best,ebs->bet",
+        pick.astype(jnp.float32),
+        slot_gate_grads.reshape(experts_here, block_count, capacity),
+        precision=highest_precision,
+    )
+    gate_grad_wide = lax.dynamic_update_slice_in_dim(
+        jnp.zeros((block_count, experts_all, own_rows), jnp.float32), gate_grad_parts, expert_begin, 1
+    )
+    prob_grads = scatter_all(gate_grad_wide.reshape(block_count * experts_all, own_rows)).T
+    back_slots = jnp.einsum(
+        "erf,edf->erd", gate_grad_low, gate_weight, preferred_element_type=jnp.float32
+    ) + jnp.einsum("erf,edf->erd", up_grad_low, up_weight, preferred_element_type=jnp.float32)
+    rows_back = scatter_all(collect(back_slots.astype(jnp.bfloat16))).astype(jnp.float32)
+    out_slots = jnp.einsum(
+        "erf,efd->erd", gated_act, down_weight, preferred_element_type=jnp.float32
+    )
+    moe_out = scatter_all(collect(out_slots.astype(jnp.bfloat16))).astype(jnp.float32)
     down_weight_grad = jnp.einsum(
-        "secf,secd->efd", act_low, all_grads, preferred_element_type=jnp.float32
+        "erf,erd->efd", gated_act, slot_grads, preferred_element_type=jnp.float32
     )
     gate_weight_grad = jnp.einsum(
-        "secd,secf->edf", all_rows, gate_grad_low, preferred_element_type=jnp.float32
+        "erd,erf->edf", slot_rows, gate_grad_low, preferred_element_type=jnp.float32
     )
     up_weight_grad = jnp.einsum(
-        "secd,secf->edf", all_rows, up_grad_low, preferred_element_type=jnp.float32
-    )
-    gate_term = jnp.einsum(
-        "secf,edf->secd", gate_grad_low, gate_weight, preferred_element_type=jnp.float32
-    )
-    back_mine = lax.psum_scatter(
-        (
-            gate_term
-            + jnp.einsum(
-                "secf,edf->secd", up_grad_low, up_weight, preferred_element_type=jnp.float32
-            )
-        ).astype(jnp.bfloat16),
-        "narrow",
-        scatter_dimension=0,
-        tiled=True,
-    )
-    expert_back = lax.all_to_all(expert_mine, "wide", split_axis=0, concat_axis=0, tiled=True)
-    input_back = lax.all_to_all(back_mine, "wide", split_axis=0, concat_axis=0, tiled=True)
-    gather_index = flat_ids * capacity + slot_of
-    returned = (
-        expert_back.reshape(-1, model_width)[gather_index]
-        .reshape(own_rows, choose_count, model_width)
-        .astype(jnp.float32)
-    )
-    moe_out = jnp.einsum("tk,tkd->td", gates, returned, precision=highest_precision)
+        "erd,erf->edf", slot_rows, up_grad_low, preferred_element_type=jnp.float32
+    )
     block_output = (hidden + moe_out).astype(jnp.bfloat16)
-    gate_grads = jnp.einsum("td,tkd->tk", cotangent_full, returned, precision=highest_precision)
-    picked = (expert_ids[:, :, None] == jnp.arange(experts_all)[None, None, :]).astype(jnp.float32)
-    prob_grads = jnp.einsum("tk,tke->te", gate_grads, picked, precision=highest_precision)
     logit_grads = route_probs * (
         prob_grads - jnp.sum(route_probs * prob_grads, axis=-1, keepdims=True)
     )
@@ -253,18 +260,14 @@
         (((0,), (0,)), ((), ())),
         precision=highest_precision,
     )
-    rows_back = (
-        input_back.reshape(-1, model_width)[gather_index]
-        .reshape(own_rows, choose_count, model_width)
-        .astype(jnp.float32)
-    )
     router_back = lax.dot_general(
         logit_grads,
         router_weight.astype(jnp.float32),
         (((1,), (1,)), ((), ())),
         precision=highest_precision,
     )
-    normed_two_grad = jnp.sum(rows_back, axis=1) + router_back
+    normed_two_grad = rows_back + router_back
+    cotangent_full = out_cotangent.astype(jnp.float32)
     hidden_path, moe_gain_part = norm_two_back(normed_two_grad)
     hidden_grad = cotangent_full + hidden_path
     hidden_grad_low = hidden_grad.astype(jnp.bfloat16)

time: 2150 us -> 1420 us (0.66)
  blocking collectives: 506 us -> 167 us
  waiting for transfers between devices: 1110 us -> 822 us
  local copies, waits for them, and re-layouts: 210 us -> 67.2 us
  matrix products: 220 us -> 281 us
    all_to_all x3 -> x0, blocking collectives: 429 us -> none  [the longest x1 143 us: local(): lax.all_to_all(send_rows, 'wide', split_axis=0, concat_axis=0, tiled=True)]
    unnamed x11 -> x10, waiting for transfers between devices: 364 us -> 0.67 us
    reduce_scatter x0 -> x3, waiting for transfers between devices: none -> 345 us  [scatter_all(): return lax.psum_scatter(parts, BOTH, scatter_dimension=0, tiled=True)]
    all_gather x2, waiting for transfers between devices: 304 us -> 77.1 us  [gather_all(): return lax.all_gather(block, BOTH, axis=0, tiled=True)]
    unnamed x170 -> x161, local copies, waits for them, and re-layouts: 142 us -> 12.6 us
    all_to_all x1 -> x0, waiting for transfers between devices: 127 us -> none  [local(): lax.all_to_all(expert_mine, 'wide', split_axis=0, concat_axis=0, tiled=True)]
    all_gather x0 -> x2, blocking collectives: none -> 86.2 us  [gather_all(): return lax.all_gather(block, BOTH, axis=0, tiled=True)]
    psum x1, waiting for transfers between devices: 167 us -> 230 us  [local(): lax.psum(joined_grad[:, :local_width].astype(jnp.bfloat16), 'wide')]
  transfers between devices with their start and end apart: 10 -> 10, of which waited for: 9 -> 8; matrix products, arithmetic and copies ran while one was open for 6% -> 16% of each run, Pallas kernels for 0% -> 0%
where the time goes in v1:
time: 1420 us; the launch traced here: 1410 us
  waiting for transfers between devices  822 us (58%)
  matrix products  281 us (20%)
  blocking collectives  167 us (12%)
  local copies, waits for them, and re-layouts  67.2 us (5%)
  other arithmetic  51.8 us (4%)
  between operations  17.1 us (1%)
    reduce_scatter x3, waiting for transfers between devices, scatter_all(): return lax.psum_scatter(parts, BOTH, scatter_dimension=0, tiled=True)  345 us
    psum x1, waiting for transfers between devices, local(): lax.psum(joined_grad[:, :local_width].astype(jnp.bfloat16), 'wide')  230 us
    psum x1, waiting for transfers between devices, local(): lax.psum((router_part, attn_gain_part, moe_gain_part), ('wide', 'narrow'))  120 us
    all_gather x2, blocking collectives, gather_all(): return lax.all_gather(block, BOTH, axis=0, tiled=True)  86.2 us
    all_gather x2, waiting for transfers between devices, gather_all(): return lax.all_gather(block, BOTH, axis=0, tiled=True)  77.1 us
    psum x1, blocking collectives, local(): lax.psum((router_part, attn_gain_part, moe_gain_part), ('wide', 'narrow'))  44.4 us
    convert_element_type x2, local copies, waits for them, and re-layouts, spread(): out.astype(jnp.bfloat16)  42.3 us
    dot_general x2, matrix products, spread(): jnp.einsum('best,btd->ebsd', pick_low, rows.reshape(block_count, own_rows...  36.3 us
  transfers between devices with their start and end apart: 10, of which 8 were waited for; matrix products, arithmetic and copies ran while one was open for 16% of the time, Pallas kernels for 0%

profile of v1, /device:TPU:0, one launch (start us, length us, event | category | flops | bytes accessed | tf_op | source)
XLA Modules:
  0.0 1406.7 jit_solution(8569591139823198937)
XLA Ops:
  23.3 8.4 all-reduce.6
  57.6 26.6 %reduce-scatter.6.cloned.1.call-done = bf16[128,2048]{1,0:T(8,128)(2,1)} async-done(((bf16[512,2048]{1,0:T(8,128)(2,1)}), bf16[128,2048]{1,0:T(8,128)(2,1)}) %reduce-scatter.6.cloned.1.call-update) | async-done | bytes 524304 | tf_op jit(solution)/shard_map/reduce_scatter | solution.py:169
  88.6 44.9 %all_gather.15 = f32[1024,128]{1,0:T(8,128)S(1)} all-gather(f32[32,128]{1,0:T(8,128)S(1)} %convolution_select_fusion), channel_id=1, replica_groups=mesh['wide'=8,'narrow'=4] {'wide','narrow'}, dimensions={0}, use_global_device_ids=true | all-gather | bytes 540672 | tf_op jit(solution)/shard_map/all_gather | solution.py:65
  135.5 41.3 %all_gather.17 = f32[1024,128]{1,0:T(8,128)S(1)} all-gather(f32[32,128]{1,0:T(8,128)S(1)} %fusion.73), channel_id=1, replica_groups=mesh['wide'=8,'narrow'=4] {'wide','narrow'}, dimensions={0}, use_global_device_ids=true | all-gather | bytes 540672 | tf_op jit(solution)/shard_map/all_gather | solution.py:65
  177.9 17.1 %convert_bitcast_fusion = bf16[4,32,48,2048]{3,2,0,1:T(8,128)(2,1)} fusion(bf16[32,128,2048,1]{2,1,3,0:T(8,128)(2,1)} %bitcast.145, f32[32,4,128]{2,1,0:T(4,128)S(1)} %constant_dynamic-slice_fusion.1), kind=kOutput, calls=%fused_computation.8 | convolution fusion | flops 3234594816 | bytes 42008576 | tf_op jit(solution)/shard_map/best,btd->ebsd/dot_general | solution.py:196
  195.0 21.2 %copy.169 = bf16[4,32,48,2048]{3,2,1,0:T(8,128)(2,1)} copy(bf16[4,32,48,2048]{3,2,0,1:T(8,128)(2,1)} %convert_bitcast_fusion) | data formatting | bytes 50331648 | tf_op jit(solution)/shard_map/convert_element_type | solution.py:202
  216.1 77.1 %all-gather.4.cloned.1.call-done = bf16[4096,2048]{1,0:T(8,128)(2,1)} async-done(((bf16[128,2048]{1,0:T(8,128)(2,1)}), bf16[4096,2048]{1,0:T(8,128)(2,1)}) %all-gather.4.cloned.1.call-update) | async-done | bytes 16777232 | tf_op jit(solution)/shard_map/all_gather | solution.py:65
  293.2 19.2 %convert_bitcast_fusion.1 = bf16[4,32,48,2048]{3,2,0,1:T(8,128)(2,1)} fusion(bf16[32,128,2048,1]{2,1,3,0:T(8,128)(2,1)} %bitcast.144, f32[32,4,128]{2,1,0:T(4,128)S(1)} %constant_dynamic-slice_fusion.1), kind=kOutput, calls=%fused_computation.9 | convolution fusion | flops 3234594816 | bytes 42008576 | tf_op jit(solution)/shard_map/best,btd->ebsd/dot_general | solution.py:196
  312.5 21.1 %copy.163 = bf16[4,32,48,2048]{3,2,1,0:T(8,128)(2,1)} copy(bf16[4,32,48,2048]{3,2,0,1:T(8,128)(2,1)} %convert_bitcast_fusion.1) | data formatting | bytes 50331648 | tf_op jit(solution)/shard_map/convert_element_type | solution.py:202
  333.6 15.8 %fusion.80 = f32[4,1536,256]{1,2,0:T(8,128)} fusion(bf16[4,1536,2048]{2,1,0:T(8,128)(2,1)} %bitcast.148, bf16[4,2048,256]{2,1,0:T(8,128)(2,1)} %param.27), kind=kOutput, calls=%fused_computation.162 | convolution fusion | flops 6442450944 | bytes 35651584 | tf_op jit(solution)/shard_map/erd,edf->erf/dot_general | solution.py:216
  349.4 14.1 %fusion.79 = f32[4,1536,256]{1,2,0:T(8,128)} fusion(bf16[4,1536,2048]{2,1,0:T(8,128)(2,1)} %bitcast.149, bf16[4,2048,256]{2,1,0:T(8,128)(2,1)S(1)} %copy-done.23), kind=kOutput, calls=%fused_computation.161 | convolution fusion | flops 6442450944 | bytes 35651584 | tf_op jit(solution)/shard_map/erd,edf->erf/dot_general | solution.py:215
  363.5 21.7 %multiply_reduce_fusion = (f32[4,1536]{1,0:T(4,128)S(1)}, bf16[4,1536,256]{1,2,0:T(8,128)(2,1)}, bf16[4,1536,256]{1,2,0:T(8,128)(2,1)}, bf16[4,1536,256]{1,2,0:T(8,128)(2,1)}) fusion(f32[4,1536,256]{1,2,0:T(8,128)} %fusion.80, f32[4,1536,256]{1,2,0:T(8,128)} %fusion.79, f32[4,1536]{1,0:T(4,128)S(1)} %mul.639, bf16[4,1536,2048]{2,1,0:T(8,128)(2,1)} %bitcast.146, ...), kind=kOutput, calls=%fused_computation.15 | convolution fusion | flops 6473902080 | bytes 51429376 | tf_op jit(solution)/shard_map/erd,efd->erf/dot_general | solution.py:219
  387.7 21.1 %fusion.81 = f32[4,1536,2048]{2,1,0:T(8,128)} fusion(bf16[4,1536,256]{1,2,0:T(8,128)(2,1)} %get-tuple-element.98, bf16[4,2048,256]{2,1,0:T(8,128)(2,1)} %param.26), kind=kOutput, calls=%fused_computation.163 | convolution fusion | flops 6442450944 | bytes 57671680 | tf_op jit(solution)/shard_map/erf,edf->erd/dot_general | solution.py:236
  408.8 28.0 %add_convert_fusion = bf16[4,1536,2048]{2,1,0:T(8,128)(2,1)} fusion(f32[4,1536,2048]{2,1,0:T(8,128)} %fusion.81, bf16[4,1536,256]{1,2,0:T(8,128)(2,1)} %get-tuple-element.100, bf16[4,2048,256]{2,1,0:T(8,128)(2,1)} %param.27), kind=kOutput, calls=%fused_computation | convolution fusion | flops 6467616768 | bytes 82837504 | tf_op jit(solution)/shard_map/erf,edf->erd/dot_general | solution.py:238
  436.8 16.8 %bitcast_convert_fusion = bf16[32,128,2048]{2,1,0:T(8,128)(2,1)} fusion(bf16[4,32,48,2048]{3,2,1,0:T(8,128)(2,1)} %bitcast.140, f32[32,4,128]{2,1,0:T(4,128)S(1)} %constant_dynamic-slice_fusion.1), kind=kOutput, calls=%fused_computation.1 | convolution fusion | flops 3230400512 | bytes 42008576 | tf_op jit(solution)/shard_map/best,ebsd->btd/dot_general | solution.py:205
  453.9 67.8 %reduce-scatter.12.cloned.1.call-done = f32[32,128]{1,0:T(8,128)} async-done(((f32[1024,128]{1,0:T(8,128)}), f32[32,128]{1,0:T(8,128)}) %reduce-scatter.12.cloned.1.call-update) | async-done | bytes 16400 | tf_op jit(solution)/shard_map/reduce_scatter | solution.py:69
  522.4 180.6 %reduce-scatter.10.cloned.1.call-done = bf16[128,2048]{1,0:T(8,128)(2,1)} async-done(((bf16[4096,2048]{1,0:T(8,128)(2,1)}), bf16[128,2048]{1,0:T(8,128)(2,1)}) %reduce-scatter.10.cloned.1.call-update) | async-done | bytes 524304 | tf_op jit(solution)/shard_map/reduce_scatter | solution.py:69
  708.4 24.0 %all-gather.8.cloned.1.call-done = bf16[512,2048]{1,0:T(8,128)(2,1)} async-done(((bf16[128,2048]{1,0:T(8,128)(2,1)}), bf16[512,2048]{1,0:T(8,128)(2,1)}) %all-gather.8.cloned.1.call-update) | async-done | bytes 2097168 | tf_op jit(solution)/shard_map/all_gather | solution.py:274
  752.3 5.9 all-reduce.5
  762.6 7.4 convolution_convert_fusion.3
  770.3 14.8 %convolution_convert_fusion = bf16[4,1536,2048]{2,1,0:T(8,128)(2,1)} fusion(bf16[4,1536,256]{1,2,0:T(8,128)(2,1)} %get-tuple-element.99, bf16[4,256,2048]{2,1,0:T(8,128)(2,1)} %param.28), kind=kOutput, calls=%fused_computation.3 | convolution fusion | flops 6455033856 | bytes 32505856 | tf_op jit(solution)/shard_map/erf,efd->erd/dot_general | solution.py:240
  785.2 17.0 %bitcast_convert_fusion.1 = bf16[32,128,2048]{2,1,0:T(8,128)(2,1)} fusion(bf16[4,32,48,2048]{3,2,1,0:T(8,128)(2,1)} %bitcast.141, f32[32,4,128]{2,1,0:T(4,128)S(1)} %constant_dynamic-slice_fusion.1), kind=kOutput, calls=%fused_computation.2 | convolution fusion | flops 3230400512 | bytes 42008576 | tf_op jit(solution)/shard_map/best,ebsd->btd/dot_general | solution.py:205
  802.3 4.5 convolution_convert_fusion.2
  814.3 17.9 %fusion.84 = f32[4,256,2048]{2,1,0:T(8,128)} fusion(bf16[4,1536,256]{1,2,0:T(8,128)(2,1)} %get-tuple-element.99, bf16[4,1536,2048]{2,1,0:T(8,128)(2,1)} %bitcast.147), kind=kOutput, calls=%fused_computation.166 | convolution fusion | flops 6442450944 | bytes 36700160 | tf_op jit(solution)/shard_map/erf,erd->efd/dot_general | solution.py:244
  832.2 17.0 %fusion.82 = f32[4,2048,256]{2,1,0:T(8,128)} fusion(bf16[4,1536,2048]{2,1,0:T(8,128)(2,1)} %bitcast.150, bf16[4,1536,256]{1,2,0:T(8,128)(2,1)} %get-tuple-element.98), kind=kOutput, calls=%fused_computation.164 | convolution fusion | flops 6442450944 | bytes 36700160 | tf_op jit(solution)/shard_map/erd,erf->edf/dot_general | solution.py:247
  849.2 16.6 %fusion.83 = f32[4,2048,256]{2,1,0:T(8,128)} fusion(bf16[4,1536,2048]{2,1,0:T(8,128)(2,1)} %bitcast.151, bf16[4,1536,256]{1,2,0:T(8,128)(2,1)S(1)} %copy-done.24), kind=kOutput, calls=%fused_computation.165 | convolution fusion | flops 6442450944 | bytes 36700160 | tf_op jit(solution)/shard_map/erd,erf->edf/dot_general | solution.py:250
  866.9 21.8 %all-reduce.7 = (bf16[512]{0:T(512)(128)(2,1)S(1)}, bf16[512]{0:T(512)(128)(2,1)S(1)}) all-reduce(bf16[512]{0:T(512)(128)(2,1)S(1)} %get-tuple-element.78, bf16[512]{0:T(512)(128)(2,1)S(1)} %get-tuple-element.62), channel_id=1, replica_groups=mesh['wide'=8,'narrow'=4] {'wide'}, use_global_device_ids=true, to_apply=%region_33.34 | all-reduce | flops 1024 | bytes 4096 | tf_op jit(solution)/shard_map/psum | solution.py:346
  891.6 96.2 %reduce-scatter.8.cloned.1.call-done = bf16[128,2048]{1,0:T(8,128)(2,1)} async-done(((bf16[4096,2048]{1,0:T(8,128)(2,1)}), bf16[128,2048]{1,0:T(8,128)(2,1)}) %reduce-scatter.8.cloned.1.call-update) | async-done | bytes 524304 | tf_op jit(solution)/shard_map/reduce_scatter | solution.py:69
  991.2 44.4 %all-reduce.4 = (f32[2048]{0:T(1024)}, f32[2048]{0:T(1024)}) all-reduce(f32[2048]{0:T(1024)S(1)} %get-tuple-element.60, f32[2048]{0:T(1024)S(1)} %get-tuple-element.81), channel_id=1, replica_groups=mesh['wide'=8,'narrow'=4] {'wide','narrow'}, use_global_device_ids=true, to_apply=%region_28.29 | all-reduce | flops 4096 | bytes 32768 | tf_op jit(solution)/shard_map/psum | solution.py:357
  1035.6 229.8 %all-reduce.14.cloned.1.call-done = (bf16[2048,512]{1,0:T(8,128)(2,1)}, bf16[2048,512]{1,0:T(8,128)(2,1)}, bf16[2048,512]{1,0:T(8,128)(2,1)}, bf16[512,2048]{1,0:T(8,128)(2,1)}) async-done(((bf16[2048,512]{1,0:T(8,128)(2,1)}, bf16[2048,512]{1,0:T(8,128)(2,1)}, bf16[2048,512]{1,0:T(8,128)(2,1)}, bf16[512,2048]{1,0:T(8,128)(2,1)}), (bf16[2048,512]{1,0:T(8,128)(2,1)}, bf16[2048,512]{1,0:T(8,128)(2,1)}, ...) | async-done | bytes 8388624 | tf_op jit(solution)/shard_map/psum | solution.py:338
  1265.4 4.3 convert_element_type.189
  1277.5 119.5 %all-reduce.12.cloned.1.call-done = f32[2048,32]{0,1:T(8,128)} async-done(((f32[2048,32]{0,1:T(8,128)}), f32[2048,32]{0,1:T(8,128)}) %all-reduce.12.cloned.1.call-update) | async-done | bytes 262160 | tf_op jit(solution)/shard_map/psum | solution.py:357
  (254 shorter events, 105.8 us)
Async XLA Ops:
  8.0 42.0 %copy-start = (bf16[512,2048]{1,0:T(8,128)(2,1)S(1)}, bf16[512,2048]{1,0:T(8,128)(2,1)}, u32[]{:S(2)}) copy-start(bf16[512,2048]{1,0:T(8,128)(2,1)} %param.23) | copy-start | bytes 6291460
  8.0 76.2 %reduce-scatter.6.cloned.1.call-start = ((), (), s32[]{:S(2)}) async-start(), calls=%async_computation.5 | async-start | bytes 2621440 | tf_op jit(solution)/shard_map/reduce_scatter | solution.py:169
  8.9 23.4 %copy-start.53 = (f32[512]{0:T(512)}, f32[512]{0:T(512)S(1)}, u32[]{:S(2)}) copy-start(f32[512]{0:T(512)S(1)} %convert_element_type.156) | copy-start | bytes 6148
  10.2 22.2 %copy-start.55 = (f32[512]{0:T(512)}, f32[512]{0:T(512)S(1)}, u32[]{:S(2)}) copy-start(f32[512]{0:T(512)S(1)} %convert_element_type.158) | copy-start | bytes 6148
  13.9 32.1 %copy-start.15 = (pred[512,512]{0,1:T(8,128)(4,1)}, pred[512,512]{0,1:T(8,128)(4,1)S(1)}, u32[]{:S(2)}) copy-start(pred[512,512]{0,1:T(8,128)(4,1)S(1)} %fusion.43) | copy-start | bytes 786436
  52.6 125.3 %all-gather.6.cloned.1.call-start = ((), (), s32[]{:S(2)}) async-start(), calls=%async_computation.8 | async-start | bytes 17301504 | tf_op jit(solution)/shard_map/all_gather | solution.py:65
  53.2 240.0 %all-gather.4.cloned.1.call-start = ((), (), s32[]{:S(2)}) async-start(), calls=%async_computation.6 | async-start | bytes 17301504 | tf_op jit(solution)/shard_map/all_gather | solution.py:65
  53.5 34.9 %copy-start.72 = (s32[128,8]{0,1:T(8,128)S(1)}, s32[128,8]{0,1:T(8,128)}, u32[]{:S(2)}) copy-start(s32[128,8]{0,1:T(8,128)} %param.30) | copy-start | bytes 12292
  57.6 75.9 %copy-start.44 = (bf16[2048,32]{0,1:T(8,128)(2,1)S(1)}, bf16[2048,32]{0,1:T(8,128)(2,1)}, u32[]{:S(2)}) copy-start(bf16[2048,32]{0,1:T(8,128)(2,1)} %param.25) | copy-start | bytes 393220
  57.6 137.3 %copy-start.46 = (f32[2048]{0:T(1024)}, f32[2048]{0:T(1024)S(1)}, u32[]{:S(2)}) copy-start(f32[2048]{0:T(1024)S(1)} %convert_element_type.165) | copy-start | bytes 24580
  88.3 433.4 %reduce-scatter.12.cloned.1.call-start = ((), (), s32[]{:S(2)}) async-start(), calls=%async_computation.10 | async-start | bytes 540672 | tf_op jit(solution)/shard_map/reduce_scatter | solution.py:69
  134.9 60.1 %copy-start.63 = (f32[128]{0:T(128)}, f32[128]{0:T(128)S(1)}, u32[]{:S(2)}) copy-start(f32[128]{0:T(128)S(1)} %get-tuple-element.135) | copy-start | bytes 1540
  135.5 59.5 %copy-start.65 = (f32[128]{0:T(128)}, f32[128]{0:T(128)S(1)}, u32[]{:S(2)}) copy-start(f32[128]{0:T(128)S(1)} %fusion.59) | copy-start | bytes 1540
  387.7 315.4 %reduce-scatter.10.cloned.1.call-start = ((), (), s32[]{:S(2)}) async-start(), calls=%async_computation.9 | async-start | bytes 17301504 | tf_op jit(solution)/shard_map/reduce_scatter | solution.py:69
  453.6 68.1 %copy-start.37 = (f32[128,32]{0,1:T(8,128)S(1)}, f32[128,32]{0,1:T(8,128)}, u32[]{:S(2)}) copy-start(f32[128,32]{0,1:T(8,128)} %copy-done.36) | copy-start | bytes 49156
  453.6 68.1 %copy-start.64 = (f32[128]{0:T(128)S(1)}, f32[128]{0:T(128)}, u32[]{:S(2)}) copy-start(f32[128]{0:T(128)} %copy-done.63) | copy-start | bytes 1540
  453.6 68.1 %copy-start.66 = (f32[128]{0:T(128)S(1)}, f32[128]{0:T(128)}, u32[]{:S(2)}) copy-start(f32[128]{0:T(128)} %copy-done.65) | copy-start | bytes 1540
  453.6 249.4 %copy-start.6 = (f32[128,2048]{1,0:T(8,128)S(1)}, f32[128,2048]{1,0:T(8,128)}, u32[]{:S(2)}) copy-start(f32[128,2048]{1,0:T(8,128)} %copy-done.5) | copy-start | bytes 3145732
  453.6 249.4 %copy-start.45 = (bf16[2048,32]{0,1:T(8,128)(2,1)S(1)}, bf16[2048,32]{0,1:T(8,128)(2,1)}, u32[]{:S(2)}) copy-start(bf16[2048,32]{0,1:T(8,128)(2,1)} %param.25) | copy-start | bytes 393220
  453.6 249.4 %copy-start.47 = (f32[2048]{0:T(1024)S(1)}, f32[2048]{0:T(1024)}, u32[]{:S(2)}) copy-start(f32[2048]{0:T(1024)} %copy-done.46) | copy-start | bytes 24580
  453.6 249.4 %copy-start.70 = (f32[128]{0:T(128)S(1)}, f32[128]{0:T(128)}, u32[]{:S(2)}) copy-start(f32[128]{0:T(128)} %copy-done.69) | copy-start | bytes 1540
  453.6 251.4 %copy-start.77 = (f32[128]{0:T(128)S(1)}, f32[128]{0:T(128)}, u32[]{:S(2)}) copy-start(f32[128]{0:T(128)} %copy-done.76) | copy-start | bytes 1540
  453.7 254.6 %copy-start.50 = (f32[4,512]{1,0:T(4,128)S(1)}, f32[4,512]{1,0:T(4,128)}, u32[]{:S(2)}) copy-start(f32[4,512]{1,0:T(4,128)} %copy-done.49) | copy-start | bytes 24580
  453.7 254.6 %copy-start.62 = (f32[4,512]{1,0:T(4,128)S(1)}, f32[4,512]{1,0:T(4,128)}, u32[]{:S(2)}) copy-start(f32[4,512]{1,0:T(4,128)} %copy-done.61) | copy-start | bytes 24580
  453.7 278.7 %all-gather.8.cloned.1.call-start = ((), (), s32[]{:S(2)}) async-start(), calls=%async_computation.11 | async-start | bytes 2621440 | tf_op jit(solution)/shard_map/all_gather | solution.py:274
  708.3 27.2 %copy-start.16 = (pred[512,512]{0,1:T(8,128)(4,1)S(1)}, pred[512,512]{0,1:T(8,128)(4,1)}, u32[]{:S(2)}) copy-start(pred[512,512]{0,1:T(8,128)(4,1)} %copy-done.15) | copy-start | bytes 786436
  708.3 181.6 %reduce-scatter.14.cloned.1.call-start = ((), (), s32[]{:S(2)}) async-start(), calls=%async_computation.12 | async-start | bytes 2621440 | tf_op jit(solution)/shard_map/reduce_scatter | solution.py:328
  770.1 217.7 %reduce-scatter.8.cloned.1.call-start = ((), (), s32[]{:S(2)}) async-start(), calls=%async_computation.7 | async-start | bytes 17301504 | tf_op jit(solution)/shard_map/reduce_scatter | solution.py:69
  802.2 463.2 %all-reduce.14.cloned.1.call-start = ((), (), s32[]{:S(2)}) async-start(), calls=%async_computation.14 | async-start | bytes 16777216 | tf_op jit(solution)/shard_map/psum | solution.py:338
  813.7 583.3 %all-reduce.12.cloned.1.call-start = ((), (), s32[]{:S(2)}) async-start(), calls=%async_computation.13 | async-start | bytes 524288 | tf_op jit(solution)/shard_map/psum | solution.py:357
  832.2 17.0 %copy-start.24 = (bf16[4,1536,256]{1,2,0:T(8,128)(2,1)S(1)}, bf16[4,1536,256]{1,2,0:T(8,128)(2,1)}, u32[]{:S(2)}) copy-start(bf16[4,1536,256]{1,2,0:T(8,128)(2,1)} %get-tuple-element.100) | copy-start | bytes 9437188
  849.2 16.6 %copy-start.48 = (f32[32,128]{1,0:T(8,128)S(1)}, f32[32,128]{1,0:T(8,128)}, u32[]{:S(2)}) copy-start(f32[32,128]{1,0:T(8,128)} %reduce-scatter.12.cloned.1.call-done) | copy-start | bytes 49156
  (57 other events, 201.9 us)
Sparse Core Ops, SparseCore 0:
  52.7 31.4 reduce-scatter.5
  708.4 23.9 all-gather.7
  770.2 32.2 reduce-scatter.13
  804.6 183.1 reduce-scatter.7
  992.8 272.5 all-reduce.13
  1271.3 125.6 all-reduce.11
Sparse Core Ops, SparseCore 1:
  56.0 120.8 all-gather.5
  180.1 113.0 all-gather.3
  387.7 133.9 reduce-scatter.11
  524.0 179.0 reduce-scatter.9

commit v2 on v1

--- a/solution.py
+++ b/solution.py
@@ -1,6 +1,10 @@
+import functools
+
 import jax
 import jax.numpy as jnp
 from jax import lax
+from jax.experimental import pallas as pl
+from jax.experimental.pallas import tpu as pltpu
 from jax.sharding import PartitionSpec as P
 
 HEAD_DIM = 128
@@ -61,12 +65,583 @@
 BOTH = ("wide", "narrow")
 
 
-def gather_all(block):
-    return lax.all_gather(block, BOTH, axis=0, tiled=True)
-
-
-def scatter_all(parts):
-    return lax.psum_scatter(parts, BOTH, scatter_dimension=0, tiled=True)
+MESH = pl.DeviceIdType.MESH
+LINE = 4
+ADD_ROWS = 16
+
+
+def flip(bit, on):
+    return bit + on * (1 - 2 * bit)
+
+
+class Place:
+    def __init__(self):
+        wide, narrow = lax.axis_index("wide"), lax.axis_index("narrow")
+        self.z, self.x = wide // 2, lax.rem(wide, 2)
+        self.y, self.core = narrow // 2, lax.rem(narrow, 2)
+
+    def device(self, z, first, second, other_core=0):
+        core = flip(self.core, other_core)
+        x = flip(self.x, first * (1 - core) + second * core)
+        y = flip(self.y, first * core + second * (1 - core))
+        return (z * 2 + x, y * 2 + core)
+
+    def block(self, z, first, second, other_core=0):
+        wide, narrow = self.device(z, first, second, other_core)
+        return wide * 4 + narrow
+
+
+def greet(devices_and_conditions):
+    barrier = pltpu.get_barrier_semaphore()
+    total = 0
+    for device, condition in devices_and_conditions:
+        if condition is None:
+            pl.semaphore_signal(barrier, inc=1, device_id=device, device_id_type=MESH)
+            total = total + 1
+        else:
+            @pl.when(condition)
+            def _():
+                pl.semaphore_signal(barrier, inc=1, device_id=device, device_id_type=MESH)
+            total = total + condition.astype(jnp.int32)
+    pl.semaphore_wait(barrier, total)
+
+
+def add_into(target, *sources):
+    rows = target.shape[0]
+    step = min(rows, ADD_ROWS)
+
+    @pl.loop(0, rows // step)
+    def _(i):
+        part = pl.ds(pl.multiple_of(i * step, step), step)
+        total = target[part].astype(jnp.float32)
+        for source in sources:
+            total = total + source[part].astype(jnp.float32)
+        target[part] = total.astype(target.dtype)
+
+
+def remote(source, target, send, recv, device):
+    return pltpu.make_async_remote_copy(
+        src_ref=source, dst_ref=target, send_sem=send, recv_sem=recv,
+        device_id=device, device_id_type=MESH,
+    )
+
+
+PARTS = 2
+
+
+def part_of(ref, part):
+    rows = ref.shape[0] // PARTS
+    return ref.at[pl.ds(part * rows, rows)]
+
+
+def gather_kernel(count, *refs):
+    ins, outs, held = refs[:count], refs[count:2 * count], refs[2 * count:3 * count]
+    send, recv, own_in, own_out = refs[3 * count:]
+    at = Place()
+    z = at.z
+    up, down = at.device(z + 1, 0, 0), at.device(z - 1, 0, 0)
+    one, two, twin = at.device(z, 1, 0), at.device(z, 0, 1), at.device(z, 0, 0, 1)
+    greet([(one, None), (two, None), (twin, None), (up, z < LINE - 1), (down, z > 0)])
+    mine = at.block(z, 0, 0)
+    routes = {"up": (0, up), "down": (1, down), "one": (2, one), "two": (3, two), "twin": (4, twin)}
+
+    def copies(block, part, route, own=False):
+        lane, device = routes[route]
+        return [
+            remote(part_of(ins[i] if own else outs[i].at[block], part), part_of(outs[i].at[block], part),
+                   send.at[i, part, lane, block], recv.at[i, part, block], device)
+            for i in range(count)
+        ]
+
+    def forward(block, part, *ways, own=False):
+        for route in ways:
+            for copy in copies(block, part, route, own):
+                copy.start()
+
+    def arrived(block, part):
+        for copy in copies(block, part, "twin"):
+            copy.wait_recv()
+
+    loads = [pltpu.make_async_copy(ins[i], held[i], own_in.at[i]) for i in range(count)]
+    for load in loads:
+        load.start()
+    for part in range(PARTS):
+        pl.when(z < LINE - 1)(functools.partial(forward, mine, part, "up", own=True))
+        pl.when(z > 0)(functools.partial(forward, mine, part, "down", own=True))
+        forward(mine, part, "one", "two", "twin", own=True)
+    stores = [pltpu.make_async_copy(held[i], outs[i].at[mine], own_out.at[i]) for i in range(count)]
+    for load, store in zip(loads, stores):
+        load.wait()
+        store.start()
+
+    def line_step(step, part):
+        @pl.when(z - step >= 0)
+        def _():
+            block = at.block(z - step, 0, 0)
+            arrived(block, part)
+            pl.when(z < LINE - 1)(functools.partial(forward, block, part, "up"))
+            forward(block, part, "one", "two", "twin")
+
+        @pl.when(z + step < LINE)
+        def _():
+            block = at.block(z + step, 0, 0)
+            arrived(block, part)
+            pl.when(z > 0)(functools.partial(forward, block, part, "down"))
+            forward(block, part, "one", "two", "twin")
+
+    def face_step(step, part, first, second):
+        def take(block):
+            arrived(block, part)
+            if not second:
+                forward(block, part, "two")
+            forward(block, part, "twin")
+        if step == 0:
+            take(at.block(z, first, second))
+        else:
+            @pl.when(z - step >= 0)
+            def _():
+                take(at.block(z - step, first, second))
+
+            @pl.when(z + step < LINE)
+            def _():
+                take(at.block(z + step, first, second))
+
+    for step in range(LINE + 2):
+        for part in range(PARTS):
+            if 1 <= step < LINE:
+                line_step(step, part)
+            if 0 <= step - 1 < LINE:
+                face_step(step - 1, part, 1, 0)
+                face_step(step - 1, part, 0, 1)
+            if 0 <= step - 2 < LINE:
+                face_step(step - 2, part, 1, 1)
+    for first in (0, 1):
+        for second in (0, 1):
+            for line in range(LINE):
+                for part in range(PARTS):
+                    arrived(at.block(line, first, second, 1), part)
+    for store in stores:
+        store.wait()
+
+    def sent(block, part, *ways):
+        for route in ways:
+            for copy in copies(block, part, route):
+                copy.wait_send()
+
+    for line in range(LINE):
+        for part in range(PARTS):
+            block = at.block(line, 0, 0)
+            pl.when((z >= line) & (z < LINE - 1))(functools.partial(sent, block, part, "up"))
+            pl.when((z <= line) & (z > 0))(functools.partial(sent, block, part, "down"))
+            sent(block, part, "one", "two", "twin")
+            sent(at.block(line, 1, 0), part, "two", "twin")
+            sent(at.block(line, 0, 1), part, "twin")
+            sent(at.block(line, 1, 1), part, "twin")
+
+
+def gather_blocks(collective_id, *arrays):
+    count, devices = len(arrays), lax.axis_size("wide") * lax.axis_size("narrow")
+    moved = sum(a.size * a.dtype.itemsize for a in arrays)
+    return pl.pallas_call(
+        functools.partial(gather_kernel, count),
+        name=f"gather_blocks_{collective_id}",
+        out_shape=tuple(jax.ShapeDtypeStruct((devices,) + a.shape, a.dtype) for a in arrays),
+        in_specs=[pl.BlockSpec(memory_space=pl.ANY)] * count,
+        out_specs=tuple(pl.BlockSpec(memory_space=pl.ANY) for _ in arrays),
+        scratch_shapes=[pltpu.VMEM(a.shape, a.dtype) for a in arrays]
+        + [
+            pltpu.SemaphoreType.DMA((count, PARTS, 5, devices)),
+            pltpu.SemaphoreType.DMA((count, PARTS, devices)),
+            pltpu.SemaphoreType.DMA((count,)),
+            pltpu.SemaphoreType.DMA((count,)),
+        ],
+        compiler_params=pltpu.CompilerParams(collective_id=collective_id, has_side_effects=True),
+        cost_estimate=pl.CostEstimate(flops=0, transcendentals=0, bytes_accessed=2 * devices * moved),
+    )(*arrays)
+
+
+ORDER = (3, 0, 2, 1)
+
+
+def scatter_kernel(count, *refs):
+    ins, outs = refs[:count], refs[count:2 * count]
+    rest = [refs[2 * count + k * count:2 * count + (k + 1) * count] for k in range(6)]
+    acc, from_twin, from_two, from_one, from_below, from_above = rest
+    load_sem, store_sem, send, recv = refs[8 * count:]
+    at = Place()
+    z = at.z
+    up, down = at.device(z + 1, 0, 0), at.device(z - 1, 0, 0)
+    one, two, twin = at.device(z, 1, 0), at.device(z, 0, 1), at.device(z, 0, 0, 1)
+    greet([(one, None), (two, None), (twin, None), (up, z < LINE - 1), (down, z > 0)])
+    units = [(line, part) for line in ORDER for part in range(PARTS)]
+    corners = [(1, 1), (1, 0), (0, 1), (0, 0)]
+
+    def slot(line, second, first):
+        return second * 8 + first * 4 + line
+
+    def load(i, part, line, second, first):
+        here = slot(line, second, first)
+        return pltpu.make_async_copy(part_of(ins[i].at[at.block(line, first, second)], part),
+                                     part_of(acc[i].at[here], part), load_sem.at[i, part, here])
+
+    def hop(i, part, source, target, lane, device):
+        return remote(part_of(source, part), part_of(target, part), send.at[i, part, lane], recv.at[i, part, lane], device)
+
+    def to_twin(i, part, line, second, first):
+        here = slot(line, second, first)
+        return hop(i, part, ins[i].at[at.block(line, first, second, 1)], from_twin[i].at[here], here, twin)
+
+    def to_two(i, part, line, first):
+        return hop(i, part, acc[i].at[slot(line, 1, first)], from_two[i].at[first * 4 + line], 16 + first * 4 + line, two)
+
+    def to_one(i, part, line):
+        return hop(i, part, acc[i].at[slot(line, 0, 1)], from_one[i].at[line], 24 + line, one)
+
+    def rise(i, part, line):
+        return hop(i, part, acc[i].at[line], from_below[i].at[line], 28 + line, up)
+
+    def fall(i, part, line):
+        return hop(i, part, acc[i].at[line], from_above[i].at[line], 32 + line, down)
+
+    def begin(line, part):
+        for second, first in corners:
+            for i in range(count):
+                to_twin(i, part, line, second, first).start()
+                load(i, part, line, second, first).start()
+
+    def gathered(line, part, second, first):
+        for i in range(count):
+            load(i, part, line, second, first).wait()
+            to_twin(i, part, line, second, first).wait_recv()
+            sources = [from_twin[i].at[slot(line, second, first)]]
+            if not second:
+                to_two(i, part, line, first).wait_recv()
+                sources.append(from_two[i].at[first * 4 + line])
+                if not first:
+                    to_one(i, part, line).wait_recv()
+                    sources.append(from_one[i].at[line])
+            add_into(part_of(acc[i].at[slot(line, second, first)], part), *[part_of(r, part) for r in sources])
+            if second:
+                to_two(i, part, line, first).start()
+            elif first:
+                to_one(i, part, line).start()
+
+    def line_hop(line, part, hops):
+        @pl.when(z == hops)
+        def _():
+            for i in range(count):
+                if 0 < hops <= line:
+                    rise(i, part, line).wait_recv()
+                    add_into(part_of(acc[i].at[line], part), part_of(from_below[i].at[line], part))
+                if hops < line:
+                    rise(i, part, line).start()
+
+        @pl.when(z == LINE - 1 - hops)
+        def _():
+            for i in range(count):
+                if 0 < hops <= LINE - 1 - line:
+                    fall(i, part, line).wait_recv()
+                    add_into(part_of(acc[i].at[line], part), part_of(from_above[i].at[line], part))
+                if hops < LINE - 1 - line:
+                    fall(i, part, line).start()
+
+    begin(*units[0])
+    begin(*units[1])
+    for step in range(len(units) + 2 + LINE):
+        if step + 2 < len(units):
+            begin(*units[step + 2])
+        if step < len(units):
+            gathered(*units[step], 1, 1)
+            gathered(*units[step], 1, 0)
+        if 0 <= step - 1 < len(units):
+            gathered(*units[step - 1], 0, 1)
+        if 0 <= step - 2 < len(units):
+            gathered(*units[step - 2], 0, 0)
+        for hops in range(LINE):
+            if 0 <= step - 2 - hops < len(units):
+                line_hop(*units[step - 2 - hops], hops)
+    stores = [pltpu.make_async_copy(acc[i].at[z], outs[i], store_sem.at[i]) for i in range(count)]
+    for store in stores:
+        store.start()
+    for line, part in units:
+        for i in range(count):
+            for second, first in corners:
+                to_twin(i, part, line, second, first).wait_send()
+            to_two(i, part, line, 0).wait_send()
+            to_two(i, part, line, 1).wait_send()
+            to_one(i, part, line).wait_send()
+            if line > 0:
+                pl.when(z < line)(rise(i, part, line).wait_send)
+            if line < LINE - 1:
+                pl.when(z > line)(fall(i, part, line).wait_send)
+    for store in stores:
+        store.wait()
+
+
+def scatter_blocks(collective_id, *arrays):
+    count = len(arrays)
+
+    def slots(n):
+        return [pltpu.VMEM((n,) + a.shape[1:], a.dtype) for a in arrays]
+    return pl.pallas_call(
+        functools.partial(scatter_kernel, count),
+        name=f"scatter_blocks_{collective_id}",
+        out_shape=tuple(jax.ShapeDtypeStruct(a.shape[1:], a.dtype) for a in arrays),
+        in_specs=[pl.BlockSpec(memory_space=pl.ANY)] * count,
+        out_specs=tuple(pl.BlockSpec(memory_space=pl.ANY) for _ in arrays),
+        scratch_shapes=slots(16) + slots(16) + slots(8) + slots(4) + slots(4) + slots(4)
+        + [
+            pltpu.SemaphoreType.DMA((count, PARTS, 16)),
+            pltpu.SemaphoreType.DMA((count,)),
+            pltpu.SemaphoreType.DMA((count, PARTS, 36)),
+            pltpu.SemaphoreType.DMA((count, PARTS, 36)),
+        ],
+        compiler_params=pltpu.CompilerParams(
+            collective_id=collective_id, has_side_effects=True, vmem_limit_bytes=60 << 20),
+        cost_estimate=pl.CostEstimate(
+            flops=0, transcendentals=0, bytes_accessed=sum(a.size * a.dtype.itemsize for a in arrays)),
+    )(*arrays)
+
+
+def sum_task(at, kind, rows, source, result, held, from_pair, from_below, from_above, load_sem, send, recv, delay):
+    z, x = at.z, at.x
+    pair = ((z * 2 + 1 - x), at.y * 2 + at.core)
+    up, down = ((z + 1) * 2 + x, at.y * 2 + at.core), ((z - 1) * 2 + x, at.y * 2 + at.core)
+    pair_first = kind == "pair"
+    for _ in range(delay):
+        yield
+
+    def part(ref, line, face):
+        return ref.at[line, face, rows]
+
+    if pair_first:
+        def load(line):
+            return pltpu.make_async_copy(part(source, line, x), held.at[line], load_sem.at[line])
+
+        def give(line):
+            return remote(part(source, line, 1 - x), from_pair.at[line], send.at[0, line], recv.at[0, line], pair)
+        for line in ORDER:
+            give(line).start()
+            load(line).start()
+        yield
+        yield
+        for line in ORDER:
+            load(line).wait()
+            give(line).wait_recv()
+            add_into(held.at[line], from_pair.at[line])
+    else:
+        def load(line):
+            return pltpu.make_async_copy(source.at[line, :, rows], held.at[line], load_sem.at[line])
+        for line in ORDER:
+            load(line).start()
+        for line in ORDER:
+            load(line).wait()
+
+    def add(target, extra):
+        if pair_first:
+            add_into(target, extra)
+        else:
+            for face in (0, 1):
+                add_into(target.at[face], extra.at[face])
+
+    def rise(line):
+        return remote(held.at[line], from_below.at[line], send.at[1, line], recv.at[1, line], up)
+
+    def fall(line):
+        return remote(held.at[line], from_above.at[line], send.at[2, line], recv.at[2, line], down)
+
+    for line in range(LINE - 1, 0, -1):
+        other = LINE - 1 - line
+
+        @pl.when(z < line)
+        def _():
+            @pl.when(z > 0)
+            def _():
+                rise(line).wait_recv()
+                add(held.at[line], from_below.at[line])
+            rise(line).start()
+
+        @pl.when(z > other)
+        def _():
+            @pl.when(z < LINE - 1)
+            def _():
+                fall(other).wait_recv()
+                add(held.at[other], from_above.at[other])
+            fall(other).start()
+        yield
+
+    @pl.when(z > 0)
+    def _():
+        rise(z).wait_recv()
+        add(held.at[z], from_below.at[z])
+
+    @pl.when(z < LINE - 1)
+    def _():
+        fall(z).wait_recv()
+        add(held.at[z], from_above.at[z])
+
+    if pair_first:
+        def over(line):
+            return remote(part(result, line, x), part(result, line, x), send.at[3, line], recv.at[3, line * 2 + x], pair)
+
+        def other_over(line):
+            return remote(part(result, line, 1 - x), part(result, line, 1 - x), send.at[3, line],
+                          recv.at[3, line * 2 + 1 - x], pair)
+
+        def climb(line):
+            return remote(part(result, line, x), part(result, line, x), send.at[4, line], recv.at[3, line * 2 + x], up)
+
+        def sink(line):
+            return remote(part(result, line, x), part(result, line, x), send.at[5, line], recv.at[3, line * 2 + x], down)
+        own = pltpu.make_async_copy(held.at[z], part(result, z, x), load_sem.at[4])
+    else:
+        mine = held.at[z]
+        swap = remote(mine.at[1 - x], from_pair, send.at[0, 0], recv.at[0, 0], pair)
+        swap.start()
+        yield
+        swap.wait_recv()
+        add_into(mine.at[x], from_pair)
+        own = pltpu.make_async_copy(mine.at[x], part(result, z, x), load_sem.at[4])
+
+        def over_block(face):
+            return remote(part(result, z, face), part(result, z, face), send.at[3, 0], recv.at[3, face], pair)
+
+        def climb(line):
+            return remote(result.at[line, :, rows], result.at[line, :, rows], send.at[4, line], recv.at[3, 4 + line], up)
+
+        def sink(line):
+            return remote(result.at[line, :, rows], result.at[line, :, rows], send.at[5, line], recv.at[3, 4 + line], down)
+    own.start()
+    own.wait()
+    if pair_first:
+        over(z).start()
+    else:
+        over_block(x).start()
+        yield
+        over_block(1 - x).wait_recv()
+
+    @pl.when(z < LINE - 1)
+    def _():
+        climb(z).start()
+
+    @pl.when(z > 0)
+    def _():
+        sink(z).start()
+    yield
+    for step in range(1, LINE):
+        @pl.when(z - step >= 0)
+        def _():
+            climb(z - step).wait_recv()
+
+            @pl.when(z < LINE - 1)
+            def _():
+                climb(z - step).start()
+            if pair_first:
+                over(z - step).start()
+
+        @pl.when(z + step < LINE)
+        def _():
+            sink(z + step).wait_recv()
+
+            @pl.when(z > 0)
+            def _():
+                sink(z + step).start()
+            if pair_first:
+                over(z + step).start()
+        yield
+    if pair_first:
+        for line in range(LINE):
+            other_over(line).wait_recv()
+    for line in range(LINE):
+        if pair_first:
+            give(line).wait_send()
+            over(line).wait_send()
+        if line > 0:
+            pl.when(z < line)(rise(line).wait_send)
+        if line < LINE - 1:
+            pl.when(z > line)(fall(line).wait_send)
+        pl.when((z >= line) & (z < LINE - 1))(climb(line).wait_send)
+        pl.when((z <= line) & (z > 0))(sink(line).wait_send)
+    if not pair_first:
+        swap.wait_send()
+        over_block(x).wait_send()
+
+
+CHUNK = 64
+
+
+def sum_wide_kernel(plan, count, *refs):
+    ins, outs, rest = refs[:count], refs[count:2 * count], list(refs[2 * count:])
+    at = Place()
+    pair = (at.z * 2 + 1 - at.x, at.y * 2 + at.core)
+    up, down = ((at.z + 1) * 2 + at.x, at.y * 2 + at.core), ((at.z - 1) * 2 + at.x, at.y * 2 + at.core)
+    greet([(pair, None), (up, at.z < LINE - 1), (down, at.z > 0)])
+    load_sem, send, recv = rest[-3:]
+    tasks = []
+    for number, (which, begin, kind, delay) in enumerate(plan):
+        held, from_pair, from_below, from_above = rest[4 * number:4 * number + 4]
+        tasks.append(sum_task(at, kind, pl.ds(begin, CHUNK), ins[which], outs[which], held, from_pair, from_below,
+                              from_above, load_sem.at[number], send.at[number], recv.at[number], delay))
+    while tasks:
+        tasks = [task for task in tasks if next(task, tasks) is not tasks]
+
+
+def sum_wide(collective_id, plan, *arrays):
+    count, steps = len(arrays), len(plan)
+    scratch = []
+    for which, _, kind, _ in plan:
+        columns, dtype = arrays[which].shape[3], arrays[which].dtype
+        lead = () if kind == "pair" else (2,)
+        block = lead + (CHUNK, columns)
+        scratch += [
+            pltpu.VMEM((LINE,) + block, dtype),
+            pltpu.VMEM(((LINE,) if kind == "pair" else ()) + (CHUNK, columns), dtype),
+            pltpu.VMEM((LINE,) + block, dtype),
+            pltpu.VMEM((LINE,) + block, dtype),
+        ]
+    moved = sum(a.size * a.dtype.itemsize for a in arrays)
+    return pl.pallas_call(
+        functools.partial(sum_wide_kernel, plan, count),
+        name=f"sum_wide_{collective_id}",
+        out_shape=tuple(jax.ShapeDtypeStruct(a.shape, a.dtype) for a in arrays),
+        in_specs=[pl.BlockSpec(memory_space=pl.ANY)] * count,
+        out_specs=tuple(pl.BlockSpec(memory_space=pl.ANY) for _ in arrays),
+        scratch_shapes=scratch + [
+            pltpu.SemaphoreType.DMA((steps, 5)),
+            pltpu.SemaphoreType.DMA((steps, 6, 4)),
+            pltpu.SemaphoreType.DMA((steps, 4, 8)),
+        ],
+        compiler_params=pltpu.CompilerParams(
+            collective_id=collective_id, has_side_effects=True, vmem_limit_bytes=48 << 20),
+        cost_estimate=pl.CostEstimate(flops=0, transcendentals=0, bytes_accessed=2 * moved),
+    )(*arrays)
+
+
+def own_exchange():
+    return lax.axis_size("wide") == 8 and lax.axis_size("narrow") == 4
+
+
+def gather_all(*arrays):
+    if own_exchange():
+        return gather_blocks(1, *arrays)
+    return tuple(lax.all_gather(a, BOTH, axis=0) for a in arrays)
+
+
+def scatter_all(*arrays):
+    if own_exchange():
+        return scatter_blocks(2, *arrays)
+    return tuple(lax.psum_scatter(a, BOTH, scatter_dimension=0) for a in arrays)
+
+
+SUM_PLAN = ((0, 0, "pair", 0), (1, 0, "line", 0), (0, 64, "pair", 1), (0, 128, "pair", 2), (0, 192, "pair", 3))
+
+
+def total_wide(joined, out_part):
+    if own_exchange():
+        shapes = joined.shape, out_part.shape
+        dealt = [a.reshape(LINE, 2, a.shape[0] // 8, a.shape[1]) for a in (joined, out_part)]
+        return tuple(a.reshape(shape) for a, shape in zip(sum_wide(3, SUM_PLAN, *dealt), shapes))
+    return lax.psum((joined, out_part), "wide")
 
 
 def local(
@@ -108,8 +683,7 @@
         chosen.astype(jnp.bfloat16),
         preferred_element_type=jnp.float32,
     )
-    places_all = gather_all(jnp.where(chosen, earlier, -1.0).T)
-    grads_all = gather_all(out_cotangent)
+    grads_all = lax.all_gather(out_cotangent, BOTH, axis=0)
     inputs_all = block_input.astype(jnp.float32)
     normed_one = rms_scale(inputs_all, attn_gain.astype(jnp.float32)).astype(jnp.bfloat16)
     joined_weight = jnp.concatenate([query_weight, key_weight, value_weight], axis=1)
@@ -178,15 +752,12 @@
     normed_two = normed_two_full.astype(jnp.bfloat16)
     logits = jnp.dot(normed_two, router_weight, preferred_element_type=jnp.float32)
     route_probs = jax.nn.softmax(logits, axis=-1)
-    rows_all = gather_all(normed_two)
-    probs_all = gather_all(route_probs.T)
+    rows_all, routes_all = gather_all(
+        normed_two, jnp.concatenate([route_probs.T, jnp.where(chosen, earlier, -1.0).T], axis=0)
+    )
     expert_begin = lax.axis_index("wide") * experts_here
-    places_here = lax.dynamic_slice_in_dim(
-        places_all.reshape(block_count, experts_all, own_rows), expert_begin, experts_here, 1
-    )
-    probs_here = lax.dynamic_slice_in_dim(
-        probs_all.reshape(block_count, experts_all, own_rows), expert_begin, experts_here, 1
-    )
+    probs_here = lax.dynamic_slice_in_dim(routes_all, expert_begin, experts_here, 1)
+    places_here = lax.dynamic_slice_in_dim(routes_all, experts_all + expert_begin, experts_here, 1)
     pick = places_here[:, :, None, :] == jnp.arange(capacity, dtype=jnp.float32)[None, None, :, None]
     pick_low = pick.astype(jnp.bfloat16)
     slot_gate = jnp.sum(jnp.where(pick, probs_here[:, :, None, :], 0.0), axis=-1)
@@ -196,7 +767,7 @@
         out = jnp.einsum(
             "best,btd->ebsd",
             pick_low,
-            rows.reshape(block_count, own_rows, model_width),
+            rows,
             preferred_element_type=jnp.float32,
         )
         return out.astype(jnp.bfloat16).reshape(experts_here, block_count * capacity, model_width)
@@ -208,7 +779,7 @@
             slots.reshape(experts_here, block_count, capacity, model_width),
             preferred_element_type=jnp.float32,
         )
-        return out.astype(jnp.bfloat16).reshape(block_count * own_rows, model_width)
+        return out.astype(jnp.bfloat16)
 
     slot_rows = spread(rows_all)
     slot_grads = spread(grads_all)
@@ -232,15 +803,16 @@
     gate_grad_wide = lax.dynamic_update_slice_in_dim(
         jnp.zeros((block_count, experts_all, own_rows), jnp.float32), gate_grad_parts, expert_begin, 1
     )
-    prob_grads = scatter_all(gate_grad_wide.reshape(block_count * experts_all, own_rows)).T
     back_slots = jnp.einsum(
         "erf,edf->erd", gate_grad_low, gate_weight, preferred_element_type=jnp.float32
     ) + jnp.einsum("erf,edf->erd", up_grad_low, up_weight, preferred_element_type=jnp.float32)
-    rows_back = scatter_all(collect(back_slots.astype(jnp.bfloat16))).astype(jnp.float32)
     out_slots = jnp.einsum(
         "erf,efd->erd", gated_act, down_weight, preferred_element_type=jnp.float32
     )
-    moe_out = scatter_all(collect(out_slots.astype(jnp.bfloat16))).astype(jnp.float32)
+    rows_back, prob_grads, moe_out = scatter_all(
+        collect(back_slots.astype(jnp.bfloat16)), gate_grad_wide, collect(out_slots.astype(jnp.bfloat16))
+    )
+    rows_back, prob_grads, moe_out = rows_back.astype(jnp.float32), prob_grads.T, moe_out.astype(jnp.float32)
     down_weight_grad = jnp.einsum(
         "erf,erd->efd", gated_act, slot_grads, preferred_element_type=jnp.float32
     )
@@ -334,26 +906,12 @@
     normed_again, norm_one_back = jax.vjp(rms_scale, input_own, attn_gain.astype(jnp.float32))
     input_path, attn_gain_part = norm_one_back(normed_one_grad)
     input_grad = (hidden_grad + input_path).astype(jnp.bfloat16)
-    summed = (
-        lax.psum(joined_grad[:, :local_width].astype(jnp.bfloat16), "wide").astype(jnp.float32),
-        lax.psum(joined_grad[:, local_width : 2 * local_width].astype(jnp.bfloat16), "wide").astype(
-            jnp.float32
-        ),
-        lax.psum(joined_grad[:, 2 * local_width :].astype(jnp.bfloat16), "wide").astype(
-            jnp.float32
-        ),
-        lax.psum(out_weight_acc.astype(jnp.bfloat16), "wide").astype(jnp.float32),
-        lax.psum(query_gain_part.astype(jnp.bfloat16), "wide").astype(jnp.float32),
-        lax.psum(key_gain_part.astype(jnp.bfloat16), "wide").astype(jnp.float32),
-    )
-    (
-        query_weight_grad,
-        key_weight_grad,
-        value_weight_grad,
-        out_weight_grad,
-        query_gain_grad,
-        key_gain_grad,
-    ) = summed
+    joined_total, out_total = total_wide(joined_grad.astype(jnp.bfloat16), out_weight_acc.astype(jnp.bfloat16))
+    joined_total, out_weight_grad = joined_total.astype(jnp.float32), out_total.astype(jnp.float32)
+    query_weight_grad = joined_total[:, :local_width]
+    key_weight_grad = joined_total[:, local_width : 2 * local_width]
+    value_weight_grad = joined_total[:, 2 * local_width :]
+    query_gain_grad, key_gain_grad = lax.psum((query_gain_part, key_gain_part), "wide")
     router_weight_grad, attn_gain_grad, moe_gain_grad = lax.psum(
         (router_part, attn_gain_part, moe_gain_part), ("wide", "narrow")
     )

time: 1420 us -> 1050 us (0.74)
  waiting for transfers between devices: 822 us -> 63.4 us
  Pallas kernels: 0 us -> 485 us
  blocking collectives: 167 us -> 70.9 us
    pallas_call x0 -> x3, Pallas kernels: none -> 485 us  [the longest x1 202 us: sum_wide(): pl.pallas_call(functools.partial(sum_wide_kernel, plan, count), name=f'su...]
    reduce_scatter x3 -> x0, waiting for transfers between devices: 345 us -> none  [scatter_all(): return lax.psum_scatter(parts, BOTH, scatter_dimension=0, tiled=True)]
    psum x1 -> x0, waiting for transfers between devices: 230 us -> none  [local(): lax.psum(joined_grad[:, :local_width].astype(jnp.bfloat16), 'wide')]
    psum x1, waiting for transfers between devices: 120 us -> 0.01 us  [local(): lax.psum((router_part, attn_gain_part, moe_gain_part), ('wide', 'narrow'))]
    all_gather x2 -> x0, blocking collectives: 86.2 us -> none  [gather_all(): return lax.all_gather(block, BOTH, axis=0, tiled=True)]
    all_gather x2 -> x1, waiting for transfers between devices: 77.1 us -> 0.01 us  [local(): grads_all = lax.all_gather(out_cotangent, BOTH, axis=0)]
  transfers between devices with their start and end apart: 10 -> 5, of which waited for: 8 -> 2; matrix products, arithmetic and copies ran while one was open for 16% -> 16% of each run, Pallas kernels for 0% -> 31%
where the time goes in v2:
time: 1050 us; the launch traced here: 1040 us
  Pallas kernels  485 us (46%)
  matrix products  279 us (27%)
  local copies, waits for them, and re-layouts  77.2 us (7%)
  blocking collectives  70.9 us (7%)
  waiting for transfers between devices  63.4 us (6%)
  other arithmetic  46.8 us (4%)
  between operations  16.5 us (2%)
    pallas_call x1, Pallas kernels, sum_wide(): pl.pallas_call(functools.partial(sum_wide_kernel, plan, count), name=f'su...  202 us
    pallas_call x1, Pallas kernels, scatter_blocks(): pl.pallas_call(functools.partial(scatter_kernel, count), name=f'scatter_b...  159 us
    pallas_call x1, Pallas kernels, gather_blocks(): pl.pallas_call(functools.partial(gather_kernel, count), name=f'gather_blo...  124 us
    convert_element_type x2, local copies, waits for them, and re-layouts, spread(): out.astype(jnp.bfloat16)  42.6 us
    psum x1, blocking collectives, local(): lax.psum((router_part, attn_gain_part, moe_gain_part), ('wide', 'narrow'))  36.9 us
    dot_general x2, matrix products, spread(): jnp.einsum('best,btd->ebsd', pick_low, rows, preferred_element_type=jnp.f...  36.5 us
    all_gather x1, waiting for transfers between devices, local(): lax.all_gather(hidden_grad_low, 'narrow', axis=0, tiled=True)  36.5 us
    dot_general x2, matrix products, collect(): jnp.einsum('best,ebsd->btd', pick_low, slots.reshape(experts_here, block_...  33.4 us
  transfers between devices with their start and end apart: 5, of which 2 were waited for; matrix products, arithmetic and copies ran while one was open for 16% of the time, Pallas kernels for 31%

profile of v2, /device:TPU:0, one launch (start us, length us, event | category | flops | bytes accessed | tf_op | source)
XLA Modules:
  0.0 1039.0 jit_solution(14500935094356021832)
XLA Ops:
  18.0 3.5 fusion.48
  23.3 8.4 all-reduce.7
  53.6 4.1 convert_element_type.141
  57.9 26.3 %reduce-scatter.3.cloned.1.call-done = bf16[128,2048]{1,0:T(8,128)(2,1)} async-done(((bf16[512,2048]{1,0:T(8,128)(2,1)}), bf16[128,2048]{1,0:T(8,128)(2,1)}) %reduce-scatter.3.cloned.1.call-update) | async-done | bytes 524304 | tf_op jit(solution)/shard_map/reduce_scatter | solution.py:743
  89.2 123.9 %gather_blocks_1.1 = (bf16[32,128,2048]{2,1,0:T(8,128)(2,1)}, f32[32,64,128]{2,1,0:T(8,128)}) custom-call(bf16[128,2048]{1,0:T(8,128)(2,1)} %copy-done.13, f32[64,128]{1,0:T(8,128)} %pad_maximum_fusion.6.refs_1_), custom_call_target="tpu_custom_call" | custom-call | bytes 35651584 | tf_op jit(solution)/shard_map/gather_blocks_1/pallas_call | solution.py:245
  215.2 19.3 %convert_bitcast_fusion = bf16[4,32,48,2048]{3,2,0,1:T(8,128)(2,1)} fusion(bf16[32,128,2048]{2,1,0:T(8,128)(2,1)} %get-tuple-element.79, f32[32,4,128]{2,1,0:T(4,128)S(1)} %get-tuple-element.130), kind=kOutput, calls=%fused_computation.8 | convolution fusion | flops 3234594816 | bytes 42008576 | tf_op jit(solution)/shard_map/best,btd->ebsd/dot_general | solution.py:767
  234.6 21.5 %copy.165 = bf16[4,32,48,2048]{3,2,1,0:T(8,128)(2,1)} copy(bf16[4,32,48,2048]{3,2,0,1:T(8,128)(2,1)} %convert_bitcast_fusion) | data formatting | bytes 50331648 | tf_op jit(solution)/shard_map/convert_element_type | solution.py:773
  256.0 14.1 %fusion.84 = f32[4,1536,256]{1,2,0:T(8,128)} fusion(bf16[4,1536,2048]{2,1,0:T(8,128)(2,1)} %bitcast.148, bf16[4,2048,256]{2,1,0:T(8,128)(2,1)S(1)} %copy-done.25), kind=kOutput, calls=%fused_computation.167 | convolution fusion | flops 6442450944 | bytes 35651584 | tf_op jit(solution)/shard_map/erd,edf->erf/dot_general | solution.py:786
  270.2 15.6 %fusion.83 = f32[4,1536,256]{1,2,0:T(8,128)} fusion(bf16[4,1536,2048]{2,1,0:T(8,128)(2,1)} %bitcast.149, bf16[4,2048,256]{2,1,0:T(8,128)(2,1)} %param.27), kind=kOutput, calls=%fused_computation.166 | convolution fusion | flops 6442450944 | bytes 35651584 | tf_op jit(solution)/shard_map/erd,edf->erf/dot_general | solution.py:787
  285.7 17.2 %convert_bitcast_fusion.1 = bf16[4,32,48,2048]{3,2,0,1:T(8,128)(2,1)} fusion(bf16[32,128,2048,1]{2,1,3,0:T(8,128)(2,1)} %bitcast.147, f32[32,4,128]{2,1,0:T(4,128)S(1)} %get-tuple-element.130), kind=kOutput, calls=%fused_computation.9 | convolution fusion | flops 3234594816 | bytes 42008576 | tf_op jit(solution)/shard_map/best,btd->ebsd/dot_general | solution.py:767
  302.9 21.1 %copy.163 = bf16[4,32,48,2048]{3,2,1,0:T(8,128)(2,1)} copy(bf16[4,32,48,2048]{3,2,0,1:T(8,128)(2,1)} %convert_bitcast_fusion.1) | data formatting | bytes 50331648 | tf_op jit(solution)/shard_map/convert_element_type | solution.py:773
  324.0 21.5 %multiply_reduce_fusion = (f32[4,1536]{1,0:T(4,128)S(1)}, bf16[4,1536,256]{1,2,0:T(8,128)(2,1)}, bf16[4,1536,256]{1,2,0:T(8,128)(2,1)}, bf16[4,1536,256]{1,2,0:T(8,128)(2,1)}) fusion(f32[4,1536,256]{1,2,0:T(8,128)} %fusion.83, f32[4,1536,256]{1,2,0:T(8,128)} %fusion.84, f32[4,1536]{1,0:T(4,128)S(1)} %mul.637, bf16[4,1536,2048]{2,1,0:T(8,128)(2,1)} %bitcast.152, ...), kind=kOutput, calls=%fused_computation.19 | convolution fusion | flops 6473902080 | bytes 51429376 | tf_op jit(solution)/shard_map/erd,efd->erf/dot_general | solution.py:790
  347.1 14.4 %convolution_convert_fusion = bf16[4,1536,2048]{2,1,0:T(8,128)(2,1)} fusion(bf16[4,1536,256]{1,2,0:T(8,128)(2,1)} %get-tuple-element.109, bf16[4,256,2048]{2,1,0:T(8,128)(2,1)} %param.28), kind=kOutput, calls=%fused_computation.3 | convolution fusion | flops 6455033856 | bytes 32505856 | tf_op jit(solution)/shard_map/erf,efd->erd/dot_general | solution.py:809
  361.5 16.8 %bitcast_convert_fusion.refs_2_ = bf16[32,128,2048]{2,1,0:T(8,128)(2,1)} fusion(bf16[4,32,48,2048]{3,2,1,0:T(8,128)(2,1)} %bitcast.146, f32[32,4,128]{2,1,0:T(4,128)S(1)} %get-tuple-element.130), kind=kOutput, calls=%fused_computation.1 | convolution fusion | flops 3230400512 | bytes 42008576 | tf_op jit(solution)/shard_map/best,ebsd->btd/dot_general | solution.py:776
  378.3 20.1 %fusion.85 = f32[4,1536,2048]{2,1,0:T(8,128)} fusion(bf16[4,1536,256]{1,2,0:T(8,128)(2,1)} %get-tuple-element.108, bf16[4,2048,256]{2,1,0:T(8,128)(2,1)S(1)} %copy-done.26), kind=kOutput, calls=%fused_computation.168 | convolution fusion | flops 6442450944 | bytes 57671680 | tf_op jit(solution)/shard_map/erf,edf->erd/dot_general | solution.py:806
  398.4 27.9 %add_convert_fusion = bf16[4,1536,2048]{2,1,0:T(8,128)(2,1)} fusion(f32[4,1536,2048]{2,1,0:T(8,128)} %fusion.85, bf16[4,1536,256]{1,2,0:T(8,128)(2,1)} %get-tuple-element.110, bf16[4,2048,256]{2,1,0:T(8,128)(2,1)} %param.27), kind=kOutput, calls=%fused_computation | convolution fusion | flops 6467616768 | bytes 82837504 | tf_op jit(solution)/shard_map/erf,edf->erd/dot_general | solution.py:808
  426.3 16.6 %bitcast_convert_fusion.1.refs_0_ = bf16[32,128,2048]{2,1,0:T(8,128)(2,1)} fusion(bf16[4,32,48,2048]{3,2,1,0:T(8,128)(2,1)} %bitcast.145, f32[32,4,128]{2,1,0:T(4,128)S(1)} %get-tuple-element.130), kind=kOutput, calls=%fused_computation.2 | convolution fusion | flops 3230400512 | bytes 42008576 | tf_op jit(solution)/shard_map/best,ebsd->btd/dot_general | solution.py:776
  444.5 158.8 %scatter_blocks_2.1 = (bf16[128,2048]{1,0:T(8,128)(2,1)}, f32[32,128]{1,0:T(8,128)}, bf16[128,2048]{1,0:T(8,128)(2,1)}) custom-call(bf16[32,128,2048]{2,1,0:T(8,128)(2,1)} %bitcast_convert_fusion.1.refs_0_, f32[32,32,128]{2,1,0:T(8,128)} %constant_dynamic-update-slice_fusion.3.refs_1_, bf16[32,128,2048]{2,1,0:T(8,128)(2,1)} %bitcast_convert_fusion.refs_2_), custom_call_target="tpu_custom_call" | custom-call | bytes 34078720 | tf_op jit(solution)/shard_map/scatter_blocks_2/pallas_call | solution.py:386
  608.5 36.5 %all-gather.4.cloned.1.call-done = bf16[512,2048]{1,0:T(8,128)(2,1)} async-done(((bf16[128,2048]{1,0:T(8,128)(2,1)}), bf16[512,2048]{1,0:T(8,128)(2,1)}) %all-gather.4.cloned.1.call-update) | async-done | bytes 2097168 | tf_op jit(solution)/shard_map/all_gather | solution.py:846
  664.8 6.0 all-reduce.6
  670.9 3.5 subtract_convert_fusion.1
  675.3 7.4 convolution_convert_fusion.3
  682.9 18.3 %fusion.88 = f32[4,256,2048]{2,1,0:T(8,128)} fusion(bf16[4,1536,256]{1,2,0:T(8,128)(2,1)} %get-tuple-element.109, bf16[4,1536,2048]{2,1,0:T(8,128)(2,1)} %bitcast.153), kind=kOutput, calls=%fused_computation.171 | convolution fusion | flops 6442450944 | bytes 36700160 | tf_op jit(solution)/shard_map/erf,erd->efd/dot_general | solution.py:816
  702.3 17.0 %fusion.86 = f32[4,2048,256]{2,1,0:T(8,128)} fusion(bf16[4,1536,2048]{2,1,0:T(8,128)(2,1)} %bitcast.150, bf16[4,1536,256]{1,2,0:T(8,128)(2,1)} %get-tuple-element.108), kind=kOutput, calls=%fused_computation.169 | convolution fusion | flops 6442450944 | bytes 36700160 | tf_op jit(solution)/shard_map/erd,erf->edf/dot_general | solution.py:819
  719.2 16.6 %fusion.87 = f32[4,2048,256]{2,1,0:T(8,128)} fusion(bf16[4,1536,2048]{2,1,0:T(8,128)(2,1)} %bitcast.151, bf16[4,1536,256]{1,2,0:T(8,128)(2,1)S(1)} %copy-done.27), kind=kOutput, calls=%fused_computation.170 | convolution fusion | flops 6442450944 | bytes 36700160 | tf_op jit(solution)/shard_map/erd,erf->edf/dot_general | solution.py:822
  735.9 8.4 convolution_convert_fusion.1
  745.5 201.9 %sum_wide_3.1 = (bf16[4,2,256,1536]{3,2,1,0:T(8,128)(2,1)}, bf16[4,2,64,2048]{3,2,1,0:T(8,128)(2,1)S(1)}) custom-call(bf16[4,2,256,1536]{3,2,1,0:T(8,128)(2,1)} %bitcast.154, bf16[4,2,64,2048]{3,2,1,0:T(8,128)(2,1)S(1)} %bitcast.144), custom_call_target="tpu_custom_call" | custom-call | bytes 16777216 | tf_op jit(solution)/shard_map/sum_wide_3/pallas_call | solution.py:603
  951.8 6.7 bitcast_convert_fusion.2
  958.5 9.8 fusion.79
  968.2 19.5 %all-reduce.5 = (f32[512]{0:T(512)}, f32[512]{0:T(512)}) all-reduce(f32[512]{0:T(512)S(1)} %get-tuple-element.92, f32[512]{0:T(512)S(1)} %get-tuple-element.87), channel_id=1, replica_groups=mesh['wide'=8,'narrow'=4] {'wide'}, use_global_device_ids=true, to_apply=%region_27.28 | all-reduce | flops 1024 | bytes 8192 | tf_op jit(solution)/shard_map/psum | solution.py:914
  989.5 3.4 fusion.41
  992.9 36.9 %all-reduce.4 = (f32[2048]{0:T(1024)}, f32[2048]{0:T(1024)}) all-reduce(f32[2048]{0:T(1024)S(1)} %get-tuple-element.85, f32[2048]{0:T(1024)S(1)} %get-tuple-element.95), channel_id=1, replica_groups=mesh['wide'=8,'narrow'=4] {'wide','narrow'}, use_global_device_ids=true, to_apply=%region_25.26 | all-reduce | flops 4096 | bytes 32768 | tf_op jit(solution)/shard_map/psum | solution.py:915
  (232 shorter events, 79.4 us)
Async XLA Ops:
  8.0 42.0 %copy-start = (bf16[512,2048]{1,0:T(8,128)(2,1)S(1)}, bf16[512,2048]{1,0:T(8,128)(2,1)}, u32[]{:S(2)}) copy-start(bf16[512,2048]{1,0:T(8,128)(2,1)} %param.23) | copy-start | bytes 6291460
  8.0 76.2 %reduce-scatter.3.cloned.1.call-start = ((), (), s32[]{:S(2)}) async-start(), calls=%async_computation.2 | async-start | bytes 2621440 | tf_op jit(solution)/shard_map/reduce_scatter | solution.py:743
  8.9 23.4 %copy-start.49 = (f32[512]{0:T(512)}, f32[512]{0:T(512)S(1)}, u32[]{:S(2)}) copy-start(f32[512]{0:T(512)S(1)} %convert_element_type.144) | copy-start | bytes 6148
  10.2 22.2 %copy-start.51 = (f32[512]{0:T(512)}, f32[512]{0:T(512)S(1)}, u32[]{:S(2)}) copy-start(f32[512]{0:T(512)S(1)} %convert_element_type.146) | copy-start | bytes 6148
  13.9 32.1 %copy-start.15 = (pred[512,512]{0,1:T(8,128)(4,1)}, pred[512,512]{0,1:T(8,128)(4,1)S(1)}, u32[]{:S(2)}) copy-start(pred[512,512]{0,1:T(8,128)(4,1)S(1)} %fusion.47) | copy-start | bytes 786436
  52.6 233.1 %all-gather.6.cloned.1.call-start = ((), (), s32[]{:S(2)}) async-start(), calls=%async_computation.6 | async-start | bytes 17301504 | tf_op jit(solution)/shard_map/all_gather | solution.py:686
  53.2 591.8 %all-gather.4.cloned.1.call-start = ((), (), s32[]{:S(2)}) async-start(), calls=%async_computation.3 | async-start | bytes 2621440 | tf_op jit(solution)/shard_map/all_gather | solution.py:846
  53.6 34.0 %copy-start.40 = (bf16[2048,32]{0,1:T(8,128)(2,1)S(1)}, bf16[2048,32]{0,1:T(8,128)(2,1)}, u32[]{:S(2)}) copy-start(bf16[2048,32]{0,1:T(8,128)(2,1)} %param.25) | copy-start | bytes 393220
  57.8 157.5 %copy-start.42 = (f32[2048]{0:T(1024)}, f32[2048]{0:T(1024)S(1)}, u32[]{:S(2)}) copy-start(f32[2048]{0:T(1024)S(1)} %convert_element_type.153) | copy-start | bytes 24580
  88.5 126.7 %copy-start.61 = (f32[128]{0:T(128)}, f32[128]{0:T(128)S(1)}, u32[]{:S(2)}) copy-start(f32[128]{0:T(128)S(1)} %fusion.63) | copy-start | bytes 1540
  234.6 21.5 %copy-start.25 = (bf16[4,2048,256]{2,1,0:T(8,128)(2,1)S(1)}, bf16[4,2048,256]{2,1,0:T(8,128)(2,1)}, u32[]{:S(2)}) copy-start(bf16[4,2048,256]{2,1,0:T(8,128)(2,1)} %param.26) | copy-start | bytes 12582916
  361.5 16.8 %copy-start.26 = (bf16[4,2048,256]{2,1,0:T(8,128)(2,1)S(1)}, bf16[4,2048,256]{2,1,0:T(8,128)(2,1)}, u32[]{:S(2)}) copy-start(bf16[4,2048,256]{2,1,0:T(8,128)(2,1)} %param.26) | copy-start | bytes 12582916
  444.4 158.9 %copy-start.36 = (f32[128,32]{0,1:T(8,128)S(1)}, f32[128,32]{0,1:T(8,128)}, u32[]{:S(2)}) copy-start(f32[128,32]{0,1:T(8,128)} %copy-done.35) | copy-start | bytes 49156
  444.4 158.9 %copy-start.60 = (f32[128]{0:T(128)S(1)}, f32[128]{0:T(128)}, u32[]{:S(2)}) copy-start(f32[128]{0:T(128)} %copy-done.59) | copy-start | bytes 1540
  444.4 158.9 %copy-start.62 = (f32[128]{0:T(128)S(1)}, f32[128]{0:T(128)}, u32[]{:S(2)}) copy-start(f32[128]{0:T(128)} %copy-done.61) | copy-start | bytes 1540
  444.4 159.7 %copy-start.6 = (f32[128,2048]{1,0:T(8,128)S(1)}, f32[128,2048]{1,0:T(8,128)}, u32[]{:S(2)}) copy-start(f32[128,2048]{1,0:T(8,128)} %copy-done.5) | copy-start | bytes 3145732
  444.4 159.7 %copy-start.41 = (bf16[2048,32]{0,1:T(8,128)(2,1)S(1)}, bf16[2048,32]{0,1:T(8,128)(2,1)}, u32[]{:S(2)}) copy-start(bf16[2048,32]{0,1:T(8,128)(2,1)} %param.25) | copy-start | bytes 393220
  444.4 159.7 %copy-start.43 = (f32[2048]{0:T(1024)S(1)}, f32[2048]{0:T(1024)}, u32[]{:S(2)}) copy-start(f32[2048]{0:T(1024)} %copy-done.42) | copy-start | bytes 24580
  444.5 159.7 %copy-start.66 = (f32[128]{0:T(128)S(1)}, f32[128]{0:T(128)}, u32[]{:S(2)}) copy-start(f32[128]{0:T(128)} %copy-done.65) | copy-start | bytes 1540
  444.5 161.7 %copy-start.73 = (f32[128]{0:T(128)S(1)}, f32[128]{0:T(128)}, u32[]{:S(2)}) copy-start(f32[128]{0:T(128)} %copy-done.72) | copy-start | bytes 1540
  444.5 162.7 %copy-start.20 = (bf16[128,2048]{1,0:T(8,128)(2,1)S(1)}, bf16[128,2048]{1,0:T(8,128)(2,1)}, u32[]{:S(2)}) copy-start(bf16[128,2048]{1,0:T(8,128)(2,1)} %param.31) | copy-start | bytes 1572868
  608.3 39.7 %copy-start.16 = (pred[512,512]{0,1:T(8,128)(4,1)S(1)}, pred[512,512]{0,1:T(8,128)(4,1)}, u32[]{:S(2)}) copy-start(pred[512,512]{0,1:T(8,128)(4,1)} %copy-done.15) | copy-start | bytes 786436
  608.4 379.4 %reduce-scatter.5.cloned.1.call-start = ((), (), s32[]{:S(2)}) async-start(), calls=%async_computation.4 | async-start | bytes 2621440 | tf_op jit(solution)/shard_map/reduce_scatter | solution.py:900
  662.9 8.0 copy-start.63
  682.8 18.4 %copy-start.44 = (f32[32,128]{1,0:T(8,128)S(1)}, f32[32,128]{1,0:T(8,128)}, u32[]{:S(2)}) copy-start(f32[32,128]{1,0:T(8,128)} %get-tuple-element.82) | copy-start | bytes 49156
  682.8 347.1 %all-reduce.10.cloned.1.call-start = ((), (), s32[]{:S(2)}) async-start(), calls=%async_computation.5 | async-start | bytes 524288 | tf_op jit(solution)/shard_map/psum | solution.py:915
  682.8 18.4 %copy-start.14 = (bf16[128,2048]{1,0:T(8,128)(2,1)S(1)}, bf16[128,2048]{1,0:T(8,128)(2,1)}, u32[]{:S(2)}) copy-start(bf16[128,2048]{1,0:T(8,128)(2,1)} %copy-done.13) | copy-start | bytes 1572868
  702.3 17.0 %copy-start.27 = (bf16[4,1536,256]{1,2,0:T(8,128)(2,1)S(1)}, bf16[4,1536,256]{1,2,0:T(8,128)(2,1)}, u32[]{:S(2)}) copy-start(bf16[4,1536,256]{1,2,0:T(8,128)(2,1)} %get-tuple-element.110) | copy-start | bytes 9437188
  719.2 16.7 %copy-start.48 = (f32[2048]{0:T(1024)S(1)}, f32[2048]{0:T(1024)}, u32[]{:S(2)}) copy-start(f32[2048]{0:T(1024)} %copy-done.47) | copy-start | bytes 24580
  719.2 16.7 %copy-start.70 = (f32[512]{0:T(512)S(1)}, f32[512]{0:T(512)}, u32[]{:S(2)}) copy-start(f32[512]{0:T(512)} %copy-done.69) | copy-start | bytes 6148
  735.9 8.4 copy-start.74
  735.9 8.4 copy-start.76
  (50 other events, 151.9 us)
Sparse Core Ops, SparseCore 0:
  52.7 31.4 reduce-scatter.2
  608.5 36.4 all-gather.3
  682.9 32.2 reduce-scatter.4
Sparse Core Ops, SparseCore 1:
  56.0 152.1 all-gather.5
  736.0 127.4 all-reduce.9

commit v3 on v2

--- a/solution.py
+++ b/solution.py
@@ -86,6 +86,9 @@
         y = flip(self.y, first * core + second * (1 - core))
         return (z * 2 + x, y * 2 + core)
 
+    def across(self, other_core=0):
+        return (self.z * 2 + self.x, (1 - self.y) * 2 + flip(self.core, other_core))
+
     def block(self, z, first, second, other_core=0):
         wide, narrow = self.device(z, first, second, other_core)
         return wide * 4 + narrow
@@ -108,7 +111,7 @@
 
 def add_into(target, *sources):
     rows = target.shape[0]
-    step = min(rows, ADD_ROWS)
+    step = ADD_ROWS if rows % ADD_ROWS == 0 else 8
 
     @pl.loop(0, rows // step)
     def _(i):
@@ -403,7 +406,7 @@
     )(*arrays)
 
 
-def sum_task(at, kind, rows, source, result, held, from_pair, from_below, from_above, load_sem, send, recv, delay):
+def sum_task(at, kind, rows, source, result, held, from_pair, from_below, from_above, load_sem, send, recv, delay, prepare=None):
     z, x = at.z, at.x
     pair = ((z * 2 + 1 - x), at.y * 2 + at.core)
     up, down = ((z + 1) * 2 + x, at.y * 2 + at.core), ((z - 1) * 2 + x, at.y * 2 + at.core)
@@ -436,6 +439,8 @@
             load(line).start()
         for line in ORDER:
             load(line).wait()
+        if prepare is not None:
+            yield from prepare(held)
 
     def add(target, extra):
         if pair_first:
@@ -567,50 +572,206 @@
         over_block(x).wait_send()
 
 
-CHUNK = 64
-
-
-def sum_wide_kernel(plan, count, *refs):
+def narrow_sum_task(at, source, result, mine, from_twin, from_peer, load_sem, send, recv):
+    twin, peer = at.device(at.z, 0, 0, 1), at.across()
+
+    def give(y):
+        return remote(source.at[y * 2 + 1 - at.core], from_twin.at[y], send.at[y], recv.at[y], twin)
+
+    def load(y):
+        return pltpu.make_async_copy(source.at[y * 2 + at.core], mine.at[y], load_sem.at[y])
+    order = (1 - at.y, at.y)
+    for y in order:
+        give(y).start()
+        load(y).start()
+    other, own = order
+    over = remote(mine.at[other], from_peer, send.at[2], recv.at[2], peer)
+    for y in order:
+        load(y).wait()
+        give(y).wait_recv()
+        add_into(mine.at[y], from_twin.at[y])
+        if y is other:
+            over.start()
+    yield
+    over.wait_recv()
+    add_into(mine.at[own], from_peer)
+    store = pltpu.make_async_copy(mine.at[own], result, load_sem.at[2])
+    store.start()
+    yield
+    store.wait()
+    over.wait_send()
+    for y in order:
+        give(y).wait_send()
+
+
+def narrow_sum_scratch(block, dtype):
+    return [
+        pltpu.VMEM((2,) + block, dtype),
+        pltpu.VMEM((2,) + block, dtype),
+        pltpu.VMEM(block, dtype),
+        pltpu.SemaphoreType.DMA((3,)),
+        pltpu.SemaphoreType.DMA((3,)),
+        pltpu.SemaphoreType.DMA((3,)),
+    ]
+
+
+def run_tasks(tasks):
+    while tasks:
+        tasks = [task for task in tasks if next(task, tasks) is not tasks]
+
+
+def narrow_sum_kernel(source, result, *scratch):
+    at = Place()
+    greet([(at.device(at.z, 0, 0, 1), None), (at.across(), None)])
+    run_tasks([narrow_sum_task(at, source, result, *scratch)])
+
+
+def narrow_sum(collective_id, parts):
+    block = parts.shape[1:]
+    return pl.pallas_call(
+        narrow_sum_kernel,
+        name=f"narrow_sum_{collective_id}",
+        out_shape=jax.ShapeDtypeStruct(block, parts.dtype),
+        in_specs=[pl.BlockSpec(memory_space=pl.ANY)],
+        out_specs=pl.BlockSpec(memory_space=pl.ANY),
+        scratch_shapes=narrow_sum_scratch(block, parts.dtype),
+        compiler_params=pltpu.CompilerParams(collective_id=collective_id, has_side_effects=True),
+    )(parts)
+
+
+def narrow_gather_kernel(block, result, held, load_sem, send, recv):
+    at = Place()
+    twin, peer = at.device(at.z, 0, 0, 1), at.across()
+    greet([(twin, None), (peer, None)])
+    here, there = at.y * 2 + at.core, (1 - at.y) * 2 + at.core
+    load = pltpu.make_async_copy(block, held, load_sem.at[0])
+    load.start()
+    over = remote(block, result.at[here], send.at[0], recv.at[here], peer)
+    beside = remote(block, result.at[here], send.at[1], recv.at[here], twin)
+    over.start()
+    beside.start()
+    load.wait()
+    store = pltpu.make_async_copy(held, result.at[here], load_sem.at[1])
+    store.start()
+    passed = remote(result.at[there], result.at[there], send.at[2], recv.at[there], twin)
+    passed.wait_recv()
+    passed.start()
+    for y in (0, 1):
+        remote(block, result.at[y * 2 + 1 - at.core], send.at[1], recv.at[y * 2 + 1 - at.core], twin).wait_recv()
+    for copy in (over, beside, passed):
+        copy.wait_send()
+    store.wait()
+
+
+def narrow_gather(collective_id, block):
+    return pl.pallas_call(
+        narrow_gather_kernel,
+        name=f"narrow_gather_{collective_id}",
+        out_shape=jax.ShapeDtypeStruct((4,) + block.shape, block.dtype),
+        in_specs=[pl.BlockSpec(memory_space=pl.ANY)],
+        out_specs=pl.BlockSpec(memory_space=pl.ANY),
+        scratch_shapes=[
+            pltpu.VMEM(block.shape, block.dtype),
+            pltpu.SemaphoreType.DMA((2,)),
+            pltpu.SemaphoreType.DMA((3,)),
+            pltpu.SemaphoreType.DMA((4,)),
+        ],
+        compiler_params=pltpu.CompilerParams(collective_id=collective_id, has_side_effects=True),
+    )(block)
+
+
+def narrow_total_kernel(values, result, others, send, recv):
+    at = Place()
+    places = [at.device(at.z, 0, 0, 1), at.across(), at.across(1)]
+    greet([(place, None) for place in places])
+    copies = [remote(values, others.at[i], send.at[i], recv.at[i], place) for i, place in enumerate(places)]
+    for copy in copies:
+        copy.start()
+    for copy in copies:
+        copy.wait()
+    result[...] = (values[...] + others[0]) + (others[1] + others[2])
+
+
+def narrow_total(collective_id, values):
+    return pl.pallas_call(
+        narrow_total_kernel,
+        name=f"narrow_total_{collective_id}",
+        out_shape=jax.ShapeDtypeStruct(values.shape, values.dtype),
+        in_specs=[pl.BlockSpec(memory_space=pltpu.VMEM)],
+        out_specs=pl.BlockSpec(memory_space=pltpu.VMEM),
+        scratch_shapes=[
+            pltpu.VMEM((3,) + values.shape, values.dtype),
+            pltpu.SemaphoreType.DMA((3,)),
+            pltpu.SemaphoreType.DMA((3,)),
+        ],
+        compiler_params=pltpu.CompilerParams(collective_id=collective_id, has_side_effects=True),
+    )(values)
+
+
+def final_sums_kernel(plan, count, *refs):
     ins, outs, rest = refs[:count], refs[count:2 * count], list(refs[2 * count:])
     at = Place()
     pair = (at.z * 2 + 1 - at.x, at.y * 2 + at.core)
     up, down = ((at.z + 1) * 2 + at.x, at.y * 2 + at.core), ((at.z - 1) * 2 + at.x, at.y * 2 + at.core)
-    greet([(pair, None), (up, at.z < LINE - 1), (down, at.z > 0)])
-    load_sem, send, recv = rest[-3:]
-    tasks = []
-    for number, (which, begin, kind, delay) in enumerate(plan):
+    twin, peer = at.device(at.z, 0, 0, 1), at.across()
+    greet([(pair, None), (twin, None), (peer, None), (up, at.z < LINE - 1), (down, at.z > 0)])
+    narrow_scratch, rest = rest[-6:], rest[:-6]
+    load_sem, send, recv, others, other_send, other_recv = rest[-6:]
+
+    def over_narrow(held):
+        beside = remote(ins[count - 2], others.at[0], other_send.at[0], other_recv.at[0], twin)
+        beside.start()
+        yield
+        beside.wait_recv()
+        for line in range(LINE):
+            for face in (0, 1):
+                add_into(held.at[line, face], others.at[0, line, face])
+        across = remote(held, others.at[1], other_send.at[1], other_recv.at[1], peer)
+        across.start()
+        yield
+        across.wait()
+        beside.wait_send()
+        for line in range(LINE):
+            for face in (0, 1):
+                add_into(held.at[line, face], others.at[1, line, face])
+    tasks = [narrow_sum_task(at, ins[-1], outs[-1], *narrow_scratch)]
+    for number, (which, begin, rows, kind, delay) in enumerate(plan):
         held, from_pair, from_below, from_above = rest[4 * number:4 * number + 4]
-        tasks.append(sum_task(at, kind, pl.ds(begin, CHUNK), ins[which], outs[which], held, from_pair, from_below,
-                              from_above, load_sem.at[number], send.at[number], recv.at[number], delay))
-    while tasks:
-        tasks = [task for task in tasks if next(task, tasks) is not tasks]
-
-
-def sum_wide(collective_id, plan, *arrays):
+        tasks.append(sum_task(at, kind, pl.ds(begin, rows), ins[which], outs[which], held, from_pair, from_below,
+                              from_above, load_sem.at[number], send.at[number], recv.at[number], delay,
+                              over_narrow if which == count - 2 else None))
+    run_tasks(tasks)
+
+
+def final_sums(collective_id, plan, *arrays):
     count, steps = len(arrays), len(plan)
     scratch = []
-    for which, _, kind, _ in plan:
+    for which, _, rows, kind, _ in plan:
         columns, dtype = arrays[which].shape[3], arrays[which].dtype
-        lead = () if kind == "pair" else (2,)
-        block = lead + (CHUNK, columns)
+        block = (() if kind == "pair" else (2,)) + (rows, columns)
         scratch += [
             pltpu.VMEM((LINE,) + block, dtype),
-            pltpu.VMEM(((LINE,) if kind == "pair" else ()) + (CHUNK, columns), dtype),
+            pltpu.VMEM(((LINE,) if kind == "pair" else ()) + (rows, columns), dtype),
             pltpu.VMEM((LINE,) + block, dtype),
             pltpu.VMEM((LINE,) + block, dtype),
         ]
+    small, parts = arrays[-2:]
     moved = sum(a.size * a.dtype.itemsize for a in arrays)
     return pl.pallas_call(
-        functools.partial(sum_wide_kernel, plan, count),
-        name=f"sum_wide_{collective_id}",
-        out_shape=tuple(jax.ShapeDtypeStruct(a.shape, a.dtype) for a in arrays),
+        functools.partial(final_sums_kernel, plan, count),
+        name=f"final_sums_{collective_id}",
+        out_shape=tuple(jax.ShapeDtypeStruct(a.shape, a.dtype) for a in arrays[:-1])
+        + (jax.ShapeDtypeStruct(parts.shape[1:], parts.dtype),),
         in_specs=[pl.BlockSpec(memory_space=pl.ANY)] * count,
         out_specs=tuple(pl.BlockSpec(memory_space=pl.ANY) for _ in arrays),
         scratch_shapes=scratch + [
             pltpu.SemaphoreType.DMA((steps, 5)),
             pltpu.SemaphoreType.DMA((steps, 6, 4)),
             pltpu.SemaphoreType.DMA((steps, 4, 8)),
-        ],
+            pltpu.VMEM((2,) + small.shape, small.dtype),
+            pltpu.SemaphoreType.DMA((2,)),
+            pltpu.SemaphoreType.DMA((2,)),
+        ] + narrow_sum_scratch(parts.shape[1:], parts.dtype),
         compiler_params=pltpu.CompilerParams(
             collective_id=collective_id, has_side_effects=True, vmem_limit_bytes=48 << 20),
         cost_estimate=pl.CostEstimate(flops=0, transcendentals=0, bytes_accessed=2 * moved),
@@ -633,15 +794,243 @@
     return tuple(lax.psum_scatter(a, BOTH, scatter_dimension=0) for a in arrays)
 
 
-SUM_PLAN = ((0, 0, "pair", 0), (1, 0, "line", 0), (0, 64, "pair", 1), (0, 128, "pair", 2), (0, 192, "pair", 3))
-
-
-def total_wide(joined, out_part):
-    if own_exchange():
-        shapes = joined.shape, out_part.shape
-        dealt = [a.reshape(LINE, 2, a.shape[0] // 8, a.shape[1]) for a in (joined, out_part)]
-        return tuple(a.reshape(shape) for a, shape in zip(sum_wide(3, SUM_PLAN, *dealt), shapes))
-    return lax.psum((joined, out_part), "wide")
+FINAL_PLAN = (
+    (4, 0, 72, "line", 0),
+    (0, 0, 128, "pair", 0),
+    (3, 0, 64, "line", 0),
+    (0, 128, 128, "pair", 1),
+    (1, 0, 128, "pair", 2),
+    (1, 128, 128, "pair", 3),
+    (2, 0, 128, "pair", 4),
+    (2, 128, 128, "pair", 5),
+)
+
+
+def total_weights(weights, gains, everywhere, parts):
+    if not own_exchange():
+        totals = tuple(a.astype(jnp.float32) for a in lax.psum(tuple(a.astype(jnp.bfloat16) for a in weights), "wide"))
+        own = lax.psum_scatter(parts, "narrow", scatter_dimension=0, tiled=True)
+        return totals, lax.psum(gains, "wide"), lax.psum(everywhere, BOTH), own
+    gain_rows = jnp.concatenate([a.reshape(-1, 128) for a in gains], axis=0)
+    mine = lax.axis_index("narrow")
+    gain_slots = lax.dynamic_update_slice_in_dim(jnp.zeros((4,) + gain_rows.shape, jnp.float32), gain_rows[None], mine, 0)
+    pieces = [a.reshape(-1, 128) for a in everywhere] + [gain_slots.reshape(-1, 128)]
+    small = jnp.concatenate(pieces, axis=0)
+    arrays = [a.astype(jnp.bfloat16).reshape(LINE, 2, a.shape[0] // 8, a.shape[1]) for a in weights]
+    results = final_sums(
+        3, FINAL_PLAN, *arrays, small.reshape(LINE, 2, small.shape[0] // 8, 128), parts.reshape(4, -1, parts.shape[1])
+    )
+    totals = tuple(r.reshape(a.shape).astype(jnp.float32) for r, a in zip(results, weights))
+    small_total = results[-2].reshape(small.shape)
+    summed, begin = [], 0
+    for array, piece in zip(everywhere, pieces):
+        summed.append(small_total[begin:begin + piece.shape[0]].reshape(array.shape))
+        begin += piece.shape[0]
+    own_gains = lax.dynamic_slice_in_dim(small_total[begin:].reshape(gain_slots.shape), mine, 1, 0).reshape(len(gains), -1)
+    return totals, tuple(own_gains[i].reshape(g.shape) for i, g in enumerate(gains)), tuple(summed), results[-1]
+
+
+def narrow_sums(collective_id, values):
+    if not own_exchange():
+        return lax.psum(values, "narrow")
+    total = narrow_total(collective_id, jnp.stack(values).reshape(-1, 128)).reshape(len(values), -1)
+    return tuple(total[i] for i in range(len(values)))
+
+
+def narrow_deal(collective_id, parts):
+    if not own_exchange():
+        return lax.psum_scatter(parts, "narrow", scatter_dimension=0, tiled=True)
+    return narrow_sum(collective_id, parts.reshape(4, -1, parts.shape[1]))
+
+
+def narrow_all(collective_id, block):
+    if not own_exchange():
+        return lax.all_gather(block, "narrow", axis=0, tiled=True)
+    return narrow_gather(collective_id, block).reshape(-1, block.shape[1])
+
+
+def experts_plain(rows_all, grads_all, places_here, probs_here, gate_weight, up_weight, down_weight, capacity):
+    block_count, own_rows, model_width = rows_all.shape
+    experts_here = gate_weight.shape[0]
+    highest_precision = lax.Precision.HIGHEST
+    pick = places_here[:, :, None, :] == jnp.arange(capacity, dtype=jnp.float32)[None, None, :, None]
+    pick_low = pick.astype(jnp.bfloat16)
+    slot_gate = jnp.sum(jnp.where(pick, probs_here[:, :, None, :], 0.0), axis=-1)
+    slot_gate = slot_gate.transpose(1, 0, 2).reshape(experts_here, block_count * capacity, 1)
+
+    def spread(rows):
+        out = jnp.einsum("best,btd->ebsd", pick_low, rows, preferred_element_type=jnp.float32)
+        return out.astype(jnp.bfloat16).reshape(experts_here, block_count * capacity, model_width)
+
+    def collect(slots):
+        out = jnp.einsum(
+            "best,ebsd->btd",
+            pick_low,
+            slots.reshape(experts_here, block_count, capacity, model_width),
+            preferred_element_type=jnp.float32,
+        )
+        return out.astype(jnp.bfloat16)
+
+    slot_rows = spread(rows_all)
+    slot_grads = spread(grads_all)
+    gate_pre = jnp.einsum("erd,edf->erf", slot_rows, gate_weight, preferred_element_type=jnp.float32)
+    up_pre = jnp.einsum("erd,edf->erf", slot_rows, up_weight, preferred_element_type=jnp.float32)
+    activated, unit_back = jax.vjp(gated_unit, gate_pre, up_pre)
+    gated_act = (activated * slot_gate).astype(jnp.bfloat16)
+    raw_act_grad = jnp.einsum("erd,efd->erf", slot_grads, down_weight, preferred_element_type=jnp.float32)
+    slot_gate_grads = jnp.sum(activated * raw_act_grad, axis=-1)
+    gate_grad_full, up_grad_full = unit_back(raw_act_grad * slot_gate)
+    gate_grad_low = gate_grad_full.astype(jnp.bfloat16)
+    up_grad_low = up_grad_full.astype(jnp.bfloat16)
+    gate_grad_parts = jnp.einsum(
+        "best,ebs->bet",
+        pick.astype(jnp.float32),
+        slot_gate_grads.reshape(experts_here, block_count, capacity),
+        precision=highest_precision,
+    )
+    back_slots = jnp.einsum(
+        "erf,edf->erd", gate_grad_low, gate_weight, preferred_element_type=jnp.float32
+    ) + jnp.einsum("erf,edf->erd", up_grad_low, up_weight, preferred_element_type=jnp.float32)
+    out_slots = jnp.einsum("erf,efd->erd", gated_act, down_weight, preferred_element_type=jnp.float32)
+    return (
+        collect(out_slots.astype(jnp.bfloat16)),
+        collect(back_slots.astype(jnp.bfloat16)),
+        gate_grad_parts,
+        jnp.einsum("erd,erf->edf", slot_rows, gate_grad_low, preferred_element_type=jnp.float32),
+        jnp.einsum("erd,erf->edf", slot_rows, up_grad_low, preferred_element_type=jnp.float32),
+        jnp.einsum("erf,erd->efd", gated_act, slot_grads, preferred_element_type=jnp.float32),
+    )
+
+
+STEP_BLOCKS = 4
+COLUMNS = 512
+
+
+def dot(left, right, left_dim=1, right_dim=0):
+    return lax.dot_general(
+        left, right, (((left_dim,), (right_dim,)), ((), ())), preferred_element_type=jnp.float32
+    )
+
+
+def experts_kernel(
+    capacity, rows, grads, places, gates, gate_w, up_w, down_w,
+    out, back, gate_grads, gate_dw, up_dw, down_dw, row_slots, grad_slots,
+):
+    experts, width = gate_w.shape[0], gate_w.shape[1]
+    tokens = rows.shape[1]
+    slot_ids = lax.broadcasted_iota(jnp.int32, (capacity, tokens), 0).astype(jnp.float32)
+
+    @pl.when(pl.program_id(0) == 0)
+    def _():
+        for target in (gate_dw, up_dw, down_dw):
+            @pl.loop(0, experts)
+            def _(e):
+                target[e] = jnp.zeros(target.shape[1:], jnp.float32)
+
+    def chunks(body):
+        @pl.loop(0, width // COLUMNS)
+        def _(i):
+            body(pl.ds(pl.multiple_of(i * COLUMNS, COLUMNS), COLUMNS))
+
+    def pick_of(block, expert):
+        return places[block, pl.ds(expert, 1), :] == slot_ids
+
+    def picks(block):
+        return jnp.concatenate(
+            [pick_of(block, e).astype(jnp.float32) for e in range(experts)], axis=0
+        ).astype(jnp.bfloat16)
+
+    for block in range(STEP_BLOCKS):
+        pick = picks(block)
+        part = pl.ds(block * capacity, capacity)
+
+        def spread(columns):
+            for source, target in ((rows, row_slots), (grads, grad_slots)):
+                slots = dot(pick, source[block, :, columns]).astype(jnp.bfloat16)
+                for e in range(experts):
+                    target[e, part, columns] = slots[e * capacity:(e + 1) * capacity]
+        chunks(spread)
+
+    @pl.loop(0, experts)
+    def _(e):
+        gate_pre, up_pre = dot(row_slots[e], gate_w[e]), dot(row_slots[e], up_w[e])
+        raw = dot(grad_slots[e], down_w[e], 1, 1)
+        slot_gate = jnp.concatenate([
+            jnp.sum(jnp.where(pick_of(block, e), gates[block, pl.ds(e, 1), :], 0.0), axis=1, keepdims=True)
+            for block in range(STEP_BLOCKS)
+        ], axis=0)
+        sigma = 1.0 / (1.0 + jnp.exp(-gate_pre))
+        silu = gate_pre * sigma
+        act = silu * up_pre
+        slot_sum = jnp.sum(act * raw, axis=1, keepdims=True)
+        for block in range(STEP_BLOCKS):
+            gate_grads[block, pl.ds(e, 1), :] = jnp.sum(
+                jnp.where(pick_of(block, e), slot_sum[block * capacity:(block + 1) * capacity], 0.0),
+                axis=0, keepdims=True,
+            )
+        gated = (act * slot_gate).astype(jnp.bfloat16)
+        act_grad = raw * slot_gate
+        gate_low = (act_grad * up_pre * sigma * (1.0 + gate_pre * (1.0 - sigma))).astype(jnp.bfloat16)
+        up_low = (act_grad * silu).astype(jnp.bfloat16)
+
+        def columns_of(columns):
+            down_dw[e, :, columns] += dot(gated, grad_slots[e, :, columns], 0, 0)
+            grad_slots[e, :, columns] = dot(gated, down_w[e, :, columns]).astype(jnp.bfloat16)
+            turned = row_slots[e, :, columns].T
+            gate_dw[e, columns, :] += dot(turned, gate_low)
+            up_dw[e, columns, :] += dot(turned, up_low)
+            row_slots[e, :, columns] = (
+                dot(gate_low, gate_w[e, columns, :], 1, 1) + dot(up_low, up_w[e, columns, :], 1, 1)
+            ).astype(jnp.bfloat16)
+        chunks(columns_of)
+
+    for block in range(STEP_BLOCKS):
+        pick = picks(block)
+        part = pl.ds(block * capacity, capacity)
+
+        def collect(columns):
+            for source, target in ((row_slots, back), (grad_slots, out)):
+                slots = jnp.concatenate([source[e, part, columns] for e in range(experts)], axis=0)
+                target[block, :, columns] = dot(pick, slots, 0, 0).astype(jnp.bfloat16)
+        chunks(collect)
+
+
+def experts_fused(rows_all, grads_all, places_here, probs_here, gate_weight, up_weight, down_weight, capacity):
+    block_count, own_rows, width = rows_all.shape
+    experts, _, hidden = gate_weight.shape
+    step_rows = STEP_BLOCKS * capacity
+
+    def stepped(*shape):
+        return pl.BlockSpec((STEP_BLOCKS,) + shape, lambda i: (i,) + (0,) * len(shape))
+
+    def whole(array):
+        return pl.BlockSpec(array.shape, lambda i: (0,) * array.ndim, pipeline_mode=pl.Buffered(1))
+    weights = (gate_weight, up_weight, down_weight)
+    flops = 2 * block_count * experts * (9 * capacity * width * hidden + 4 * capacity * own_rows * width)
+    return pl.pallas_call(
+        functools.partial(experts_kernel, capacity),
+        name="experts",
+        grid=(block_count // STEP_BLOCKS,),
+        out_shape=(
+            jax.ShapeDtypeStruct(rows_all.shape, jnp.bfloat16),
+            jax.ShapeDtypeStruct(rows_all.shape, jnp.bfloat16),
+            jax.ShapeDtypeStruct((block_count, experts, own_rows), jnp.float32),
+        ) + tuple(jax.ShapeDtypeStruct(w.shape, jnp.float32) for w in weights),
+        in_specs=[
+            stepped(own_rows, width), stepped(own_rows, width), stepped(experts, own_rows), stepped(experts, own_rows),
+        ] + [whole(w) for w in weights],
+        out_specs=(stepped(own_rows, width), stepped(own_rows, width), stepped(experts, own_rows))
+        + tuple(whole(w) for w in weights),
+        scratch_shapes=[
+            pltpu.VMEM((experts, step_rows, width), jnp.bfloat16),
+            pltpu.VMEM((experts, step_rows, width), jnp.bfloat16),
+        ],
+        compiler_params=pltpu.CompilerParams(
+            dimension_semantics=("arbitrary",), vmem_limit_bytes=67_000_000),
+        cost_estimate=pl.CostEstimate(
+            flops=flops, transcendentals=0,
+            bytes_accessed=4 * 2 * rows_all.size + sum(6 * w.size for w in weights)),
+    )(rows_all, grads_all, places_here, probs_here, *weights)
 
 
 def local(
@@ -692,8 +1081,8 @@
     key_proj = projected[:, local_width : 2 * local_width]
     value_proj = projected[:, 2 * local_width :]
     rope_cos, rope_sin = rope_tables(group_rows, head_size)
-    query_total, key_total = lax.psum(
-        (jnp.sum(query_proj * query_proj, axis=1), jnp.sum(key_proj * key_proj, axis=1)), "narrow"
+    query_total, key_total = narrow_sums(
+        4, (jnp.sum(query_proj * query_proj, axis=1), jnp.sum(key_proj * key_proj, axis=1))
     )
     query_inverse = lax.rsqrt(query_total / model_width + norm_epsilon)[:, None]
     key_inverse = lax.rsqrt(key_total / model_width + norm_epsilon)[:, None]
@@ -740,11 +1129,8 @@
 
     mixed_blocks, log_totals = lax.map(attend, jnp.arange(blocks))
     heads_out = mixed_blocks.reshape(group_rows, local_width).astype(jnp.bfloat16)
-    attn_own = lax.psum_scatter(
-        jnp.dot(heads_out, out_weight, preferred_element_type=jnp.float32).astype(jnp.bfloat16),
-        "narrow",
-        scatter_dimension=0,
-        tiled=True,
+    attn_own = narrow_deal(
+        6, jnp.dot(heads_out, out_weight, preferred_element_type=jnp.float32).astype(jnp.bfloat16)
     ).astype(jnp.float32)
     input_own = lax.dynamic_slice_in_dim(inputs_all, row_begin, own_rows, 0)
     hidden = input_own + attn_own
@@ -758,70 +1144,17 @@
     expert_begin = lax.axis_index("wide") * experts_here
     probs_here = lax.dynamic_slice_in_dim(routes_all, expert_begin, experts_here, 1)
     places_here = lax.dynamic_slice_in_dim(routes_all, experts_all + expert_begin, experts_here, 1)
-    pick = places_here[:, :, None, :] == jnp.arange(capacity, dtype=jnp.float32)[None, None, :, None]
-    pick_low = pick.astype(jnp.bfloat16)
-    slot_gate = jnp.sum(jnp.where(pick, probs_here[:, :, None, :], 0.0), axis=-1)
-    slot_gate = slot_gate.transpose(1, 0, 2).reshape(experts_here, block_count * capacity, 1)
-
-    def spread(rows):
-        out = jnp.einsum(
-            "best,btd->ebsd",
-            pick_low,
-            rows,
-            preferred_element_type=jnp.float32,
-        )
-        return out.astype(jnp.bfloat16).reshape(experts_here, block_count * capacity, model_width)
-
-    def collect(slots):
-        out = jnp.einsum(
-            "best,ebsd->btd",
-            pick_low,
-            slots.reshape(experts_here, block_count, capacity, model_width),
-            preferred_element_type=jnp.float32,
-        )
-        return out.astype(jnp.bfloat16)
-
-    slot_rows = spread(rows_all)
-    slot_grads = spread(grads_all)
-    gate_pre = jnp.einsum("erd,edf->erf", slot_rows, gate_weight, preferred_element_type=jnp.float32)
-    up_pre = jnp.einsum("erd,edf->erf", slot_rows, up_weight, preferred_element_type=jnp.float32)
-    activated, unit_back = jax.vjp(gated_unit, gate_pre, up_pre)
-    gated_act = (activated * slot_gate).astype(jnp.bfloat16)
-    raw_act_grad = jnp.einsum(
-        "erd,efd->erf", slot_grads, down_weight, preferred_element_type=jnp.float32
-    )
-    slot_gate_grads = jnp.sum(activated * raw_act_grad, axis=-1)
-    gate_grad_full, up_grad_full = unit_back(raw_act_grad * slot_gate)
-    gate_grad_low = gate_grad_full.astype(jnp.bfloat16)
-    up_grad_low = up_grad_full.astype(jnp.bfloat16)
-    gate_grad_parts = jnp.einsum(
-        "best,ebs->bet",
-        pick.astype(jnp.float32),
-        slot_gate_grads.reshape(experts_here, block_count, capacity),
-        precision=highest_precision,
+    experts = experts_fused if own_exchange() and capacity % 16 == 0 else experts_plain
+    out_parts, back_parts, gate_grad_parts, gate_weight_grad, up_weight_grad, down_weight_grad = experts(
+        rows_all, grads_all, places_here, probs_here, gate_weight, up_weight, down_weight, capacity
     )
     gate_grad_wide = lax.dynamic_update_slice_in_dim(
         jnp.zeros((block_count, experts_all, own_rows), jnp.float32), gate_grad_parts, expert_begin, 1
     )
-    back_slots = jnp.einsum(
-        "erf,edf->erd", gate_grad_low, gate_weight, preferred_element_type=jnp.float32
-    ) + jnp.einsum("erf,edf->erd", up_grad_low, up_weight, preferred_element_type=jnp.float32)
-    out_slots = jnp.einsum(
-        "erf,efd->erd", gated_act, down_weight, preferred_element_type=jnp.float32
-    )
     rows_back, prob_grads, moe_out = scatter_all(
-        collect(back_slots.astype(jnp.bfloat16)), gate_grad_wide, collect(out_slots.astype(jnp.bfloat16))
+        back_parts, gate_grad_wide, out_parts
     )
     rows_back, prob_grads, moe_out = rows_back.astype(jnp.float32), prob_grads.T, moe_out.astype(jnp.float32)
-    down_weight_grad = jnp.einsum(
-        "erf,erd->efd", gated_act, slot_grads, preferred_element_type=jnp.float32
-    )
-    gate_weight_grad = jnp.einsum(
-        "erd,erf->edf", slot_rows, gate_grad_low, preferred_element_type=jnp.float32
-    )
-    up_weight_grad = jnp.einsum(
-        "erd,erf->edf", slot_rows, up_grad_low, preferred_element_type=jnp.float32
-    )
     block_output = (hidden + moe_out).astype(jnp.bfloat16)
     logit_grads = route_probs * (
         prob_grads - jnp.sum(route_probs * prob_grads, axis=-1, keepdims=True)
@@ -843,7 +1176,7 @@
     hidden_path, moe_gain_part = norm_two_back(normed_two_grad)
     hidden_grad = cotangent_full + hidden_path
     hidden_grad_low = hidden_grad.astype(jnp.bfloat16)
-    gathered_piece = lax.all_gather(hidden_grad_low, "narrow", axis=0, tiled=True)
+    gathered_piece = narrow_all(7, hidden_grad_low)
     heads_grad_acc = contract_last(gathered_piece, out_weight)
     out_weight_acc = contract_rows(heads_out, gathered_piece)
     heads_grad_low = heads_grad_acc.astype(jnp.bfloat16).reshape(group_rows, local_heads, head_size)
@@ -882,9 +1215,8 @@
     key_gain_part = jnp.sum(key_normed_grad * key_proj * key_inverse, axis=0)
     query_gained = query_normed_grad * query_scale
     key_gained = key_normed_grad * key_scale
-    query_dot, key_dot = lax.psum(
-        (jnp.sum(query_proj * query_gained, axis=1), jnp.sum(key_proj * key_gained, axis=1)),
-        "narrow",
+    query_dot, key_dot = narrow_sums(
+        5, (jnp.sum(query_proj * query_gained, axis=1), jnp.sum(key_proj * key_gained, axis=1))
     )
     query_proj_grad = (
         query_inverse * query_gained
@@ -896,25 +1228,24 @@
     proj_grad_low = jnp.concatenate(
         [query_proj_grad, key_proj_grad, value_grad.reshape(group_rows, local_width)], axis=1
     ).astype(jnp.bfloat16)
-    joined_grad = contract_rows(normed_one, proj_grad_low)
-    normed_one_grad = lax.psum_scatter(
-        contract_last(proj_grad_low, joined_weight).astype(jnp.bfloat16),
-        "narrow",
-        scatter_dimension=0,
-        tiled=True,
-    ).astype(jnp.float32)
-    normed_again, norm_one_back = jax.vjp(rms_scale, input_own, attn_gain.astype(jnp.float32))
-    input_path, attn_gain_part = norm_one_back(normed_one_grad)
+    weight_parts = tuple(
+        contract_rows(normed_one, proj_grad_low[:, i * local_width : (i + 1) * local_width]) for i in range(3)
+    ) + (out_weight_acc,)
+    normed_one_part = contract_last(proj_grad_low, joined_weight)
+    scaled_inputs = rms_scale(inputs_all, 1.0)
+    attn_gain_part = jnp.sum(normed_one_part * scaled_inputs, axis=0)
+    totals, gain_totals, summed, normed_one_own = total_weights(
+        weight_parts,
+        (query_gain_part, key_gain_part),
+        (router_part, attn_gain_part, moe_gain_part),
+        normed_one_part.astype(jnp.bfloat16),
+    )
+    query_weight_grad, key_weight_grad, value_weight_grad, out_weight_grad = totals
+    query_gain_grad, key_gain_grad = gain_totals
+    router_weight_grad, attn_gain_grad, moe_gain_grad = summed
+    _, norm_one_back = jax.vjp(lambda v: rms_scale(v, attn_gain.astype(jnp.float32)), input_own)
+    (input_path,) = norm_one_back(normed_one_own.astype(jnp.float32))
     input_grad = (hidden_grad + input_path).astype(jnp.bfloat16)
-    joined_total, out_total = total_wide(joined_grad.astype(jnp.bfloat16), out_weight_acc.astype(jnp.bfloat16))
-    joined_total, out_weight_grad = joined_total.astype(jnp.float32), out_total.astype(jnp.float32)
-    query_weight_grad = joined_total[:, :local_width]
-    key_weight_grad = joined_total[:, local_width : 2 * local_width]
-    value_weight_grad = joined_total[:, 2 * local_width :]
-    query_gain_grad, key_gain_grad = lax.psum((query_gain_part, key_gain_part), "wide")
-    router_weight_grad, attn_gain_grad, moe_gain_grad = lax.psum(
-        (router_part, attn_gain_part, moe_gain_part), ("wide", "narrow")
-    )
     return (
         block_output,
         input_grad,

time: 1050 us -> 881 us (0.84)
  Pallas kernels: 485 us -> 746 us
  matrix products: 279 us -> 39.7 us
  blocking collectives: 70.9 us -> 0 us
  waiting for transfers between devices: 63.4 us -> 0.7 us
  local copies, waits for them, and re-layouts: 77.2 us -> 29.1 us
    pallas_call x1 -> x6, Pallas kernels: 202 us -> 472 us  [the longest x1 236 us: final_sums(): pl.pallas_call(functools.partial(final_sums_kernel, plan, count), name=f'...]
    dot_general x14 -> x0, matrix products: 237 us -> none  [the longest x2 36.5 us: spread(): jnp.einsum('best,btd->ebsd', pick_low, rows, preferred_element_type=jnp.f...]
    psum x4 -> x0, blocking collectives: 70.9 us -> none  [the longest x1 36.9 us: local(): lax.psum((router_part, attn_gain_part, moe_gain_part), ('wide', 'narrow'))]
    convert_element_type x2 -> x0, local copies, waits for them, and re-layouts: 42.6 us -> none  [spread(): out.astype(jnp.bfloat16)]
    all_gather x1 -> x0, waiting for transfers between devices: 36.5 us -> none  [local(): lax.all_gather(hidden_grad_low, 'narrow', axis=0, tiled=True)]
    reduce_scatter x2 -> x0, waiting for transfers between devices: 26.3 us -> none  [the longest x1 26.3 us: local(): lax.psum_scatter(jnp.dot(heads_out, out_weight, preferred_element_type=jn...]
  transfers between devices with their start and end apart: 5 -> 1, of which waited for: 2 -> 0; matrix products, arithmetic and copies ran while one was open for 16% -> 4% of each run, Pallas kernels for 31% -> 16%
where the time goes in v3:
time: 881 us; the launch traced here: 871 us
  Pallas kernels  746 us (85%)
  other arithmetic  40.1 us (5%)
  matrix products  39.7 us (5%)
  local copies, waits for them, and re-layouts  29.1 us (3%)
  between operations  15.5 us (2%)
    pallas_call x1, Pallas kernels, final_sums(): pl.pallas_call(functools.partial(final_sums_kernel, plan, count), name=f'...  236 us
    pallas_call x1, Pallas kernels, experts_fused(): pl.pallas_call(functools.partial(experts_kernel, capacity), name='experts...  191 us
    pallas_call x1, Pallas kernels, scatter_blocks(): pl.pallas_call(functools.partial(scatter_kernel, count), name=f'scatter_b...  160 us
    pallas_call x1, Pallas kernels, gather_blocks(): pl.pallas_call(functools.partial(gather_kernel, count), name=f'gather_blo...  114 us
    pallas_call x1, Pallas kernels, narrow_sum(): pl.pallas_call(narrow_sum_kernel, name=f'narrow_sum_{collective_id}', out...  18.2 us
  transfers between devices with their start and end apart: 1, of which 0 were waited for; matrix products, arithmetic and copies ran while one was open for 4% of the time, Pallas kernels for 16%

profile of v3, /device:TPU:0, one launch (start us, length us, event | category | flops | bytes accessed | tf_op | source)
XLA Modules:
  0.0 871.4 jit_solution(12890403201855461862)
XLA Ops:
  8.6 4.3 convert_element_type.126
  16.2 3.5 fusion.57
  20.8 5.9 narrow_total_4.1
  29.2 2.5 reshape.356
  31.7 2.5 reshape.355
  35.3 3.6 fusion.59
  45.2 3.0 convolution_convert_fusion.4
  48.2 18.2 %narrow_sum_6.1 = bf16[128,2048]{1,0:T(8,128)(2,1)} custom-call(bf16[4,128,2048]{2,1,0:T(8,128)(2,1)} %bitcast.154), custom_call_target="tpu_custom_call" | custom-call | tf_op jit(solution)/shard_map/narrow_sum_6/pallas_call | solution.py:631
  70.4 114.4 %gather_blocks_1.1 = (bf16[32,128,2048]{2,1,0:T(8,128)(2,1)}, f32[32,64,128]{2,1,0:T(8,128)}) custom-call(bf16[128,2048]{1,0:T(8,128)(2,1)} %copy-done.17, f32[64,128]{1,0:T(8,128)} %pad_maximum_fusion.4.refs_1_), custom_call_target="tpu_custom_call" | custom-call | bytes 35651584 | tf_op jit(solution)/shard_map/gather_blocks_1/pallas_call | solution.py:248
  187.1 190.9 %experts.1 = (bf16[32,128,2048]{2,1,0:T(8,128)(2,1)}, bf16[32,128,2048]{2,1,0:T(8,128)(2,1)}, f32[32,4,128]{2,1,0:T(4,128)}, f32[4,2048,256]{2,1,0:T(8,128)}, f3...) custom-call(bf16[32,128,2048]{2,1,0:T(8,128)(2,1)} %get-tuple-element.88.rows, bf16[32,128,2048]{2,1,0:T(8,128)(2,1)} %bitcast.175, ...), custom_call_target="tpu_custom_call" | custom-call | flops 70866960384 | bytes 104857600 | tf_op jit(solution)/shard_map/experts/pallas_call | solution.py:1010
  379.7 160.0 %scatter_blocks_2.1 = (bf16[128,2048]{1,0:T(8,128)(2,1)}, f32[32,128]{1,0:T(8,128)}, bf16[128,2048]{1,0:T(8,128)(2,1)}) custom-call(bf16[32,128,2048]{2,1,0:T(8,128)(2,1)} %get-tuple-element.90.refs_0_, f32[32,32,128]{2,1,0:T(8,128)} %copy-done.32, bf16[32,128,2048]{2,1,0:T(8,128)(2,1)} %get-tuple-element.92.refs_2_), custom_call_target="tpu_custom_call" | custom-call | bytes 34078720 | tf_op jit(solution)/shard_map/scatter_blocks_2/pallas_call | solution.py:389
  540.6 2.0 multiply_reduce_fusion.5
  544.8 15.7 %narrow_gather_7.1 = bf16[4,128,2048]{2,1,0:T(8,128)(2,1)} custom-call(bf16[128,2048]{1,0:T(8,128)(2,1)} %fusion.56.block), custom_call_target="tpu_custom_call" | custom-call | tf_op jit(solution)/shard_map/narrow_gather_7/pallas_call | solution.py:667
  560.5 3.7 convolution_convert_fusion.5
  569.2 2.0 fusion.14
  572.6 2.6 convolution_convert_fusion
  575.2 2.9 convolution_convert_fusion.1
  578.0 2.1 copy.100
  580.1 2.9 fusion.42
  583.0 3.0 multiply_add_fusion.1
  588.7 4.9 narrow_total_5.1
  594.5 2.8 subtract_convert_fusion
  597.4 2.8 convolution_convert_fusion.3
  600.1 2.8 convolution_convert_fusion.2
  602.9 4.7 fusion.58
  608.0 236.0 %final_sums_3.1 = (bf16[4,2,256,512]{3,2,1,0:T(8,128)(2,1)S(1)}, bf16[4,2,256,512]{3,2,1,0:T(8,128)(2,1)S(1)}, bf16[4,2,256,512]{3,2,1,0:T(8,128)(2,1)}, bf16[4,...) custom-call(bf16[4,2,256,512]{3,2,1,0:T(8,128)(2,1)} %bitcast.157, ...), custom_call_target="tpu_custom_call" | custom-call | bytes 21561344 | tf_op jit(solution)/shard_map/final_sums_3/pallas_call | solution.py:760
  846.2 2.7 bitcast_convert_fusion.3
  848.9 2.7 bitcast_convert_fusion.2
  851.7 2.7 bitcast_convert_fusion.1
  855.0 2.7 bitcast_convert_fusion
  859.0 2.2 copy.89
  861.2 2.8 fusion.21
  (215 shorter events, 40.3 us)
Async XLA Ops:
  7.2 5.7 copy-start.13
  7.2 179.9 %all-gather.3.cloned.1.call-start = ((), (), s32[]{:S(2)}) async-start(), calls=%async_computation | async-start | bytes 17301504 | tf_op jit(solution)/shard_map/all_gather | solution.py:1075
  8.6 4.8 copy-start.36
  16.2 10.5 %copy-start.67 = (bf16[512]{0:T(512)(128)(2,1)S(1)}, bf16[512]{0:T(512)(128)(2,1)}, u32[]{:S(2)}) copy-start(bf16[512]{0:T(512)(128)(2,1)} %param.21) | copy-start | bytes 3076
  16.2 10.6 %copy-start.68 = (bf16[512]{0:T(512)(128)(2,1)S(1)}, bf16[512]{0:T(512)(128)(2,1)}, u32[]{:S(2)}) copy-start(bf16[512]{0:T(512)(128)(2,1)} %param.22) | copy-start | bytes 3076
  19.7 22.8 %copy-start.2 = (f32[512,1536]{1,0:T(8,128)}, f32[512,1536]{1,0:T(8,128)S(1)}, u32[]{:S(2)}) copy-start(f32[512,1536]{1,0:T(8,128)S(1)} %fusion.57) | copy-start | bytes 9437188
  26.8 7.5 copy-start.46
  26.8 7.4 copy-start.48
  27.6 6.7 copy-start.50
  27.6 6.7 copy-start.52
  45.2 21.2 %copy-start.63 = (bf16[2048]{0:T(1024)(128)(2,1)S(1)}, bf16[2048]{0:T(1024)(128)(2,1)}, u32[]{:S(2)}) copy-start(bf16[2048]{0:T(1024)(128)(2,1)} %param.24) | copy-start | bytes 12292
  48.2 21.0 %copy-start.42 = (bf16[2048,32]{0,1:T(8,128)(2,1)S(1)}, bf16[2048,32]{0,1:T(8,128)(2,1)}, u32[]{:S(2)}) copy-start(bf16[2048,32]{0,1:T(8,128)(2,1)} %param.25) | copy-start | bytes 393220
  48.2 21.4 %copy-start.64 = (s32[128,8]{0,1:T(8,128)S(1)}, s32[128,8]{0,1:T(8,128)}, u32[]{:S(2)}) copy-start(s32[128,8]{0,1:T(8,128)} %param.30) | copy-start | bytes 12292
  48.2 138.3 %copy-start.45 = (f32[8,128]{1,0:T(8,128)S(1)}, f32[8,128]{1,0:T(8,128)}, u32[]{:S(2)}) copy-start(f32[8,128]{1,0:T(8,128)} %narrow_total_4.1) | copy-start | bytes 12292
  69.5 117.6 %copy-start.54 = (f32[128]{0:T(128)}, f32[128]{0:T(128)S(1)}, u32[]{:S(2)}) copy-start(f32[128]{0:T(128)S(1)} %get-tuple-element.189) | copy-start | bytes 1540
  69.6 117.5 %copy-start.56 = (f32[128]{0:T(128)}, f32[128]{0:T(128)S(1)}, u32[]{:S(2)}) copy-start(f32[128]{0:T(128)S(1)} %fusion.41) | copy-start | bytes 1540
  379.7 160.1 %copy-start.55 = (f32[128]{0:T(128)S(1)}, f32[128]{0:T(128)}, u32[]{:S(2)}) copy-start(f32[128]{0:T(128)} %copy-done.54) | copy-start | bytes 1540
  379.7 160.1 %copy-start.57 = (f32[128]{0:T(128)S(1)}, f32[128]{0:T(128)}, u32[]{:S(2)}) copy-start(f32[128]{0:T(128)} %copy-done.56) | copy-start | bytes 1540
  379.7 160.9 %copy-start.5 = (f32[128,2048]{1,0:T(8,128)S(1)}, f32[128,2048]{1,0:T(8,128)}, u32[]{:S(2)}) copy-start(f32[128,2048]{1,0:T(8,128)} %copy-done.4) | copy-start | bytes 3145732
  379.7 160.9 %copy-start.43 = (bf16[2048,32]{0,1:T(8,128)(2,1)S(1)}, bf16[2048,32]{0,1:T(8,128)(2,1)}, u32[]{:S(2)}) copy-start(bf16[2048,32]{0,1:T(8,128)(2,1)} %param.25) | copy-start | bytes 393220
  379.7 160.9 %copy-start.62 = (f32[128]{0:T(128)S(1)}, f32[128]{0:T(128)}, u32[]{:S(2)}) copy-start(f32[128]{0:T(128)} %copy-done.61) | copy-start | bytes 1540
  379.7 162.9 %copy-start.70 = (f32[128]{0:T(128)S(1)}, f32[128]{0:T(128)}, u32[]{:S(2)}) copy-start(f32[128]{0:T(128)} %copy-done.69) | copy-start | bytes 1540
  379.7 163.9 %copy-start.22 = (bf16[128,2048]{1,0:T(8,128)(2,1)S(1)}, bf16[128,2048]{1,0:T(8,128)(2,1)}, u32[]{:S(2)}) copy-start(bf16[128,2048]{1,0:T(8,128)(2,1)} %param.31) | copy-start | bytes 1572868
  544.8 19.4 %copy-start.19 = (pred[512,512]{0,1:T(8,128)(4,1)S(1)}, pred[512,512]{0,1:T(8,128)(4,1)}, u32[]{:S(2)}) copy-start(pred[512,512]{0,1:T(8,128)(4,1)} %copy-done.18) | copy-start | bytes 786436
  575.1 5.0 copy-start.44
  575.2 7.8 copy-start.30
  586.0 8.5 copy-start.59
  586.0 8.5 copy-start.60
  597.4 5.5 slice-start
  855.0 6.2 copy-start.6
  855.0 6.2 copy-start.12
  855.0 6.2 copy-start.23
  (45 other events, 115.7 us)
Sparse Core Ops, SparseCore 0:
  10.9 147.3 all-gather.2

commit v4 on v3

--- a/solution.py
+++ b/solution.py
@@ -94,6 +94,17 @@
         return wide * 4 + narrow
 
 
+    def group(self, turn):
+        return (flip(self.z // 2, turn // 4) * 4 + flip(lax.rem(self.z, 2), lax.rem(turn // 2, 2)) * 2
+                + flip(self.x, lax.rem(turn, 2)))
+
+    def stored(self, line, first, second, other_core=0):
+        core = flip(self.core, other_core)
+        turn = (flip(self.z // 2, line // 2) * 4 + flip(lax.rem(self.z, 2), line % 2) * 2
+                + first * (1 - core) + second * core)
+        return turn * 4 + self.device(line, first, second, other_core)[1]
+
+
 def greet(devices_and_conditions):
     barrier = pltpu.get_barrier_semaphore()
     total = 0
@@ -137,130 +148,120 @@
     return ref.at[pl.ds(part * rows, rows)]
 
 
-def gather_kernel(count, *refs):
-    ins, outs, held = refs[:count], refs[count:2 * count], refs[2 * count:3 * count]
-    send, recv, own_in, own_out = refs[3 * count:]
-    at = Place()
-    z = at.z
-    up, down = at.device(z + 1, 0, 0), at.device(z - 1, 0, 0)
-    one, two, twin = at.device(z, 1, 0), at.device(z, 0, 1), at.device(z, 0, 0, 1)
-    greet([(one, None), (two, None), (twin, None), (up, z < LINE - 1), (down, z > 0)])
-    mine = at.block(z, 0, 0)
-    routes = {"up": (0, up), "down": (1, down), "one": (2, one), "two": (3, two), "twin": (4, twin)}
-
-    def copies(block, part, route, own=False):
-        lane, device = routes[route]
+class Gather:
+    def __init__(self, at, ins, outs, held, send, recv, own_sem):
+        self.at, self.ins, self.outs, self.held = at, ins, outs, held
+        self.send, self.recv, self.own_sem = send, recv, own_sem
+        self.count = len(ins)
+        z = at.z
+        up, down = at.device(z + 1, 0, 0), at.device(z - 1, 0, 0)
+        one, two, twin = at.device(z, 1, 0), at.device(z, 0, 1), at.device(z, 0, 0, 1)
+        self.routes = {"up": (0, up), "down": (1, down), "one": (2, one), "two": (3, two), "twin": (4, twin)}
+
+    def greet(self):
+        z = self.at.z
+        conditions = {"up": z < LINE - 1, "down": z > 0}
+        greet([(device, conditions.get(name)) for name, (_, device) in self.routes.items()])
+
+    def copies(self, block, part, route, own=False):
+        lane, device = self.routes[route]
         return [
-            remote(part_of(ins[i] if own else outs[i].at[block], part), part_of(outs[i].at[block], part),
-                   send.at[i, part, lane, block], recv.at[i, part, block], device)
-            for i in range(count)
+            remote(part_of(self.ins[i] if own else self.outs[i].at[block], part), part_of(self.outs[i].at[block], part),
+                   self.send.at[i, part, lane, block], self.recv.at[i, part, block], device)
+            for i in range(self.count)
         ]
 
-    def forward(block, part, *ways, own=False):
+    def forward(self, block, part, *ways, own=False):
         for route in ways:
-            for copy in copies(block, part, route, own):
+            for copy in self.copies(block, part, route, own):
                 copy.start()
 
-    def arrived(block, part):
-        for copy in copies(block, part, "twin"):
+    def arrived(self, block, part):
+        for copy in self.copies(block, part, "twin"):
             copy.wait_recv()
 
-    loads = [pltpu.make_async_copy(ins[i], held[i], own_in.at[i]) for i in range(count)]
-    for load in loads:
-        load.start()
-    for part in range(PARTS):
-        pl.when(z < LINE - 1)(functools.partial(forward, mine, part, "up", own=True))
-        pl.when(z > 0)(functools.partial(forward, mine, part, "down", own=True))
-        forward(mine, part, "one", "two", "twin", own=True)
-    stores = [pltpu.make_async_copy(held[i], outs[i].at[mine], own_out.at[i]) for i in range(count)]
-    for load, store in zip(loads, stores):
-        load.wait()
-        store.start()
-
-    def line_step(step, part):
-        @pl.when(z - step >= 0)
-        def _():
-            block = at.block(z - step, 0, 0)
-            arrived(block, part)
-            pl.when(z < LINE - 1)(functools.partial(forward, block, part, "up"))
-            forward(block, part, "one", "two", "twin")
-
-        @pl.when(z + step < LINE)
-        def _():
-            block = at.block(z + step, 0, 0)
-            arrived(block, part)
-            pl.when(z > 0)(functools.partial(forward, block, part, "down"))
-            forward(block, part, "one", "two", "twin")
-
-    def face_step(step, part, first, second):
-        def take(block):
-            arrived(block, part)
-            if not second:
-                forward(block, part, "two")
-            forward(block, part, "twin")
-        if step == 0:
-            take(at.block(z, first, second))
-        else:
+    def begin(self):
+        z, mine = self.at.z, self.at.block(self.at.z, 0, 0)
+        for part in range(PARTS):
+            pl.when(z < LINE - 1)(functools.partial(self.forward, mine, part, "up", own=True))
+            pl.when(z > 0)(functools.partial(self.forward, mine, part, "down", own=True))
+            self.forward(mine, part, "one", "two", "twin", own=True)
+        for way in (0, 1):
+            moves = [
+                pltpu.make_async_copy(self.ins[i], self.held[i], self.own_sem.at[i]) if way == 0
+                else pltpu.make_async_copy(self.held[i], self.outs[i].at[mine], self.own_sem.at[i])
+                for i in range(self.count)
+            ]
+            for move in moves:
+                move.start()
+            for move in moves:
+                move.wait()
+
+    def line(self, step):
+        z = self.at.z
+        for part in range(PARTS):
             @pl.when(z - step >= 0)
             def _():
-                take(at.block(z - step, first, second))
+                block = self.at.block(z - step, 0, 0)
+                self.arrived(block, part)
+                pl.when(z < LINE - 1)(functools.partial(self.forward, block, part, "up"))
+                self.forward(block, part, "one", "two", "twin")
 
             @pl.when(z + step < LINE)
             def _():
-                take(at.block(z + step, first, second))
-
-    for step in range(LINE + 2):
+                block = self.at.block(z + step, 0, 0)
+                self.arrived(block, part)
+                pl.when(z > 0)(functools.partial(self.forward, block, part, "down"))
+                self.forward(block, part, "one", "two", "twin")
+
+    def face(self, step, first, second):
+        z = self.at.z
+        ways = ("twin",) if second else ("two", "twin")
         for part in range(PARTS):
-            if 1 <= step < LINE:
-                line_step(step, part)
-            if 0 <= step - 1 < LINE:
-                face_step(step - 1, part, 1, 0)
-                face_step(step - 1, part, 0, 1)
-            if 0 <= step - 2 < LINE:
-                face_step(step - 2, part, 1, 1)
-    for first in (0, 1):
-        for second in (0, 1):
-            for line in range(LINE):
-                for part in range(PARTS):
-                    arrived(at.block(line, first, second, 1), part)
-    for store in stores:
-        store.wait()
-
-    def sent(block, part, *ways):
-        for route in ways:
-            for copy in copies(block, part, route):
-                copy.wait_send()
-
-    for line in range(LINE):
-        for part in range(PARTS):
-            block = at.block(line, 0, 0)
-            pl.when((z >= line) & (z < LINE - 1))(functools.partial(sent, block, part, "up"))
-            pl.when((z <= line) & (z > 0))(functools.partial(sent, block, part, "down"))
-            sent(block, part, "one", "two", "twin")
-            sent(at.block(line, 1, 0), part, "two", "twin")
-            sent(at.block(line, 0, 1), part, "twin")
-            sent(at.block(line, 1, 1), part, "twin")
-
-
-def gather_blocks(collective_id, *arrays):
-    count, devices = len(arrays), lax.axis_size("wide") * lax.axis_size("narrow")
-    moved = sum(a.size * a.dtype.itemsize for a in arrays)
-    return pl.pallas_call(
-        functools.partial(gather_kernel, count),
-        name=f"gather_blocks_{collective_id}",
-        out_shape=tuple(jax.ShapeDtypeStruct((devices,) + a.shape, a.dtype) for a in arrays),
-        in_specs=[pl.BlockSpec(memory_space=pl.ANY)] * count,
-        out_specs=tuple(pl.BlockSpec(memory_space=pl.ANY) for _ in arrays),
-        scratch_shapes=[pltpu.VMEM(a.shape, a.dtype) for a in arrays]
-        + [
-            pltpu.SemaphoreType.DMA((count, PARTS, 5, devices)),
-            pltpu.SemaphoreType.DMA((count, PARTS, devices)),
-            pltpu.SemaphoreType.DMA((count,)),
-            pltpu.SemaphoreType.DMA((count,)),
-        ],
-        compiler_params=pltpu.CompilerParams(collective_id=collective_id, has_side_effects=True),
-        cost_estimate=pl.CostEstimate(flops=0, transcendentals=0, bytes_accessed=2 * devices * moved),
-    )(*arrays)
+            def take(line):
+                block = self.at.block(line, first, second)
+                self.arrived(block, part)
+                self.forward(block, part, *ways)
+            if step == 0:
+                take(z)
+            else:
+                pl.when(z - step >= 0)(functools.partial(take, z - step))
+                pl.when(z + step < LINE)(functools.partial(take, z + step))
+
+    def faces(self, step):
+        self.face(step, 1, 0)
+        self.face(step, 0, 1)
+
+    def from_twin(self, group):
+        for y in (0, 1):
+            for part in range(PARTS):
+                self.arrived(group * 4 + y * 2 + 1 - self.at.core, part)
+
+    def end(self):
+        z = self.at.z
+
+        def sent(block, part, *ways):
+            for route in ways:
+                for copy in self.copies(block, part, route):
+                    copy.wait_send()
+
+        for line in range(LINE):
+            for part in range(PARTS):
+                block = self.at.block(line, 0, 0)
+                pl.when((z >= line) & (z < LINE - 1))(functools.partial(sent, block, part, "up"))
+                pl.when((z <= line) & (z > 0))(functools.partial(sent, block, part, "down"))
+                sent(block, part, "one", "two", "twin")
+                sent(self.at.block(line, 1, 0), part, "two", "twin")
+                sent(self.at.block(line, 0, 1), part, "twin")
+                sent(self.at.block(line, 1, 1), part, "twin")
+
+
+PARTS = 2
+
+
+def part_of(ref, part):
+    rows = ref.shape[0] // PARTS
+    return ref.at[pl.ds(part * rows, rows)]
 
 
 ORDER = (3, 0, 2, 1)
@@ -284,7 +285,7 @@
 
     def load(i, part, line, second, first):
         here = slot(line, second, first)
-        return pltpu.make_async_copy(part_of(ins[i].at[at.block(line, first, second)], part),
+        return pltpu.make_async_copy(part_of(ins[i].at[at.stored(line, first, second)], part),
                                      part_of(acc[i].at[here], part), load_sem.at[i, part, here])
 
     def hop(i, part, source, target, lane, device):
@@ -292,7 +293,7 @@
 
     def to_twin(i, part, line, second, first):
         here = slot(line, second, first)
-        return hop(i, part, ins[i].at[at.block(line, first, second, 1)], from_twin[i].at[here], here, twin)
+        return hop(i, part, ins[i].at[at.stored(line, first, second, 1)], from_twin[i].at[here], here, twin)
 
     def to_two(i, part, line, first):
         return hop(i, part, acc[i].at[slot(line, 1, first)], from_two[i].at[first * 4 + line], 16 + first * 4 + line, two)
@@ -782,12 +783,6 @@
     return lax.axis_size("wide") == 8 and lax.axis_size("narrow") == 4
 
 
-def gather_all(*arrays):
-    if own_exchange():
-        return gather_blocks(1, *arrays)
-    return tuple(lax.all_gather(a, BOTH, axis=0) for a in arrays)
-
-
 def scatter_all(*arrays):
     if own_exchange():
         return scatter_blocks(2, *arrays)
@@ -903,7 +898,6 @@
 
 
 STEP_BLOCKS = 4
-COLUMNS = 512
 
 
 def dot(left, right, left_dim=1, right_dim=0):
@@ -913,27 +907,60 @@
 
 
 def experts_kernel(
-    capacity, rows, grads, places, gates, gate_w, up_w, down_w,
-    out, back, gate_grads, gate_dw, up_dw, down_dw, row_slots, grad_slots,
+    capacity, rows_own, grads_own, routes_own, gate_w, up_w, down_w,
+    rows_all, grads_all, routes_all, out, back, gate_grads, gate_dw, up_dw, down_dw,
+    row_slots, grad_slots, rows_held, grads_held, routes_held, load_sem, send, recv, own_sem,
 ):
-    experts, width = gate_w.shape[0], gate_w.shape[1]
-    tokens = rows.shape[1]
+    experts = gate_w.shape[0]
+    tokens = rows_own.shape[0]
+    everywhere = routes_own.shape[0] // 2
+    turn = pl.program_id(0)
+    turns = LINE * 2
+    at = Place()
+    first_expert = lax.axis_index("wide") * experts
+    gathered, held = (rows_all, grads_all, routes_all), (rows_held, grads_held, routes_held)
+    gather = Gather(at, (rows_own, grads_own, routes_own), gathered, [h.at[1, 0] for h in held], send, recv, own_sem)
     slot_ids = lax.broadcasted_iota(jnp.int32, (capacity, tokens), 0).astype(jnp.float32)
 
-    @pl.when(pl.program_id(0) == 0)
+    def loads(number):
+        group = at.group(number)
+        slot = lax.rem(number, 2)
+        return [
+            pltpu.make_async_copy(gathered[i].at[pl.ds(group * STEP_BLOCKS, STEP_BLOCKS)], held[i].at[slot],
+                                  load_sem.at[i, slot])
+            for i in range(3)
+        ]
+
+    def fetch(number):
+        gather.from_twin(at.group(number))
+        for load in loads(number):
+            load.start()
+
+    def on(number, *work):
+        @pl.when(turn == number)
+        def _():
+            for piece, *arguments in work:
+                piece(*arguments)
+
+    @pl.when(turn == 0)
     def _():
+        gather.greet()
+        gather.begin()
         for target in (gate_dw, up_dw, down_dw):
             @pl.loop(0, experts)
             def _(e):
                 target[e] = jnp.zeros(target.shape[1:], jnp.float32)
-
-    def chunks(body):
-        @pl.loop(0, width // COLUMNS)
-        def _(i):
-            body(pl.ds(pl.multiple_of(i * COLUMNS, COLUMNS), COLUMNS))
+        gather.line(1)
+        gather.faces(0)
+        fetch(jnp.int32(0))
+
+    for load in loads(turn):
+        load.wait()
+    slot = lax.rem(turn, 2)
+    rows, grads, routes = rows_held.at[slot], grads_held.at[slot], routes_held.at[slot]
 
     def pick_of(block, expert):
-        return places[block, pl.ds(expert, 1), :] == slot_ids
+        return routes[block, pl.ds(everywhere + first_expert + expert, 1), :] == slot_ids
 
     def picks(block):
         return jnp.concatenate(
@@ -943,20 +970,21 @@
     for block in range(STEP_BLOCKS):
         pick = picks(block)
         part = pl.ds(block * capacity, capacity)
-
-        def spread(columns):
-            for source, target in ((rows, row_slots), (grads, grad_slots)):
-                slots = dot(pick, source[block, :, columns]).astype(jnp.bfloat16)
-                for e in range(experts):
-                    target[e, part, columns] = slots[e * capacity:(e + 1) * capacity]
-        chunks(spread)
+        for source, target in ((rows, row_slots), (grads, grad_slots)):
+            slots = dot(pick, source[block]).astype(jnp.bfloat16)
+            for e in range(experts):
+                target[e, part] = slots[e * capacity:(e + 1) * capacity]
+
+    on(1, (gather.line, 2), (gather.faces, 1))
+    on(2, (gather.line, 3), (gather.faces, 2))
 
     @pl.loop(0, experts)
     def _(e):
         gate_pre, up_pre = dot(row_slots[e], gate_w[e]), dot(row_slots[e], up_w[e])
         raw = dot(grad_slots[e], down_w[e], 1, 1)
         slot_gate = jnp.concatenate([
-            jnp.sum(jnp.where(pick_of(block, e), gates[block, pl.ds(e, 1), :], 0.0), axis=1, keepdims=True)
+            jnp.sum(jnp.where(pick_of(block, e), routes[block, pl.ds(first_expert + e, 1), :], 0.0),
+                    axis=1, keepdims=True)
             for block in range(STEP_BLOCKS)
         ], axis=0)
         sigma = 1.0 / (1.0 + jnp.exp(-gate_pre))
@@ -972,32 +1000,37 @@
         act_grad = raw * slot_gate
         gate_low = (act_grad * up_pre * sigma * (1.0 + gate_pre * (1.0 - sigma))).astype(jnp.bfloat16)
         up_low = (act_grad * silu).astype(jnp.bfloat16)
-
-        def columns_of(columns):
-            down_dw[e, :, columns] += dot(gated, grad_slots[e, :, columns], 0, 0)
-            grad_slots[e, :, columns] = dot(gated, down_w[e, :, columns]).astype(jnp.bfloat16)
-            turned = row_slots[e, :, columns].T
-            gate_dw[e, columns, :] += dot(turned, gate_low)
-            up_dw[e, columns, :] += dot(turned, up_low)
-            row_slots[e, :, columns] = (
-                dot(gate_low, gate_w[e, columns, :], 1, 1) + dot(up_low, up_w[e, columns, :], 1, 1)
-            ).astype(jnp.bfloat16)
-        chunks(columns_of)
+        down_dw[e] += dot(gated, grad_slots[e], 0, 0)
+        grad_slots[e] = dot(gated, down_w[e]).astype(jnp.bfloat16)
+        turned = row_slots[e].T
+        gate_dw[e] += dot(turned, gate_low)
+        up_dw[e] += dot(turned, up_low)
+        row_slots[e] = (dot(gate_low, gate_w[e], 1, 1) + dot(up_low, up_w[e], 1, 1)).astype(jnp.bfloat16)
+
+    on(0, (gather.face, 0, 1, 1))
+    on(2, (gather.face, 1, 1, 1))
+    on(3, (gather.faces, 3))
+    on(4, (gather.face, 2, 1, 1))
+    on(6, (gather.face, 3, 1, 1))
+
+    @pl.when(turn < turns - 1)
+    def _():
+        fetch(turn + 1)
 
     for block in range(STEP_BLOCKS):
         pick = picks(block)
         part = pl.ds(block * capacity, capacity)
-
-        def collect(columns):
-            for source, target in ((row_slots, back), (grad_slots, out)):
-                slots = jnp.concatenate([source[e, part, columns] for e in range(experts)], axis=0)
-                target[block, :, columns] = dot(pick, slots, 0, 0).astype(jnp.bfloat16)
-        chunks(collect)
-
-
-def experts_fused(rows_all, grads_all, places_here, probs_here, gate_weight, up_weight, down_weight, capacity):
-    block_count, own_rows, width = rows_all.shape
+        for source, target in ((row_slots, back), (grad_slots, out)):
+            slots = jnp.concatenate([source[e, part] for e in range(experts)], axis=0)
+            target[block] = dot(pick, slots, 0, 0).astype(jnp.bfloat16)
+
+    on(turns - 1, (gather.end,))
+
+
+def gather_experts(collective_id, rows, grads, routes, gate_weight, up_weight, down_weight, capacity):
+    own_rows, width = rows.shape
     experts, _, hidden = gate_weight.shape
+    block_count = LINE * 2 * STEP_BLOCKS
     step_rows = STEP_BLOCKS * capacity
 
     def stepped(*shape):
@@ -1005,32 +1038,40 @@
 
     def whole(array):
         return pl.BlockSpec(array.shape, lambda i: (0,) * array.ndim, pipeline_mode=pl.Buffered(1))
-    weights = (gate_weight, up_weight, down_weight)
+    weights, owns = (gate_weight, up_weight, down_weight), (rows, grads, routes)
     flops = 2 * block_count * experts * (9 * capacity * width * hidden + 4 * capacity * own_rows * width)
-    return pl.pallas_call(
+    shapes = jax.ShapeDtypeStruct
+    results = pl.pallas_call(
         functools.partial(experts_kernel, capacity),
-        name="experts",
+        name="gather_experts",
         grid=(block_count // STEP_BLOCKS,),
-        out_shape=(
-            jax.ShapeDtypeStruct(rows_all.shape, jnp.bfloat16),
-            jax.ShapeDtypeStruct(rows_all.shape, jnp.bfloat16),
-            jax.ShapeDtypeStruct((block_count, experts, own_rows), jnp.float32),
-        ) + tuple(jax.ShapeDtypeStruct(w.shape, jnp.float32) for w in weights),
-        in_specs=[
-            stepped(own_rows, width), stepped(own_rows, width), stepped(experts, own_rows), stepped(experts, own_rows),
-        ] + [whole(w) for w in weights],
-        out_specs=(stepped(own_rows, width), stepped(own_rows, width), stepped(experts, own_rows))
+        out_shape=tuple(shapes((block_count,) + a.shape, a.dtype) for a in owns)
+        + (
+            shapes((block_count, own_rows, width), jnp.bfloat16),
+            shapes((block_count, own_rows, width), jnp.bfloat16),
+            shapes((block_count, experts, own_rows), jnp.float32),
+        ) + tuple(shapes(w.shape, jnp.float32) for w in weights),
+        in_specs=[pl.BlockSpec(memory_space=pl.ANY)] * 3 + [whole(w) for w in weights],
+        out_specs=(pl.BlockSpec(memory_space=pl.ANY),) * 3
+        + (stepped(own_rows, width), stepped(own_rows, width), stepped(experts, own_rows))
         + tuple(whole(w) for w in weights),
         scratch_shapes=[
             pltpu.VMEM((experts, step_rows, width), jnp.bfloat16),
             pltpu.VMEM((experts, step_rows, width), jnp.bfloat16),
+        ] + [pltpu.VMEM((2, STEP_BLOCKS) + a.shape, a.dtype) for a in owns] + [
+            pltpu.SemaphoreType.DMA((3, 2)),
+            pltpu.SemaphoreType.DMA((3, PARTS, 5, block_count)),
+            pltpu.SemaphoreType.DMA((3, PARTS, block_count)),
+            pltpu.SemaphoreType.DMA((3,)),
         ],
         compiler_params=pltpu.CompilerParams(
+            collective_id=collective_id, has_side_effects=True,
             dimension_semantics=("arbitrary",), vmem_limit_bytes=67_000_000),
         cost_estimate=pl.CostEstimate(
             flops=flops, transcendentals=0,
-            bytes_accessed=4 * 2 * rows_all.size + sum(6 * w.size for w in weights)),
-    )(rows_all, grads_all, places_here, probs_here, *weights)
+            bytes_accessed=8 * block_count * rows.size + sum(6 * w.size for w in weights)),
+    )(*owns, *weights)
+    return results[3:]
 
 
 def local(
@@ -1072,7 +1113,6 @@
         chosen.astype(jnp.bfloat16),
         preferred_element_type=jnp.float32,
     )
-    grads_all = lax.all_gather(out_cotangent, BOTH, axis=0)
     inputs_all = block_input.astype(jnp.float32)
     normed_one = rms_scale(inputs_all, attn_gain.astype(jnp.float32)).astype(jnp.bfloat16)
     joined_weight = jnp.concatenate([query_weight, key_weight, value_weight], axis=1)
@@ -1138,16 +1178,17 @@
     normed_two = normed_two_full.astype(jnp.bfloat16)
     logits = jnp.dot(normed_two, router_weight, preferred_element_type=jnp.float32)
     route_probs = jax.nn.softmax(logits, axis=-1)
-    rows_all, routes_all = gather_all(
-        normed_two, jnp.concatenate([route_probs.T, jnp.where(chosen, earlier, -1.0).T], axis=0)
-    )
+    routes = jnp.concatenate([route_probs.T, jnp.where(chosen, earlier, -1.0).T], axis=0)
     expert_begin = lax.axis_index("wide") * experts_here
-    probs_here = lax.dynamic_slice_in_dim(routes_all, expert_begin, experts_here, 1)
-    places_here = lax.dynamic_slice_in_dim(routes_all, experts_all + expert_begin, experts_here, 1)
-    experts = experts_fused if own_exchange() and capacity % 16 == 0 else experts_plain
-    out_parts, back_parts, gate_grad_parts, gate_weight_grad, up_weight_grad, down_weight_grad = experts(
-        rows_all, grads_all, places_here, probs_here, gate_weight, up_weight, down_weight, capacity
-    )
+    expert_weights = (gate_weight, up_weight, down_weight)
+    if own_exchange():
+        results = gather_experts(1, normed_two, out_cotangent, routes, *expert_weights, capacity)
+    else:
+        rows_all, grads_all, routes_all = (lax.all_gather(a, BOTH, axis=0) for a in (normed_two, out_cotangent, routes))
+        probs_here = lax.dynamic_slice_in_dim(routes_all, expert_begin, experts_here, 1)
+        places_here = lax.dynamic_slice_in_dim(routes_all, experts_all + expert_begin, experts_here, 1)
+        results = experts_plain(rows_all, grads_all, places_here, probs_here, *expert_weights, capacity)
+    out_parts, back_parts, gate_grad_parts, gate_weight_grad, up_weight_grad, down_weight_grad = results
     gate_grad_wide = lax.dynamic_update_slice_in_dim(
         jnp.zeros((block_count, experts_all, own_rows), jnp.float32), gate_grad_parts, expert_begin, 1
     )

time: 881 us -> 817 us (0.927)
  Pallas kernels: 746 us -> 687 us
  local copies, waits for them, and re-layouts: 29.1 us -> 47.2 us
  between operations: 15.5 us -> 2.27 us
    pallas_call x2 -> x1, Pallas kernels: 305 us -> 240 us  [gather_experts(): pl.pallas_call(functools.partial(experts_kernel, capacity), name='gather_...]
    unnamed x155 -> x174, local copies, waits for them, and re-layouts: 11.5 us -> 32.2 us
  transfers between devices with their start and end apart: 1 -> 0, of which waited for: 0 -> 0; matrix products, arithmetic and copies ran while one was open for 4% -> 0% of each run, Pallas kernels for 16% -> 0%
where the time goes in v4:
time: 817 us; the launch traced here: 808 us
  Pallas kernels  687 us (84%)
  local copies, waits for them, and re-layouts  47.2 us (6%)
  matrix products  38.2 us (5%)
  other arithmetic  32.6 us (4%)
    pallas_call x1, Pallas kernels, gather_experts(): pl.pallas_call(functools.partial(experts_kernel, capacity), name='gather_...  240 us
    pallas_call x1, Pallas kernels, final_sums(): pl.pallas_call(functools.partial(final_sums_kernel, plan, count), name=f'...  237 us
    pallas_call x1, Pallas kernels, scatter_blocks(): pl.pallas_call(functools.partial(scatter_kernel, count), name=f'scatter_b...  165 us
    unnamed x174, local copies, waits for them, and re-layouts  32.2 us
    pallas_call x1, Pallas kernels, narrow_sum(): pl.pallas_call(narrow_sum_kernel, name=f'narrow_sum_{collective_id}', out...  17.7 us

profile of v4, /device:TPU:0, one launch (start us, length us, event | category | flops | bytes accessed | tf_op | source)
XLA Modules:
  0.0 807.5 jit_solution(1644128750020214075)
XLA Ops:
  0.7 1.9 constant_dynamic-update-slice_fusion.2
  6.2 3.5 fusion.57
  10.8 5.9 narrow_total_4.1
  17.8 1.6 multiply_multiply_fusion
  19.4 2.5 reshape.356
  21.9 2.5 reshape.355
  24.5 3.6 fusion.59
  34.9 2.6 convolution_convert_fusion.4
  37.5 17.7 %narrow_sum_6.1 = bf16[128,2048]{1,0:T(8,128)(2,1)} custom-call(bf16[4,128,2048]{2,1,0:T(8,128)(2,1)} %bitcast.155), custom_call_target="tpu_custom_call" | custom-call | tf_op jit(solution)/shard_map/narrow_sum_6/pallas_call | solution.py:632
  55.3 2.5 convert_element_type.126
  63.2 240.2 %gather_experts.1 = (bf16[32,128,2048]{2,1,0:T(8,128)(2,1)}, bf16[32,128,2048]{2,1,0:T(8,128)(2,1)}, f32[32,64,128]{2,1,0:T(8,128)}, bf16[32,128,2048]{2,1,0:T(8...) custom-call(bf16[128,2048]{1,0:T(8,128)(2,1)} %copy-done.23, ...), custom_call_target="tpu_custom_call" | custom-call | flops 70866960384 | bytes 104857600 | tf_op jit(solution)/shard_map/gather_experts/pallas_call | solution.py:1044
  305.2 165.5 %scatter_blocks_2.1 = (bf16[128,2048]{1,0:T(8,128)(2,1)}, f32[32,128]{1,0:T(8,128)}, bf16[128,2048]{1,0:T(8,128)(2,1)}) custom-call(bf16[32,128,2048]{2,1,0:T(8,128)(2,1)} %get-tuple-element.86.refs_0_, f32[32,32,128]{2,1,0:T(8,128)} %copy-done.33, bf16[32,128,2048]{2,1,0:T(8,128)(2,1)} %get-tuple-element.88.refs_2_), custom_call_target="tpu_custom_call" | custom-call | bytes 34078720 | tf_op jit(solution)/shard_map/scatter_blocks_2/pallas_call | solution.py:390
  471.4 2.0 multiply_reduce_fusion.5
  475.6 15.8 %narrow_gather_7.1 = bf16[4,128,2048]{2,1,0:T(8,128)(2,1)} custom-call(bf16[128,2048]{1,0:T(8,128)(2,1)} %fusion.56.block), custom_call_target="tpu_custom_call" | custom-call | tf_op jit(solution)/shard_map/narrow_gather_7/pallas_call | solution.py:668
  491.5 3.7 convolution_convert_fusion.5
  504.0 4.9 narrow_total_5.1
  509.9 3.0 subtract_convert_fusion
  512.9 2.7 convolution_convert_fusion.3
  515.7 2.7 convolution_convert_fusion.2
  519.7 2.9 convolution_convert_fusion.1
  522.6 2.6 convolution_convert_fusion
  525.2 2.1 copy.100
  527.3 7.8 fusion.58
  536.1 237.3 %final_sums_3.1 = (bf16[4,2,256,512]{3,2,1,0:T(8,128)(2,1)S(1)}, bf16[4,2,256,512]{3,2,1,0:T(8,128)(2,1)S(1)}, bf16[4,2,256,512]{3,2,1,0:T(8,128)(2,1)}, bf16[4,...) custom-call(bf16[4,2,256,512]{3,2,1,0:T(8,128)(2,1)} %bitcast.156, ...), custom_call_target="tpu_custom_call" | custom-call | bytes 21561344 | tf_op jit(solution)/shard_map/final_sums_3/pallas_call | solution.py:761
  773.8 1.5 fusion.21
  775.9 2.7 bitcast_convert_fusion.3
  778.6 2.7 bitcast_convert_fusion.2
  781.4 2.7 bitcast_convert_fusion.1
  784.7 2.7 bitcast_convert_fusion
  788.7 7.5 copy.139
  796.2 7.5 copy.140
  803.7 3.4 copy.141
  (229 shorter events, 36.9 us)
Async XLA Ops:
  3.7 6.0 copy-start.42
  6.2 11.3 %copy-start.75 = (bf16[512]{0:T(512)(128)(2,1)S(1)}, bf16[512]{0:T(512)(128)(2,1)}, u32[]{:S(2)}) copy-start(bf16[512]{0:T(512)(128)(2,1)} %param.21) | copy-start | bytes 3076
  6.2 11.3 %copy-start.76 = (bf16[512]{0:T(512)(128)(2,1)S(1)}, bf16[512]{0:T(512)(128)(2,1)}, u32[]{:S(2)}) copy-start(bf16[512]{0:T(512)(128)(2,1)} %param.22) | copy-start | bytes 3076
  6.2 11.3 %copy-start.67 = (s32[512]{0:T(512)S(1)}, s32[512]{0:T(512)}, u32[]{:S(2)}) copy-start(s32[512]{0:T(512)} %param.29) | copy-start | bytes 6148
  9.7 23.0 %copy-start.3 = (f32[512,1536]{1,0:T(8,128)}, f32[512,1536]{1,0:T(8,128)S(1)}, u32[]{:S(2)}) copy-start(f32[512,1536]{1,0:T(8,128)S(1)} %fusion.57) | copy-start | bytes 9437188
  17.5 7.0 copy-start.55
  17.5 7.0 copy-start.57
  17.5 7.0 copy-start.59
  17.5 6.9 copy-start.61
  17.8 14.9 %copy-start.19 = (pred[512,512]{0,1:T(8,128)(4,1)}, pred[512,512]{0,1:T(8,128)(4,1)S(1)}, u32[]{:S(2)}) copy-start(pred[512,512]{0,1:T(8,128)(4,1)S(1)} %fusion.27) | copy-start | bytes 786436
  34.9 20.4 %copy-start.16 = (bf16[512,2048]{1,0:T(8,128)(2,1)S(1)}, bf16[512,2048]{1,0:T(8,128)(2,1)}, u32[]{:S(2)}) copy-start(bf16[512,2048]{1,0:T(8,128)(2,1)} %param.16) | copy-start | bytes 6291460
  55.3 5.2 copy-start.72
  55.3 6.0 copy-start.51
  305.1 165.5 %copy-start.64 = (f32[128]{0:T(128)S(1)}, f32[128]{0:T(128)}, u32[]{:S(2)}) copy-start(f32[128]{0:T(128)} %copy-done.63) | copy-start | bytes 1540
  305.1 165.5 %copy-start.66 = (f32[128]{0:T(128)S(1)}, f32[128]{0:T(128)}, u32[]{:S(2)}) copy-start(f32[128]{0:T(128)} %copy-done.65) | copy-start | bytes 1540
  305.1 166.3 %copy-start.6 = (f32[128,2048]{1,0:T(8,128)S(1)}, f32[128,2048]{1,0:T(8,128)}, u32[]{:S(2)}) copy-start(f32[128,2048]{1,0:T(8,128)} %copy-done.5) | copy-start | bytes 3145732
  305.1 166.3 %copy-start.52 = (bf16[2048,32]{0,1:T(8,128)(2,1)S(1)}, bf16[2048,32]{0,1:T(8,128)(2,1)}, u32[]{:S(2)}) copy-start(bf16[2048,32]{0,1:T(8,128)(2,1)} %param.25) | copy-start | bytes 393220
  305.1 166.3 %copy-start.69 = (f32[128]{0:T(128)S(1)}, f32[128]{0:T(128)}, u32[]{:S(2)}) copy-start(f32[128]{0:T(128)} %copy-done.68) | copy-start | bytes 1540
  305.1 168.3 %copy-start.78 = (f32[128]{0:T(128)S(1)}, f32[128]{0:T(128)}, u32[]{:S(2)}) copy-start(f32[128]{0:T(128)} %copy-done.77) | copy-start | bytes 1540
  305.1 169.3 %copy-start.40 = (bf16[128,2048]{1,0:T(8,128)(2,1)S(1)}, bf16[128,2048]{1,0:T(8,128)(2,1)}, u32[]{:S(2)}) copy-start(bf16[128,2048]{1,0:T(8,128)(2,1)} %grads_own.1) | copy-start | bytes 1572868
  475.6 19.5 %copy-start.20 = (pred[512,512]{0,1:T(8,128)(4,1)S(1)}, pred[512,512]{0,1:T(8,128)(4,1)}, u32[]{:S(2)}) copy-start(pred[512,512]{0,1:T(8,128)(4,1)} %copy-done.19) | copy-start | bytes 786436
  501.4 8.5 %copy-start.54 = (f32[8,128]{1,0:T(8,128)S(1)}, f32[8,128]{1,0:T(8,128)}, u32[]{:S(2)}) copy-start(f32[8,128]{1,0:T(8,128)} %narrow_total_4.1) | copy-start | bytes 12292
  503.4 9.5 %copy-start.74 = (f32[512]{0:T(512)S(1)}, f32[512]{0:T(512)}, u32[]{:S(2)}) copy-start(f32[512]{0:T(512)} %copy-done.73) | copy-start | bytes 6148
  527.2 7.8 copy-start.24
  527.2 7.8 copy-start.53
  536.0 237.4 %copy-start.8 = (f32[512,2048]{1,0:T(8,128)S(1)}, f32[512,2048]{1,0:T(8,128)}, u32[]{:S(2)}) copy-start(f32[512,2048]{1,0:T(8,128)} %convert_element_type.126) | copy-start | bytes 12582916
  536.0 237.7 %copy-start.7 = (f32[128,2048]{1,0:T(8,128)S(1)}, f32[128,2048]{1,0:T(8,128)}, u32[]{:S(2)}) copy-start(f32[128,2048]{1,0:T(8,128)} %copy-done.5) | copy-start | bytes 3145732
  536.1 237.7 %copy-start.14 = (f32[128,2048]{1,0:T(8,128)S(1)}, f32[128,2048]{1,0:T(8,128)}, u32[]{:S(2)}) copy-start(f32[128,2048]{1,0:T(8,128)} %copy-done.13) | copy-start | bytes 3145732
  536.1 237.7 %copy-start.41 = (bf16[128,2048]{1,0:T(8,128)(2,1)S(1)}, bf16[128,2048]{1,0:T(8,128)(2,1)}, u32[]{:S(2)}) copy-start(bf16[128,2048]{1,0:T(8,128)(2,1)} %grads_own.1) | copy-start | bytes 1572868
  536.1 237.7 %copy-start.50 = (bf16[128,2048]{1,0:T(8,128)(2,1)S(1)}, bf16[128,2048]{1,0:T(8,128)(2,1)}, u32[]{:S(2)}) copy-start(bf16[128,2048]{1,0:T(8,128)(2,1)} %get-tuple-element.89) | copy-start | bytes 1572868
  788.7 15.0 %slice-start = ((s8[8388608]{0:T(1024)(128)(4,1)}), s8[4194304]{0:T(1024)(128)(4,1)S(1)}, s32[]{:S(2)}) async-start(s8[8388608]{0:T(1024)(128)(4,1)} %bitcast.151), calls=%async_computation | async-start | bytes 8388608
  796.2 7.5 slice-start.1
  (52 other events, 115.0 us)

commit v5 on v4

--- a/solution.py
+++ b/solution.py
@@ -197,40 +197,45 @@
             for move in moves:
                 move.wait()
 
-    def line(self, step):
+    def line(self, step, part):
         z = self.at.z
-        for part in range(PARTS):
-            @pl.when(z - step >= 0)
-            def _():
-                block = self.at.block(z - step, 0, 0)
-                self.arrived(block, part)
-                pl.when(z < LINE - 1)(functools.partial(self.forward, block, part, "up"))
-                self.forward(block, part, "one", "two", "twin")
-
-            @pl.when(z + step < LINE)
-            def _():
-                block = self.at.block(z + step, 0, 0)
-                self.arrived(block, part)
-                pl.when(z > 0)(functools.partial(self.forward, block, part, "down"))
-                self.forward(block, part, "one", "two", "twin")
-
-    def face(self, step, first, second):
+
+        @pl.when(z - step >= 0)
+        def _():
+            block = self.at.block(z - step, 0, 0)
+            self.arrived(block, part)
+            pl.when(z < LINE - 1)(functools.partial(self.forward, block, part, "up"))
+            self.forward(block, part, "one", "two", "twin")
+
+        @pl.when(z + step < LINE)
+        def _():
+            block = self.at.block(z + step, 0, 0)
+            self.arrived(block, part)
+            pl.when(z > 0)(functools.partial(self.forward, block, part, "down"))
+            self.forward(block, part, "one", "two", "twin")
+
+    def face(self, step, part, first, second):
         z = self.at.z
         ways = ("twin",) if second else ("two", "twin")
-        for part in range(PARTS):
-            def take(line):
-                block = self.at.block(line, first, second)
-                self.arrived(block, part)
-                self.forward(block, part, *ways)
-            if step == 0:
-                take(z)
-            else:
-                pl.when(z - step >= 0)(functools.partial(take, z - step))
-                pl.when(z + step < LINE)(functools.partial(take, z + step))
-
-    def faces(self, step):
-        self.face(step, 1, 0)
-        self.face(step, 0, 1)
+
+        def take(line):
+            block = self.at.block(line, first, second)
+            self.arrived(block, part)
+            self.forward(block, part, *ways)
+        if step == 0:
+            take(z)
+        else:
+            pl.when(z - step >= 0)(functools.partial(take, z - step))
+            pl.when(z + step < LINE)(functools.partial(take, z + step))
+
+    def piece(self, kind, step, part):
+        if kind == "line":
+            self.line(step, part)
+        elif kind == "faces":
+            self.face(step, part, 1, 0)
+            self.face(step, part, 0, 1)
+        else:
+            self.face(step, part, 1, 1)
 
     def from_twin(self, group):
         for y in (0, 1):
@@ -898,6 +903,30 @@
 
 
 STEP_BLOCKS = 4
+GATHER_PLAN = (
+    (-1, 1, "faces", 0, 0),
+    (-1, 1, "faces", 0, 1),
+    (-1, 1, "line", 1, 1),
+    (-1, 1, "line", 1, 0),
+    (0, 0, "corner", 0, 0),
+    (0, 0, "corner", 0, 1),
+    (1, 1, "faces", 1, 0),
+    (1, 1, "faces", 1, 1),
+    (2, 1, "corner", 1, 0),
+    (2, 3, "line", 2, 0),
+    (2, 3, "line", 2, 1),
+    (2, 3, "corner", 1, 1),
+    (3, 4, "faces", 2, 0),
+    (3, 4, "faces", 2, 1),
+    (4, 0, "corner", 2, 0),
+    (4, 2, "corner", 2, 1),
+    (4, 3, "line", 3, 0),
+    (4, 4, "line", 3, 1),
+    (5, 0, "faces", 3, 0),
+    (5, 0, "faces", 3, 1),
+    (6, 1, "corner", 3, 0),
+    (6, 1, "corner", 3, 1),
+)
 
 
 def dot(left, right, left_dim=1, right_dim=0):
@@ -936,11 +965,14 @@
         for load in loads(number):
             load.start()
 
-    def on(number, *work):
-        @pl.when(turn == number)
-        def _():
-            for piece, *arguments in work:
-                piece(*arguments)
+    def issue(place, expert=None):
+        for number in sorted({entry[0] for entry in GATHER_PLAN}):
+            work = [entry[2:] for entry in GATHER_PLAN if entry[:2] == (number, place)]
+            if work:
+                @pl.when(turn == number if expert is None else (turn == number) & (expert == place - 1))
+                def _():
+                    for piece in work:
+                        gather.piece(*piece)
 
     @pl.when(turn == 0)
     def _():
@@ -950,8 +982,9 @@
             @pl.loop(0, experts)
             def _(e):
                 target[e] = jnp.zeros(target.shape[1:], jnp.float32)
-        gather.line(1)
-        gather.faces(0)
+        for entry in GATHER_PLAN:
+            if entry[0] < 0:
+                gather.piece(*entry[2:])
         fetch(jnp.int32(0))
 
     for load in loads(turn):
@@ -975,8 +1008,7 @@
             for e in range(experts):
                 target[e, part] = slots[e * capacity:(e + 1) * capacity]
 
-    on(1, (gather.line, 2), (gather.faces, 1))
-    on(2, (gather.line, 3), (gather.faces, 2))
+    issue(0)
 
     @pl.loop(0, experts)
     def _(e):
@@ -1006,12 +1038,8 @@
         gate_dw[e] += dot(turned, gate_low)
         up_dw[e] += dot(turned, up_low)
         row_slots[e] = (dot(gate_low, gate_w[e], 1, 1) + dot(up_low, up_w[e], 1, 1)).astype(jnp.bfloat16)
-
-    on(0, (gather.face, 0, 1, 1))
-    on(2, (gather.face, 1, 1, 1))
-    on(3, (gather.faces, 3))
-    on(4, (gather.face, 2, 1, 1))
-    on(6, (gather.face, 3, 1, 1))
+        for place in range(1, 5):
+            issue(place, e)
 
     @pl.when(turn < turns - 1)
     def _():
@@ -1024,7 +1052,8 @@
             slots = jnp.concatenate([source[e, part] for e in range(experts)], axis=0)
             target[block] = dot(pick, slots, 0, 0).astype(jnp.bfloat16)
 
-    on(turns - 1, (gather.end,))
+    issue(5)
+    pl.when(turn == turns - 1)(gather.end)
 
 
 def gather_experts(collective_id, rows, grads, routes, gate_weight, up_weight, down_weight, capacity):

time: 817 us -> 792 us (0.969)
  Pallas kernels: 687 us -> 663 us
    pallas_call x1, Pallas kernels: 240 us -> 220 us  [gather_experts(): pl.pallas_call(functools.partial(experts_kernel, capacity), name='gather_...]
where the time goes in v5:
time: 792 us; the launch traced here: 783 us
  Pallas kernels  663 us (84%)
  local copies, waits for them, and re-layouts  47.2 us (6%)
  matrix products  38.2 us (5%)
  other arithmetic  32.6 us (4%)
    pallas_call x1, Pallas kernels, final_sums(): pl.pallas_call(functools.partial(final_sums_kernel, plan, count), name=f'...  235 us
    pallas_call x1, Pallas kernels, gather_experts(): pl.pallas_call(functools.partial(experts_kernel, capacity), name='gather_...  220 us
    pallas_call x1, Pallas kernels, scatter_blocks(): pl.pallas_call(functools.partial(scatter_kernel, count), name=f'scatter_b...  164 us
    unnamed x174, local copies, waits for them, and re-layouts  32.2 us
    pallas_call x1, Pallas kernels, narrow_sum(): pl.pallas_call(narrow_sum_kernel, name=f'narrow_sum_{collective_id}', out...  17.7 us

profile of v5, /device:TPU:0, one launch (start us, length us, event | category | flops | bytes accessed | tf_op | source)
XLA Modules:
  0.0 782.8 jit_solution(6768458724462963718)
XLA Ops:
  0.7 1.9 constant_dynamic-update-slice_fusion.2
  6.2 3.5 fusion.57
  10.8 5.9 narrow_total_4.1
  17.8 1.6 multiply_multiply_fusion
  19.4 2.5 reshape.356
  21.9 2.5 reshape.355
  24.5 3.6 fusion.59
  34.9 2.6 convolution_convert_fusion.4
  37.5 17.7 %narrow_sum_6.1 = bf16[128,2048]{1,0:T(8,128)(2,1)} custom-call(bf16[4,128,2048]{2,1,0:T(8,128)(2,1)} %bitcast.155), custom_call_target="tpu_custom_call" | custom-call | tf_op jit(solution)/shard_map/narrow_sum_6/pallas_call | solution.py:637
  55.3 2.5 convert_element_type.126
  63.2 220.1 %gather_experts.1 = (bf16[32,128,2048]{2,1,0:T(8,128)(2,1)}, bf16[32,128,2048]{2,1,0:T(8,128)(2,1)}, f32[32,64,128]{2,1,0:T(8,128)}, bf16[32,128,2048]{2,1,0:T(8...) custom-call(bf16[128,2048]{1,0:T(8,128)(2,1)} %copy-done.23, ...), custom_call_target="tpu_custom_call" | custom-call | flops 70866960384 | bytes 104857600 | tf_op jit(solution)/shard_map/gather_experts/pallas_call | solution.py:1073
  285.1 163.5 %scatter_blocks_2.1 = (bf16[128,2048]{1,0:T(8,128)(2,1)}, f32[32,128]{1,0:T(8,128)}, bf16[128,2048]{1,0:T(8,128)(2,1)}) custom-call(bf16[32,128,2048]{2,1,0:T(8,128)(2,1)} %get-tuple-element.86.refs_0_, f32[32,32,128]{2,1,0:T(8,128)} %copy-done.33, bf16[32,128,2048]{2,1,0:T(8,128)(2,1)} %get-tuple-element.88.refs_2_), custom_call_target="tpu_custom_call" | custom-call | bytes 34078720 | tf_op jit(solution)/shard_map/scatter_blocks_2/pallas_call | solution.py:395
  449.4 2.0 multiply_reduce_fusion.5
  453.7 15.5 %narrow_gather_7.1 = bf16[4,128,2048]{2,1,0:T(8,128)(2,1)} custom-call(bf16[128,2048]{1,0:T(8,128)(2,1)} %fusion.56.block), custom_call_target="tpu_custom_call" | custom-call | tf_op jit(solution)/shard_map/narrow_gather_7/pallas_call | solution.py:673
  469.2 3.7 convolution_convert_fusion.5
  481.7 4.9 narrow_total_5.1
  487.6 3.0 subtract_convert_fusion
  490.6 2.7 convolution_convert_fusion.3
  493.4 2.7 convolution_convert_fusion.2
  497.4 2.9 convolution_convert_fusion.1
  500.3 2.6 convolution_convert_fusion
  502.9 2.1 copy.100
  505.0 7.8 fusion.58
  513.8 234.9 %final_sums_3.1 = (bf16[4,2,256,512]{3,2,1,0:T(8,128)(2,1)S(1)}, bf16[4,2,256,512]{3,2,1,0:T(8,128)(2,1)S(1)}, bf16[4,2,256,512]{3,2,1,0:T(8,128)(2,1)}, bf16[4,...) custom-call(bf16[4,2,256,512]{3,2,1,0:T(8,128)(2,1)} %bitcast.156, ...), custom_call_target="tpu_custom_call" | custom-call | bytes 21561344 | tf_op jit(solution)/shard_map/final_sums_3/pallas_call | solution.py:766
  749.1 1.5 fusion.21
  751.2 2.7 bitcast_convert_fusion.3
  753.9 2.7 bitcast_convert_fusion.2
  756.7 2.7 bitcast_convert_fusion.1
  760.0 2.7 bitcast_convert_fusion
  764.0 7.5 copy.139
  771.5 7.5 copy.140
  779.0 3.4 copy.141
  (229 shorter events, 36.9 us)
Async XLA Ops:
  3.7 6.0 copy-start.42
  6.2 11.3 %copy-start.75 = (bf16[512]{0:T(512)(128)(2,1)S(1)}, bf16[512]{0:T(512)(128)(2,1)}, u32[]{:S(2)}) copy-start(bf16[512]{0:T(512)(128)(2,1)} %param.21) | copy-start | bytes 3076
  6.2 11.3 %copy-start.76 = (bf16[512]{0:T(512)(128)(2,1)S(1)}, bf16[512]{0:T(512)(128)(2,1)}, u32[]{:S(2)}) copy-start(bf16[512]{0:T(512)(128)(2,1)} %param.22) | copy-start | bytes 3076
  6.2 11.3 %copy-start.67 = (s32[512]{0:T(512)S(1)}, s32[512]{0:T(512)}, u32[]{:S(2)}) copy-start(s32[512]{0:T(512)} %param.29) | copy-start | bytes 6148
  9.7 23.0 %copy-start.3 = (f32[512,1536]{1,0:T(8,128)}, f32[512,1536]{1,0:T(8,128)S(1)}, u32[]{:S(2)}) copy-start(f32[512,1536]{1,0:T(8,128)S(1)} %fusion.57) | copy-start | bytes 9437188
  17.5 7.0 copy-start.55
  17.5 7.0 copy-start.57
  17.5 7.0 copy-start.59
  17.5 6.9 copy-start.61
  17.8 14.9 %copy-start.19 = (pred[512,512]{0,1:T(8,128)(4,1)}, pred[512,512]{0,1:T(8,128)(4,1)S(1)}, u32[]{:S(2)}) copy-start(pred[512,512]{0,1:T(8,128)(4,1)S(1)} %fusion.27) | copy-start | bytes 786436
  34.9 20.4 %copy-start.16 = (bf16[512,2048]{1,0:T(8,128)(2,1)S(1)}, bf16[512,2048]{1,0:T(8,128)(2,1)}, u32[]{:S(2)}) copy-start(bf16[512,2048]{1,0:T(8,128)(2,1)} %param.16) | copy-start | bytes 6291460
  55.3 5.2 copy-start.72
  55.3 6.0 copy-start.51
  285.1 163.6 %copy-start.64 = (f32[128]{0:T(128)S(1)}, f32[128]{0:T(128)}, u32[]{:S(2)}) copy-start(f32[128]{0:T(128)} %copy-done.63) | copy-start | bytes 1540
  285.1 163.6 %copy-start.66 = (f32[128]{0:T(128)S(1)}, f32[128]{0:T(128)}, u32[]{:S(2)}) copy-start(f32[128]{0:T(128)} %copy-done.65) | copy-start | bytes 1540
  285.1 164.3 %copy-start.6 = (f32[128,2048]{1,0:T(8,128)S(1)}, f32[128,2048]{1,0:T(8,128)}, u32[]{:S(2)}) copy-start(f32[128,2048]{1,0:T(8,128)} %copy-done.5) | copy-start | bytes 3145732
  285.1 164.3 %copy-start.52 = (bf16[2048,32]{0,1:T(8,128)(2,1)S(1)}, bf16[2048,32]{0,1:T(8,128)(2,1)}, u32[]{:S(2)}) copy-start(bf16[2048,32]{0,1:T(8,128)(2,1)} %param.25) | copy-start | bytes 393220
  285.1 164.4 %copy-start.69 = (f32[128]{0:T(128)S(1)}, f32[128]{0:T(128)}, u32[]{:S(2)}) copy-start(f32[128]{0:T(128)} %copy-done.68) | copy-start | bytes 1540
  285.1 166.4 %copy-start.78 = (f32[128]{0:T(128)S(1)}, f32[128]{0:T(128)}, u32[]{:S(2)}) copy-start(f32[128]{0:T(128)} %copy-done.77) | copy-start | bytes 1540
  285.1 167.4 %copy-start.40 = (bf16[128,2048]{1,0:T(8,128)(2,1)S(1)}, bf16[128,2048]{1,0:T(8,128)(2,1)}, u32[]{:S(2)}) copy-start(bf16[128,2048]{1,0:T(8,128)(2,1)} %grads_own.1) | copy-start | bytes 1572868
  453.7 19.2 %copy-start.20 = (pred[512,512]{0,1:T(8,128)(4,1)S(1)}, pred[512,512]{0,1:T(8,128)(4,1)}, u32[]{:S(2)}) copy-start(pred[512,512]{0,1:T(8,128)(4,1)} %copy-done.19) | copy-start | bytes 786436
  479.1 8.5 %copy-start.54 = (f32[8,128]{1,0:T(8,128)S(1)}, f32[8,128]{1,0:T(8,128)}, u32[]{:S(2)}) copy-start(f32[8,128]{1,0:T(8,128)} %narrow_total_4.1) | copy-start | bytes 12292
  481.1 9.5 %copy-start.74 = (f32[512]{0:T(512)S(1)}, f32[512]{0:T(512)}, u32[]{:S(2)}) copy-start(f32[512]{0:T(512)} %copy-done.73) | copy-start | bytes 6148
  504.9 7.8 copy-start.24
  504.9 7.8 copy-start.53
  513.7 235.0 %copy-start.8 = (f32[512,2048]{1,0:T(8,128)S(1)}, f32[512,2048]{1,0:T(8,128)}, u32[]{:S(2)}) copy-start(f32[512,2048]{1,0:T(8,128)} %convert_element_type.126) | copy-start | bytes 12582916
  513.7 235.3 %copy-start.7 = (f32[128,2048]{1,0:T(8,128)S(1)}, f32[128,2048]{1,0:T(8,128)}, u32[]{:S(2)}) copy-start(f32[128,2048]{1,0:T(8,128)} %copy-done.5) | copy-start | bytes 3145732
  513.8 235.3 %copy-start.14 = (f32[128,2048]{1,0:T(8,128)S(1)}, f32[128,2048]{1,0:T(8,128)}, u32[]{:S(2)}) copy-start(f32[128,2048]{1,0:T(8,128)} %copy-done.13) | copy-start | bytes 3145732
  513.8 235.3 %copy-start.41 = (bf16[128,2048]{1,0:T(8,128)(2,1)S(1)}, bf16[128,2048]{1,0:T(8,128)(2,1)}, u32[]{:S(2)}) copy-start(bf16[128,2048]{1,0:T(8,128)(2,1)} %grads_own.1) | copy-start | bytes 1572868
  513.8 235.3 %copy-start.50 = (bf16[128,2048]{1,0:T(8,128)(2,1)S(1)}, bf16[128,2048]{1,0:T(8,128)(2,1)}, u32[]{:S(2)}) copy-start(bf16[128,2048]{1,0:T(8,128)(2,1)} %get-tuple-element.89) | copy-start | bytes 1572868
  764.0 15.0 %slice-start = ((s8[8388608]{0:T(1024)(128)(4,1)}), s8[4194304]{0:T(1024)(128)(4,1)S(1)}, s32[]{:S(2)}) async-start(s8[8388608]{0:T(1024)(128)(4,1)} %bitcast.151), calls=%async_computation | async-start | bytes 8388608
  771.5 7.5 slice-start.1
  (52 other events, 115.0 us)
